TPU v7x, 32 devices: a whole 2x2x4 slice. The times are simulated.
32 devices in a mesh: seq: 4 (over y, x), dp: 8 (over z, core).
Axes of the slice: x: 2, y: 2, z: 4, core: 2. Of those that a mesh axis runs over, the one named last changes fastest.
Arguments:
- tokens: bfloat16 [24, 208, 768], P('dp', 'seq'), may hold values from -6 to 6
- key_mask: int32 [24, 208], P('dp'), may hold values 0 or 1
- prompts: float32 [50, 768], replicated, may hold values from -6 to 6
- gain_one: float32 [768], replicated, may hold values from 0.1 to 1.9
- shift_one: float32 [768], replicated, may hold values from -3 to 3
- w_qkv: bfloat16 [768, 2304], replicated, may hold values from -0.21875 to 0.21875
- b_qkv: float32 [2304], replicated, may hold values from -3 to 3
- w_out: bfloat16 [768, 768], replicated, may hold values from -0.875 to 0.875
- b_out: float32 [768], replicated, may hold values from -2 to 2
- gain_two: float32 [768], replicated, may hold values from 0.1 to 1.9
- shift_two: float32 [768], replicated, may hold values from -3 to 3
- w_up: bfloat16 [768, 3072], replicated, may hold values from -0.21875 to 0.21875
- b_up: float32 [3072], replicated, may hold values from -3 to 3
- w_down: bfloat16 [3072, 768], replicated, may hold values from -0.109375 to 0.109375
- b_down: float32 [768], replicated, may hold values from -2 to 2
- cotangent: bfloat16 [24, 208, 768], P('dp', 'seq'), may hold values from -6 to 6
- start_factor: float32 [768, 8], replicated, may hold values from -6 to 6
- error_buffer: float32 [8, 50, 768], P('dp'), may hold values from -12 to 12
- momentum: float32 [50, 768], replicated, may hold values from -0.875 to 0.875
Outputs:
- layer_out: bfloat16 [24, 208, 768], P('dp', 'seq')
- input_grad: bfloat16 [24, 208, 768], P('dp', 'seq')
- left_basis: float32 [50, 8], replicated
- right_sum: float32 [768, 8], replicated
- new_error: float32 [8, 50, 768], P('dp')
- new_momentum: float32 [50, 768], replicated
- new_prompts: float32 [50, 768], replicated
- prompt_copy: bfloat16 [50, 768], replicated
All inputs are finite; a program needn't handle non-finite values. No bound on the sum of `key_mask` on one device may be relied on, other than what follows from the above.
Results may differ from a plain program's by a relative error of at most 0.015.
Values may be sent and summed in bfloat16 or wider, within the bound.
No kernel may reach another device: no remote copies, remote signals or barrier semaphores. Data moves between devices by JAX's collectives and lax.ppermute only.
A program may use at most 64 MiB of HBM per device.

v0:
```python
import math

import jax
import jax.numpy as jnp
from jax import lax
from jax.sharding import PartitionSpec as P

HEADS = 12


highest = lax.Precision.HIGHEST
norm_eps = 1e-06
momentum_decay = 0.5
rate_scale = 3.0


def layer_norm(values, gain, shift):
    center = values - jnp.mean(values, axis=-1, keepdims=True)
    spread = jnp.mean(center * center, axis=-1, keepdims=True)
    return center * lax.rsqrt(spread + norm_eps) * gain + shift


def norm_back(values, gain, shift, grad):
    return jax.vjp(lambda inner: layer_norm(inner, gain, shift), values)[1](grad)[0]


def back_dot(grad, weight):
    return lax.dot_general(
        grad, weight, (((grad.ndim - 1,), (1,)), ((), ())), preferred_element_type=jnp.float32
    )


def orthonormal(matrix):
    columns = []
    for index in range(matrix.shape[1]):
        column = matrix[:, index]
        for earlier in columns:
            column = column - jnp.sum(earlier * column) * earlier
        column = column * lax.rsqrt(jnp.sum(column * column) + 1e-12)
        columns.append(column)
    return jnp.stack(columns, 1)


def body(
    tokens,
    key_mask,
    prompts,
    gain_one,
    shift_one,
    w_qkv,
    b_qkv,
    w_out,
    b_out,
    gain_two,
    shift_two,
    w_up,
    b_up,
    w_down,
    b_down,
    cotangent,
    start_factor,
    error_buffer,
    momentum,
):
    images, local_rows, width = tokens.shape
    head = width // HEADS
    scale = head ** (-0.5)
    f32 = jnp.float32
    bf16 = jnp.bfloat16
    rows = tokens.astype(f32)
    normed = layer_norm(rows, gain_one, shift_one).astype(bf16)
    prompt_rows = prompts.astype(bf16).astype(f32)
    normed_prompt = layer_norm(prompt_rows, gain_one, shift_one).astype(bf16)
    w_kv = w_qkv[:, width:]
    b_kv = b_qkv[width:]
    prompt_kv = (jnp.dot(normed_prompt, w_kv, preferred_element_type=f32) + b_kv).astype(bf16)
    qkv = (jnp.dot(normed, w_qkv, preferred_element_type=f32) + b_qkv).astype(bf16)
    query = qkv[..., :width]
    all_kv = lax.all_gather(qkv[..., width:], "seq", axis=1, tiled=True)
    total_rows = all_kv.shape[1]
    prompt_count = prompt_kv.shape[0]
    query4 = query.reshape(images, local_rows, HEADS, head)
    key_rows = all_kv[..., :width].reshape(images, total_rows, HEADS, head)
    value_rows = all_kv[..., width:].reshape(images, total_rows, HEADS, head)
    key_prompt = prompt_kv[:, :width].reshape(prompt_count, HEADS, head)
    value_prompt = prompt_kv[:, width:].reshape(prompt_count, HEADS, head)
    raw = jnp.concatenate(
        [
            jnp.einsum("bqhd,khd->bhqk", query4, key_prompt, preferred_element_type=f32),
            jnp.einsum("bqhd,bkhd->bhqk", query4, key_rows, preferred_element_type=f32),
        ],
        -1,
    )
    keep = jnp.concatenate([jnp.ones((images, prompt_count), bool), key_mask == 1], -1)[
        :, None, None, :
    ]
    probs = jax.nn.softmax(jnp.where(keep, raw * scale, -jnp.inf), axis=-1)
    weights = probs.astype(bf16)
    mixed = jnp.einsum(
        "bhqk,khd->bqhd", weights[..., :prompt_count], value_prompt, preferred_element_type=f32
    )
    mixed = mixed + jnp.einsum(
        "bhqk,bkhd->bqhd", weights[..., prompt_count:], value_rows, preferred_element_type=f32
    )
    mixed = mixed.reshape(images, local_rows, width).astype(bf16)
    resid = rows + jnp.dot(mixed, w_out, preferred_element_type=f32) + b_out
    normed_two = layer_norm(resid, gain_two, shift_two).astype(bf16)
    hidden = jnp.dot(normed_two, w_up, preferred_element_type=f32) + b_up
    act = jax.nn.gelu(hidden, approximate=False).astype(bf16)
    layer_out = (resid + jnp.dot(act, w_down, preferred_element_type=f32) + b_down).astype(bf16)
    grad_out = cotangent.astype(f32)
    grad_act = back_dot(grad_out.astype(bf16), w_down)
    grad_hidden = jax.vjp(lambda inner: jax.nn.gelu(inner, approximate=False), hidden)[1](grad_act)[
        0
    ].astype(bf16)
    grad_resid = grad_out + norm_back(resid, gain_two, shift_two, back_dot(grad_hidden, w_up))
    grad_mixed = (
        back_dot(grad_resid.astype(bf16), w_out)
        .astype(bf16)
        .reshape(images, local_rows, HEADS, head)
    )
    grad_probs = jnp.concatenate(
        [
            jnp.einsum("bqhd,khd->bhqk", grad_mixed, value_prompt, preferred_element_type=f32),
            jnp.einsum("bqhd,bkhd->bhqk", grad_mixed, value_rows, preferred_element_type=f32),
        ],
        -1,
    )
    grad_raw = probs * (grad_probs - jnp.sum(probs * grad_probs, axis=-1, keepdims=True))
    grad_raw = (scale * grad_raw).astype(bf16)
    raw_prompt = grad_raw[..., :prompt_count]
    raw_rows = grad_raw[..., prompt_count:]
    grad_query = jnp.einsum("bhqk,khd->bqhd", raw_prompt, key_prompt, preferred_element_type=f32)
    grad_query = grad_query + jnp.einsum(
        "bhqk,bkhd->bqhd", raw_rows, key_rows, preferred_element_type=f32
    )
    grad_key_rows = jnp.einsum("bhqk,bqhd->bkhd", raw_rows, query4, preferred_element_type=f32)
    grad_value_rows = jnp.einsum(
        "bhqk,bqhd->bkhd", weights[..., prompt_count:], grad_mixed, preferred_element_type=f32
    )
    grad_kv_rows = jnp.concatenate(
        [
            grad_key_rows.reshape(images, total_rows, width),
            grad_value_rows.reshape(images, total_rows, width),
        ],
        -1,
    )
    grad_kv_local = lax.psum_scatter(grad_kv_rows, "seq", scatter_dimension=1, tiled=True).astype(
        bf16
    )
    grad_qkv = jnp.concatenate(
        [grad_query.reshape(images, local_rows, width).astype(bf16), grad_kv_local], -1
    )
    grad_rows = grad_resid + norm_back(rows, gain_one, shift_one, back_dot(grad_qkv, w_qkv))
    input_grad = grad_rows.astype(bf16)
    grad_key_prompt = jnp.einsum("bhqk,bqhd->khd", raw_prompt, query4, preferred_element_type=f32)
    grad_value_prompt = jnp.einsum(
        "bhqk,bqhd->khd", weights[..., :prompt_count], grad_mixed, preferred_element_type=f32
    )
    grad_prompt_kv = jnp.concatenate(
        [
            grad_key_prompt.reshape(prompt_count, width),
            grad_value_prompt.reshape(prompt_count, width),
        ],
        -1,
    )
    w_kv_wide = w_kv.astype(f32)
    grad_normed = lax.dot_general(
        lax.psum(grad_prompt_kv, "seq"), w_kv_wide, (((1,), (1,)), ((), ())), precision=highest
    )
    grad_prompt = norm_back(prompt_rows, gain_one, shift_one, grad_normed)
    combined = grad_prompt + error_buffer[0]
    left = lax.psum(jnp.dot(combined, start_factor, precision=highest), "dp")
    left_basis = orthonormal(left)
    right_local = lax.dot_general(combined, left_basis, (((0,), (0,)), ((), ())), precision=highest)
    right_sum = lax.psum(right_local, "dp")
    new_error = combined - lax.dot_general(
        left_basis, right_local, (((1,), (1,)), ((), ())), precision=highest
    )
    image_total = images * lax.axis_size("dp")
    update = (
        lax.dot_general(left_basis, right_sum, (((1,), (1,)), ((), ())), precision=highest)
        / image_total
    )
    new_momentum = momentum_decay * momentum + update
    new_prompts = prompts - rate_scale * math.sqrt(image_total) * new_momentum
    return (
        layer_out,
        input_grad,
        left_basis,
        right_sum,
        new_error[None],
        new_momentum,
        new_prompts,
        new_prompts.astype(bf16),
    )


def solution(mesh):
    placed = (
        P("dp", "seq", None),
        P("dp", None),
        P(),
        P(),
        P(),
        P(),
        P(),
        P(),
        P(),
        P(),
        P(),
        P(),
        P(),
        P(),
        P(),
        P("dp", "seq", None),
        P(),
        P("dp", None, None),
        P(),
    )
    return jax.shard_map(
        body,
        mesh=mesh,
        in_specs=placed,
        out_specs=(
            P("dp", "seq", None),
            P("dp", "seq", None),
            P(),
            P(),
            P("dp", None, None),
            P(),
            P(),
            P(),
        ),
        check_vma=False,
    )
```

profile of v0, /device:TPU:0, one launch (start us, length us, event | category | flops | bytes accessed | tf_op | source)
XLA Modules:
  0.0 411.6 jit_solution(12133789005603025342)
XLA Ops:
  9.6 2.9 fusion.13
  12.6 1.2 copy.85
  14.7 2.2 fusion.21
  18.3 1.4 copy.88
  21.1 34.7 %all-gather.2.cloned.1.call-done = bf16[3,208,1536]{2,0,1:T(4,128)(2,1)} async-done(((bf16[3,52,1536]{2,0,1:T(4,128)(2,1)}), bf16[3,208,1536]{2,0,1:T(4,128)(2,1)}) %all-gather.2.cloned.1.call-update) | async-done | bytes 1916944 | tf_op jit(solution)/shard_map/all_gather | solution.py:79
  55.7 3.6 fusion.160
  59.4 3.4 copy.135
  62.8 2.1 copy.134
  65.0 1.8 fusion.93
  66.8 8.5 %fusion.162 = (f32[3,12,52]{2,1,0:T(8,128)S(1)}, f32[3,12,52,258]{3,2,1,0:T(8,128)S(1)}) fusion(f32[3,12,52,208]{3,2,1,0:T(8,128)S(1)} %fusion.93, f32[3,12,52,50]{3,2,1,0:T(8,128)S(1)} %copy-done.24, pred[3,258]{1,0:T(4,128)(4,1)S(1)} %concatenate.18), kind=kOutput, calls=%fused_computation.284 | output fusion | flops 2415137 | bytes 3872070 | tf_op jit(solution)/shard_map/sub | solution.py:97
  75.6 1.3 copy-done.15
  79.4 5.4 %fusion.86 = (u8[52,3072]{1,0:T(8,128)(4,1)S(1)}, u8[52,3072]{1,0:T(8,128)(4,1)S(1)}, f32[3,52,3072]{2,1,0:T(8,128)}) fusion(f32[3072]{0:T(1024)S(1)} %copy-done.46, bf16[768,3072]{1,0:T(8,128)(2,1)} %param.30, f32[3,52,768]{2,1,0:T(8,128)S(1)} %get-tuple-element.108, f32[768]{0:T(1024)S(1)} %copy-done.48, f32[768]{0:T(1024)S(1)} %copy-done.49, ...), kind=kOutput, calls=%fused_computation.111 | convolution fusion | flops 743089152 | bytes 7453920 | tf_op jit(solution)/shard_map/dot_general | solution.py:108
  84.8 11.1 %multiply_reduce_fusion.1 = (f32[3,52]{1,0:T(4,128)S(1)}, f32[3,52,768]{2,1,0:T(8,128)}) fusion(f32[3,52,768]{2,1,0:T(8,128)S(1)} %get-tuple-element.108, f32[3,52]{1,0:T(4,128)S(1)} %broadcast_multiply_fusion, f32[768]{0:T(1024)S(1)} %copy-done.49, bf16[768,3072]{1,0:T(8,128)(2,1)} %param.30, bf16[3,52,768]{2,1,0:T(8,128)(2,1)S(1)} %copy-done.25, ...), kind=kOutput, calls=%fused_computation.107 | convolution fusion | flops 1509580672 | bytes 12876000 | tf_op jit(solution)/shard_map/dot_general | solution.py:28
  95.9 1.6 fusion.159
  98.3 2.2 convolution_convert_fusion
  100.5 1.3 reshape.145
  102.3 2.2 fusion.98
  105.4 1.4 copy-done.16
  106.8 20.1 %multiply_convert_fusion = bf16[3,12,52,258]{3,2,1,0:T(8,128)(2,1)S(1)} fusion(f32[3,12,52,208]{3,2,1,0:T(8,128)S(1)} %fusion.100, f32[3,12,52,50]{3,2,1,0:T(8,128)S(1)} %convolution_bitcast_fusion.2, f32[3,12,52,258]{3,2,1,0:T(8,128)S(1)} %copy-done.16, f32[3,12,52]{2,1,0:T(8,128)S(1)} %get-tuple-element.105), kind=kOutput, calls=%fused_computation.21 | output fusion | flops 4348913 | bytes 4837248 | tf_op jit(solution)/shard_map/sub | solution.py:129
  126.9 1.3 convolution_bitcast_fusion.7
  128.2 1.4 convolution_bitcast_fusion.1
  131.3 6.3 %fusion.55 = bf16[3,52,768]{2,1,0:T(8,128)(2,1)} fusion(f32[3,52,768]{2,1,0:T(8,128)S(1)} %copy-done.14, bf16[3072,768]{1,0:T(8,128)(2,1)S(1)} %bitcast.206, f32[3,52,3072]{2,1,0:T(8,128)S(1)} %copy-done.52, f32[768]{0:T(1024)S(1)} %copy-done.50, u8[52,3072]{1,0:T(8,128)(4,1)S(1)} %copy-done.56, u8[52,3072]{1,0:T(8,128)(4,1)S(1)} %copy-done.54), kind=kOutput, calls=%fused_computation.71 | convolution fusion | flops 770006016 | bytes 7676928 | tf_op jit(solution)/shard_map/dot_general | solution.py:110
  138.4 3.0 copy.107
  141.4 1.9 copy.110
  143.3 1.8 reshape.148
  145.1 1.8 pad_maximum_fusion.3
  146.9 2.3 fusion.41
  150.4 2.0 copy.106
  152.3 4.4 %pad_maximum_fusion = f32[3,208,1536]{2,1,0:T(8,128)} fusion(f32[3,208,768]{2,1,0:T(8,128)} %copy.107, f32[3,208,768]{2,1,0:T(8,128)} %copy.106), kind=kLoop, calls=%fused_computation.11 | loop fusion | flops 958464 | bytes 7667712 | tf_op jit(solution)/shard_map/concatenate | solution.py:141
  156.7 137.0 %all-reduce.6 = bf16[3,208,1536]{2,1,0:T(8,128)(2,1)S(1)} all-reduce(f32[3,208,1536]{2,1,0:T(8,128)} %pad_maximum_fusion), channel_id=2, replica_groups=mesh['seq'=4,'dp'=8] {'seq'}, use_global_device_ids=true, to_apply=%region_11.12.clone | all-reduce | flops 958464 | bytes 5750784
  293.9 3.5 fusion.83
  298.8 4.2 %fusion.123 = (f32[50]{0:T(128)S(1)}, f32[50,768]{1,0:T(8,128)S(1)}) fusion(bf16[50,768]{1,0:T(8,128)(2,1)S(1)} %copy-done.18, f32[50]{0:T(128)S(1)} %copy-done.36, f32[768]{0:T(1024)S(1)} %copy-done.40, f32[50,1536]{1,0:T(8,128)} %all-reduce.5.cloned.1.call-done, bf16[768,2304]{1,0:T(8,128)(2,1)} %param.24), kind=kOutput, calls=%fused_computation.150 | convolution fusion | flops 707980736 | bytes 2937232 | tf_op jit(solution)/shard_map/dot_general | solution.py:168
  303.6 14.9 %psum.22 = f32[50,8]{0,1:T(8,128)S(1)} all-reduce(f32[50,8]{0,1:T(8,128)S(1)} %fusion.166), channel_id=1, replica_groups=mesh['seq'=4,'dp'=8] {'dp'}, use_global_device_ids=true, to_apply=%region_17.18 | all-reduce | flops 400 | bytes 3200 | tf_op jit(solution)/shard_map/psum | solution.py:173
  320.4 1.3 fusion.136
  322.4 1.9 multiply_reduce_fusion.29
  324.3 4.5 %multiply_reduce_fusion.9 = (f32[]{:T(128)}, f32[]{:T(128)}, f32[]{:T(128)}, f32[]{:T(128)}, f32[]{:T(128)}, /*index=5*/f32[]{:T(128)}, f32[50]{0:T(128)S(1)}, f...) fusion(f32[50]{0:T(128)S(1)} %get-tuple-element.94, f32[50]{0:T(128)S(1)} %get-tuple-element.93, ...), kind=kLoop, calls=%fused_computation.213 | loop fusion | flops 1194 | bytes 2648 | tf_op jit(solution)/shard_map/reduce_sum | solution.py:38
  329.6 4.4 %multiply_reduce_fusion.8 = (f32[]{:T(128)}, f32[]{:T(128)}, f32[]{:T(128)}, f32[]{:T(128)}, f32[]{:T(128)}, /*index=5*/f32[50]{0:T(128)S(1)}) fusion(f32[50]{0:T(128)S(1)} %get-tuple-element.91, f32[50]{0:T(128)S(1)} %get-tuple-element.94, f32[]{:T(128)} %get-tuple-element.55, f32[50]{0:T(128)S(1)} %get-tuple-element.90, f32[]{:T(128)} %get-tuple-element.56, ...), kind=kLoop, calls=%fused_computation.211 | loop fusion | flops 1145 | bytes 1648 | tf_op jit(solution)/shard_map/reduce_sum | solution.py:38
  334.0 1.9 multiply_reduce_fusion.25
  336.5 1.9 multiply_reduce_fusion.22
  338.4 5.1 %multiply_reduce_fusion.7 = (f32[]{:T(128)}, f32[]{:T(128)}, f32[]{:T(128)}, f32[]{:T(128)}, f32[50]{0:T(128)S(1)}, /*index=5*/f32[50]{0:T(128)S(1)}, f32[50]{0:T(128)S(1)}) fusion(f32[50]{0:T(128)S(1)} %get-tuple-element.83, f32[50]{0:T(128)S(1)} %get-tuple-element.82, f32[]{:T(128)} %get-tuple-element.81, f32[50]{0:T(128)S(1)} %get-tuple-element.86, ...), kind=kLoop, calls=%fused_computation.209 | loop fusion | flops 1096 | bytes 2044 | tf_op jit(solution)/shard_map/reduce_sum | solution.py:38
  344.2 3.1 multiply_reduce_fusion.6
  347.3 1.9 multiply_reduce_fusion.16
  349.9 3.1 multiply_reduce_fusion.5
  353.0 1.3 multiply_reduce_fusion.10
  354.9 1.3 multiply_reduce_fusion.4
  356.2 1.9 multiply_reduce_fusion.3
  358.7 17.6 %subtract_multiply_fusion = (f32[50,1]{0,1:T(1,128)S(1)}, f32[50,1]{0,1:T(1,128)S(1)}, f32[50,1]{0,1:T(1,128)S(1)}, f32[50,1]{0,1:T(1,128)S(1)}, f32[50,1]{0,1:T...) fusion(f32[50,1]{0,1:T(1,128)S(1)} %get-tuple-element.96, f32[]{:T(128)S(6)} %rsqrt.67, f32[]{:T(128)} %multiply_reduce_fusion.4, ...), kind=kLoop, calls=%fused_computation.202 | loop fusion | flops 3150 | bytes 3140 | tf_op jit(solution)/shard_map/mul | solution.py:39
  376.9 26.0 %psum.23 = f32[768,8]{0,1:T(8,128)S(1)} all-reduce(f32[768,8]{0,1:T(8,128)S(1)} %fusion.167), channel_id=1, replica_groups=mesh['seq'=4,'dp'=8] {'dp'}, use_global_device_ids=true, to_apply=%region_54.55 | all-reduce | flops 6144 | bytes 49152 | tf_op jit(solution)/shard_map/psum | solution.py:176
  (177 shorter events, 19.6 us)
Async XLA Ops:
  7.2 71.5 %copy-start = (bf16[768,768]{1,0:T(8,128)(2,1)S(1)}, bf16[768,768]{1,0:T(8,128)(2,1)}, u32[]{:S(2)}) copy-start(bf16[768,768]{1,0:T(8,128)(2,1)} %param.26) | copy-start | bytes 3538948
  7.2 48.6 %all-gather.2.cloned.1.call-start = ((), (), s32[]{:S(2)}) async-start(), calls=%async_computation | async-start | bytes 3194880 | tf_op jit(solution)/shard_map/all_gather | solution.py:79
  12.5 2.1 copy-start.39
  12.5 2.1 copy-start.47
  13.8 285.0 %all-reduce.5.cloned.1.call-start = ((), (), s32[]{:S(2)}) async-start(), calls=%async_computation.1 | async-start | bytes 688128 | tf_op jit(solution)/shard_map/psum | solution.py:169
  14.0 3.1 copy-start.35
  14.2 2.9 copy-start.44
  14.7 2.5 copy-start.42
  17.1 59.8 %copy-start.22 = (bf16[50,12,64]{2,1,0:T(8,128)(2,1)}, bf16[50,12,64]{2,1,0:T(8,128)(2,1)S(1)}, u32[]{:S(2)}) copy-start(bf16[50,12,64]{2,1,0:T(8,128)(2,1)S(1)} %reshape.140) | copy-start | bytes 230404
  17.3 2.4 copy-start.20
  17.7 109.2 %copy-start.2 = (bf16[3,52,12,64]{3,2,1,0:T(8,128)(2,1)}, bf16[3,52,12,64]{3,2,1,0:T(8,128)(2,1)S(1)}, u32[]{:S(2)}) copy-start(bf16[3,52,12,64]{3,2,1,0:T(8,128)(2,1)S(1)} %reshape.142) | copy-start | bytes 718852
  17.7 2.0 copy-start.51
  17.7 3.2 copy-start.41
  65.0 1.8 copy-start.24
  75.2 1.7 copy-start.15
  75.2 2.1 copy-start.9
  79.1 5.7 %copy-start.13 = (f32[3,52,768]{2,1,0:T(8,128)}, f32[3,52,768]{2,1,0:T(8,128)S(1)}, u32[]{:S(2)}) copy-start(f32[3,52,768]{2,1,0:T(8,128)S(1)} %get-tuple-element.108) | copy-start | bytes 1437700
  79.4 5.4 %copy-start.25 = (bf16[3,52,768]{2,1,0:T(8,128)(2,1)S(1)}, bf16[3,52,768]{2,1,0:T(8,128)(2,1)}, u32[]{:S(2)}) copy-start(bf16[3,52,768]{2,1,0:T(8,128)(2,1)} %param.34) | copy-start | bytes 718852
  84.8 11.1 %copy-start.53 = (u8[52,3072]{1,0:T(8,128)(4,1)}, u8[52,3072]{1,0:T(8,128)(4,1)S(1)}, u32[]{:S(2)}) copy-start(u8[52,3072]{1,0:T(8,128)(4,1)S(1)} %get-tuple-element.32) | copy-start | bytes 479236
  84.8 11.1 %copy-start.55 = (u8[52,3072]{1,0:T(8,128)(4,1)}, u8[52,3072]{1,0:T(8,128)(4,1)S(1)}, u32[]{:S(2)}) copy-start(u8[52,3072]{1,0:T(8,128)(4,1)S(1)} %get-tuple-element.33) | copy-start | bytes 479236
  95.9 6.0 %copy-start.7 = (bf16[3,12,52,258]{3,2,1,0:T(8,128)(2,1)S(1)}, bf16[3,12,52,258]{3,2,1,0:T(8,128)(2,1)}, u32[]{:S(2)}) copy-start(bf16[3,12,52,258]{3,2,1,0:T(8,128)(2,1)} %copy-done.6) | copy-start | bytes 2897860
  102.2 2.2 copy-start.23
  102.2 2.7 copy-start.10
  104.9 1.9 copy-start.16
  104.9 25.4 %slice-start = ((s8[4718592]{0:T(1024)(128)(4,1)}), s8[4194304]{0:T(1024)(128)(4,1)S(1)}, s32[]{:S(2)}) async-start(s8[4718592]{0:T(1024)(128)(4,1)} %bitcast.205), calls=%async_computation.2 | async-start | bytes 8388608
  106.8 21.4 %copy-start.21 = (bf16[50,12,64]{2,1,0:T(8,128)(2,1)S(1)}, bf16[50,12,64]{2,1,0:T(8,128)(2,1)}, u32[]{:S(2)}) copy-start(bf16[50,12,64]{2,1,0:T(8,128)(2,1)} %copy-done.20) | copy-start | bytes 230404
  106.8 23.6 %slice-start.1 = ((s8[4718592]{0:T(1024)(128)(4,1)}), s8[524288]{0:T(1024)(128)(4,1)S(1)}, s32[]{:S(2)}) async-start(s8[4718592]{0:T(1024)(128)(4,1)} %bitcast.205), calls=%async_computation.3 | async-start | bytes 1048576
  126.9 3.5 copy-start.19
  129.5 1.8 copy-start.52
  129.5 1.8 copy-start.54
  129.6 1.8 copy-start.56
  141.4 5.5 %copy-start.8 = (bf16[3,208,768]{1,2,0:T(8,128)(2,1)S(1)}, bf16[3,208,768]{1,2,0:T(8,128)(2,1)}, u32[]{:S(2)}) copy-start(bf16[3,208,768]{1,2,0:T(8,128)(2,1)} %copy.134) | copy-start | bytes 2875396
  156.7 137.2 %copy-start.5 = (bf16[3,52,768]{2,1,0:T(8,128)(2,1)S(1)}, bf16[3,52,768]{2,1,0:T(8,128)(2,1)}, u32[]{:S(2)}) copy-start(bf16[3,52,768]{2,1,0:T(8,128)(2,1)} %param.19) | copy-start | bytes 718852
  156.7 137.2 %copy-start.29 = (bf16[3,52,768]{2,1,0:T(8,128)(2,1)S(1)}, bf16[3,52,768]{2,1,0:T(8,128)(2,1)}, u32[]{:S(2)}) copy-start(bf16[3,52,768]{2,1,0:T(8,128)(2,1)} %convert_element_type.90) | copy-start | bytes 718852
  156.7 137.2 %copy-start.40 = (f32[768]{0:T(1024)S(1)}, f32[768]{0:T(1024)}, u32[]{:S(2)}) copy-start(f32[768]{0:T(1024)} %param.22) | copy-start | bytes 9220
  293.9 3.8 copy-start.12
  293.9 3.8 copy-start.26
  297.4 1.4 copy-start.18
  297.4 1.4 copy-start.36
  297.8 5.3 %copy-start.45 = (f32[50]{0:T(128)S(1)}, f32[50]{0:T(128)}, u32[]{:S(2)}) copy-start(f32[50]{0:T(128)} %copy-done.44) | copy-start | bytes 604
  297.8 5.3 %copy-start.43 = (f32[50]{0:T(128)S(1)}, f32[50]{0:T(128)}, u32[]{:S(2)}) copy-start(f32[50]{0:T(128)} %copy-done.42) | copy-start | bytes 604
  298.8 4.5 %copy-start.31 = (f32[1,50,768]{2,0,1:T(1,128)S(1)}, f32[1,50,768]{2,0,1:T(1,128)}, u32[]{:S(2)}) copy-start(f32[1,50,768]{2,0,1:T(1,128)} %param.36) | copy-start | bytes 460804
  298.8 4.6 %copy-start.34 = (f32[768,8]{0,1:T(8,128)S(1)}, f32[768,8]{0,1:T(8,128)}, u32[]{:S(2)}) copy-start(f32[768,8]{0,1:T(8,128)} %param.35) | copy-start | bytes 73732
  298.8 104.9 %copy-start.28 = (f32[50,768]{1,0:T(8,128)S(1)}, f32[50,768]{1,0:T(8,128)}, u32[]{:S(2)}) copy-start(f32[50,768]{1,0:T(8,128)} %param.21) | copy-start | bytes 460804
  298.8 104.9 %copy-start.30 = (f32[50,768]{1,0:T(8,128)S(1)}, f32[50,768]{1,0:T(8,128)}, u32[]{:S(2)}) copy-start(f32[50,768]{1,0:T(8,128)} %param.37) | copy-start | bytes 460804
  298.8 106.0 %copy-start.1 = (bf16[768,768]{1,0:T(8,128)(2,1)S(1)}, bf16[768,768]{1,0:T(8,128)(2,1)}, u32[]{:S(2)}) copy-start(bf16[768,768]{1,0:T(8,128)(2,1)} %param.26) | copy-start | bytes 3538948
  376.3 28.5 %copy-start.33 = (f32[50,8]{0,1:T(8,128)}, f32[50,8]{0,1:T(8,128)S(1)}, u32[]{:S(2)}) copy-start(f32[50,8]{0,1:T(8,128)S(1)} %stack.2) | copy-start | bytes 4804
  402.8 2.0 copy-start.32
  (13 other events, 14.9 us)
Sparse Core Ops, SparseCore 0:
  13.9 41.7 all-gather.1
  147.0 45.0 all-reduce.4
where the time goes:
time: 413 us; the launch traced here: 412 us
  blocking collectives  178 us (43%)
  other arithmetic  93.3 us (23%)
  matrix products  52.6 us (13%)
  waiting for transfers between devices  34.7 us (8%)
  local copies, waits for them, and re-layouts  32 us (8%)
  between operations  21.1 us (5%)
    unnamed x1, blocking collectives  137 us
    all_gather x1, waiting for transfers between devices, body(): all_kv = lax.all_gather(qkv[..., width:], 'seq', axis=1, tiled=True)  34.7 us
    reduce_sum x10, other arithmetic, orthonormal(): column = column - jnp.sum(earlier * column) * earlier  27.3 us
    psum x1, blocking collectives, body(): right_sum = lax.psum(right_local, 'dp')  26 us
    sub x1, other arithmetic, body(): grad_probs - jnp.sum(probs * grad_probs, axis=-1, keepdims=True)  20.1 us
    mul x1, other arithmetic, orthonormal(): column = column * lax.rsqrt(jnp.sum(column * column) + 1e-12)  17.6 us
    dot_general x3, matrix products, back_dot(): lax.dot_general(grad, weight, (((grad.ndim - 1,), (1,)), ((), ())), prefe...  16.8 us
    psum x1, blocking collectives, body(): left = lax.psum(jnp.dot(combined, start_factor, precision=highest), 'dp')  14.9 us
  transfers between devices with their start and end apart: 2, of which 1 were waited for; matrix products, arithmetic and copies ran while one was open for 5% of the time, Pallas kernels for 0%

commit v1 on v0

v1 whole, which is shorter than its diff:
```python
import functools
import math

import jax
import jax.numpy as jnp
from jax import lax
from jax.experimental import pallas as pl
from jax.experimental.pallas import tpu as pltpu
from jax.sharding import PartitionSpec as P

HEADS = 12
EPS = 1e-06
MOMENTUM_DECAY = 0.5
RATE_SCALE = 3.0
HIGHEST = lax.Precision.HIGHEST
F32 = jnp.float32
BF16 = jnp.bfloat16
VMEM = pl.BlockSpec(memory_space=pltpu.VMEM)
ANY = pl.BlockSpec(memory_space=pl.ANY)
MIB = 1 << 20
LOG2E = 1.4426950408889634


def up(value, unit):
    return -(-value // unit) * unit


def dot(a, b):
    return jnp.dot(a, b, preferred_element_type=F32)


def dot_nt(a, b, precision=None):
    return lax.dot_general(
        a, b, (((1,), (1,)), ((), ())), precision=precision, preferred_element_type=F32
    )


def dot_tn(a, b, precision=None):
    return lax.dot_general(
        a, b, (((0,), (0,)), ((), ())), precision=precision, preferred_element_type=F32
    )


def normalize(values):
    center = values - jnp.mean(values, axis=-1, keepdims=True)
    rstd = lax.rsqrt(jnp.mean(center * center, axis=-1, keepdims=True) + EPS)
    return center * rstd, rstd


def norm_back(hat, rstd, gain, grad):
    inner = grad * gain
    mean = jnp.mean(inner, axis=-1, keepdims=True)
    along = jnp.mean(inner * hat, axis=-1, keepdims=True)
    return rstd * (inner - mean - hat * along)


def call(kernel, outs, ins, scratch=(), in_specs=None, out_specs=None, flops=0, vmem=8 * MIB, name=None):
    in_bytes = sum(x.size * x.dtype.itemsize for x in ins)
    return pl.pallas_call(
        kernel,
        out_shape=[jax.ShapeDtypeStruct(s, d) for s, d in outs],
        in_specs=in_specs or [VMEM] * len(ins),
        out_specs=out_specs or [VMEM] * len(outs),
        scratch_shapes=list(scratch),
        compiler_params=pltpu.CompilerParams(vmem_limit_bytes=vmem),
        cost_estimate=pl.CostEstimate(flops=flops, bytes_accessed=in_bytes, transcendentals=0),
        name=name,
    )(*ins)


def pick_kernel(seq, images, tok, cot, *refs):
    outs, sem = refs[:-1], refs[-1]
    me = lax.axis_index("seq")
    copies = []
    for k in range(seq):
        index = jnp.minimum(me ^ k, images - 1)
        for part, source in enumerate((tok, cot)):
            copies.append(
                pltpu.make_async_copy(source.at[index], outs[2 * k + part], sem.at[2 * k + part])
            )
    for copy in copies:
        copy.start()
    for copy in copies:
        copy.wait()


def prompt_kernel(prompts, gain, shift, w_qkv, b_qkv, w_out, w_up, w_down, out):
    count, width = prompts.shape
    rows = prompts[...].astype(BF16).astype(F32)
    hat, _ = normalize(rows)
    normed = (hat * gain[...] + shift[...]).astype(BF16)
    out[...] = jnp.zeros_like(out)
    for part in range(2):
        cols = pl.ds((part + 1) * width, width)
        here = dot(normed, w_qkv[:, cols]) + b_qkv[:, cols]
        out[:count, pl.ds(part * width, width)] = here.astype(BF16)


def main_kernel(
    seq,
    images,
    *refs,
):
    toks = refs[:seq]
    cots = refs[seq : 2 * seq]
    (
        mask,
        pkv,
        prompts,
        gain_one,
        shift_one,
        w_qkv,
        b_qkv,
        w_out,
        b_out,
        gain_two,
        shift_two,
        w_up,
        b_up,
        w_down,
        pgrad,
        act,
        resid,
        dres,
        p_bf,
        ds_bf,
        query,
        dmix,
        k_t,
        x,
        gbuf,
        tbuf,
        keys,
        values,
        v_t,
        mix_t,
        p_f,
        dhid,
        normed,
    ) = refs[2 * seq :]
    me = lax.axis_index("seq")
    chunk = toks[0].shape[0]
    rows, width = x.shape
    head = width // HEADS
    ff = act.shape[1]
    nkeys = keys.shape[0]
    count = prompts.shape[0]
    scale = head ** (-0.5)
    live = jnp.where(me < images, 1.0, 0.0)
    for k in range(seq):
        tbuf[k] = toks[k][...]
    for c in range(seq):
        x[pl.ds(c * chunk, chunk), :] = tbuf[me ^ c].astype(F32) * live
    for k in range(seq):
        tbuf[k] = cots[k][...]
    for c in range(seq):
        gbuf[pl.ds(c * chunk, chunk), :] = tbuf[me ^ c].astype(F32) * live

    hat, _ = normalize(x[...])
    normed[...] = (hat * gain_one[...] + shift_one[...]).astype(BF16)
    query[...] = (dot(normed[...], w_qkv[:, :width]) + b_qkv[:, :width]).astype(BF16)
    for part, dest in enumerate((keys, values)):
        cols = pl.ds((part + 1) * width, width)
        dest[:rows, :] = (dot(normed[...], w_qkv[:, cols]) + b_qkv[:, cols]).astype(BF16)
        dest[rows:, :] = pkv[: nkeys - rows, pl.ds(part * width, width)]
    k_t[...] = keys[...].T
    v_t[...] = values[...].T

    index = jnp.minimum(me, images - 1)
    mrow = mask[pl.ds(index, 1), :].astype(F32)
    mcol = dot_tn(
        jnp.broadcast_to(mrow, (8, rows)).astype(BF16), jnp.full((8, rows), 0.125, BF16)
    )
    bias_rows = jnp.where(mcol > 0.5, 0.0, -jnp.inf)
    rest = lax.broadcasted_iota(jnp.int32, (nkeys - rows, rows), 0)
    bias = jnp.concatenate([bias_rows, jnp.where(rest < count, 0.0, -jnp.inf)], 0)

    lane = lax.broadcasted_iota(jnp.int32, (rows, 2 * head), 1) // head
    for pair in range(HEADS // 2):
        cols = pl.ds(pair * 2 * head, 2 * head)
        qp = query[:, cols]
        kp = keys[:, cols]
        for side in range(2):
            h = pair * 2 + side
            qm = jnp.where(lane == side, qp, jnp.zeros_like(qp))
            score = dot_nt(kp, qm) * (scale * LOG2E) + bias
            top = jnp.max(score, axis=0, keepdims=True)
            ex = jnp.exp2(score - top)
            total = jnp.sum(ex, axis=0, keepdims=True)
            prob = ex * (1.0 / total)
            p_f[h] = prob
            weight = prob.astype(BF16)
            p_bf[h] = weight
            part = pl.ds(h * head, head)
            mix_t[part, :] = dot(v_t[part, :], weight).astype(BF16)

    resid[...] = x[...] + dot_tn(mix_t[...], w_out[...]) + b_out[...]
    hat_two, rstd_two = normalize(resid[...])
    normed[...] = (hat_two * gain_two[...] + shift_two[...]).astype(BF16)
    grad_out = gbuf[...].astype(BF16)
    step = 256

    def mlp(c, carry):
        cols = pl.ds(pl.multiple_of(c * step, step), step)
        hidden = dot(normed[...], w_up[:, cols]) + b_up[:, cols]
        grad = dot_nt(grad_out, w_down[cols, :])
        cdf = 0.5 * (1.0 + lax.erf(hidden * math.sqrt(0.5)))
        act[:, cols] = (hidden * cdf).astype(BF16)
        pdf = jnp.exp(-0.5 * hidden * hidden) * (1.0 / math.sqrt(2.0 * math.pi))
        dhid[:, cols] = (grad * (cdf + hidden * pdf)).astype(BF16)
        return carry

    lax.fori_loop(0, ff // step, mlp, 0)
    hat_two, rstd_two = normalize(resid[...])
    grad_resid = gbuf[...] + norm_back(
        hat_two, rstd_two, gain_two[...], dot_nt(dhid[...], w_up[...])
    )
    dres[...] = grad_resid
    dmix[...] = dot_nt(grad_resid.astype(BF16), w_out[...]).astype(BF16)

    gk = []
    gv = []
    for pair in range(HEADS // 2):
        cols = pl.ds(pair * 2 * head, 2 * head)
        qp = query[:, cols]
        gp = dmix[:, cols]
        vp = values[:, cols]
        gkp = jnp.zeros((nkeys - rows, 2 * head), F32)
        gvp = jnp.zeros((nkeys - rows, 2 * head), F32)
        for side in range(2):
            h = pair * 2 + side
            qm = jnp.where(lane == side, qp, jnp.zeros_like(qp))
            gm = jnp.where(lane == side, gp, jnp.zeros_like(gp))
            dprob = dot_nt(vp, gm)
            prob = p_f[h]
            both = prob * dprob
            inner = jnp.sum(both, axis=0, keepdims=True)
            draw = ((both - prob * inner) * scale).astype(BF16)
            ds_bf[h] = draw
            gkp = gkp + dot(draw[rows:, :], qm)
            gvp = gvp + dot(p_bf[h, rows:, :], gm)
        gk.append(gkp)
        gv.append(gvp)
    pad = pgrad.shape[0]
    grad_kv = jnp.concatenate(gk + gv, 1)[:pad, :]
    first = grad_kv.astype(BF16)
    left = grad_kv - first.astype(F32)
    second = left.astype(BF16)
    third = (left - second.astype(F32)).astype(BF16)
    w_kv = w_qkv[:, pl.ds(width, 2 * width)]
    three = dot_nt(jnp.concatenate([first, second, third], 0), w_kv)
    grad_normed = three[:pad] + three[pad : 2 * pad] + three[2 * pad :]
    prompt_rows = prompts[...].astype(BF16).astype(F32)
    hat_p, rstd_p = normalize(prompt_rows)
    pgrad[...] = jnp.zeros_like(pgrad)
    pgrad[:count, :] = norm_back(hat_p, rstd_p, gain_one[...], grad_normed[:count, :])


def send_out(me, seq, value, wide, cbuf, outs):
    chunk = outs[0].shape[0]
    wide[...] = value
    for c in range(seq):
        cbuf[c] = wide[pl.ds(c * chunk, chunk), :].astype(BF16)
    for k in range(seq):
        outs[k][...] = cbuf[me ^ k]


def down_kernel(seq, act, resid, w_down, b_down, *refs):
    outs, (wide, cbuf) = refs[:seq], refs[seq:]
    value = resid[...] + dot(act[...], w_down[...]) + b_down[...]
    send_out(lax.axis_index("seq"), seq, value, wide, cbuf, outs)


def attn_back_kernel(p_bf, ds_bf, query, dmix, k_t, dqkv, q_t):
    rows, width = query.shape
    head = width // HEADS
    lane = lax.broadcasted_iota(jnp.int32, (rows, 2 * head), 1) // head
    for pair in range(HEADS // 2):
        cols = pl.ds(pair * 2 * head, 2 * head)
        qp = query[:, cols]
        gp = dmix[:, cols]
        gk = jnp.zeros((rows, 2 * head), F32)
        gv = jnp.zeros((rows, 2 * head), F32)
        for side in range(2):
            h = pair * 2 + side
            part = pl.ds(h * head, head)
            q_t[part, :] = dot(k_t[part, :], ds_bf[h]).astype(BF16)
            gk = gk + dot(ds_bf[h, :rows, :], jnp.where(lane == side, qp, jnp.zeros_like(qp)))
            gv = gv + dot(p_bf[h, :rows, :], jnp.where(lane == side, gp, jnp.zeros_like(gp)))
        dqkv[:, pl.ds(width + pair * 2 * head, 2 * head)] = gk.astype(BF16)
        dqkv[:, pl.ds(2 * width + pair * 2 * head, 2 * head)] = gv.astype(BF16)
    dqkv[:, :width] = q_t[...].T


def input_kernel(seq, dqkv, w_qkv, x, dres, gain, *refs):
    outs, (wide, cbuf) = refs[:seq], refs[seq:]
    hat, rstd = normalize(x[...])
    value = dres[...] + norm_back(hat, rstd, gain[...], dot_nt(dqkv[...], w_qkv[...]))
    send_out(lax.axis_index("seq"), seq, value, wide, cbuf, outs)


def place_kernel(seq, images, *refs):
    ins, (out, sem) = refs[:seq], refs[seq:]
    me = lax.axis_index("seq")

    def copy(k):
        return pltpu.make_async_copy(ins[k], out.at[me ^ k], sem.at[k])

    for k in range(seq):
        @pl.when((me ^ k) < images)
        def _():
            copy(k).start()

    for k in range(seq):
        @pl.when((me ^ k) < images)
        def _():
            copy(k).wait()


def final_kernel(
    total, mine, other, combined, start_t, prompts, momentum,
    basis_t, right_t, error, new_momentum, new_prompts, prompt_copy, whole,
):
    half = mine.shape[1]
    count, width = prompts.shape
    rank = start_t.shape[0]
    core = lax.rem(lax.axis_index("dp"), 2)
    whole[:, :half] = jnp.where(core == 0, mine[...], other[...])
    whole[:, half:] = jnp.where(core == 0, other[...], mine[...])
    summed = whole[...]
    left = dot_nt(start_t[...], summed, HIGHEST)
    row = lax.broadcasted_iota(jnp.int32, left.shape, 0)
    for j in range(rank):
        pivot = left[j : j + 1, :]
        pivot = pivot * lax.rsqrt(jnp.sum(pivot * pivot, axis=1, keepdims=True) + 1e-12)
        along = jnp.sum(left * pivot, axis=1, keepdims=True)
        left = jnp.where(row > j, left - along * pivot, jnp.where(row == j, pivot, left))
    right = jnp.dot(left, summed, precision=HIGHEST, preferred_element_type=F32)
    mine_w = combined[...]
    right_w = jnp.dot(left, mine_w, precision=HIGHEST, preferred_element_type=F32)
    error[:, 0, :] = (mine_w - dot_tn(left, right_w, HIGHEST))[:count, :]
    update = dot_tn(left, right, HIGHEST)[:count, :] / total
    moved = MOMENTUM_DECAY * momentum[...] + update
    fresh = prompts[...] - RATE_SCALE * math.sqrt(total) * moved
    basis_t[...] = left[:, :count]
    right_t[...] = right
    new_momentum[...] = moved
    new_prompts[...] = fresh
    prompt_copy[...] = fresh.astype(BF16)


def flip(k, n):
    return [(i, i ^ k) for i in range(n)]


def body(
    tokens,
    key_mask,
    prompts,
    gain_one,
    shift_one,
    w_qkv,
    b_qkv,
    w_out,
    b_out,
    gain_two,
    shift_two,
    w_up,
    b_up,
    w_down,
    b_down,
    cotangent,
    start_factor,
    error_buffer,
    momentum,
):
    images, chunk, width = tokens.shape
    seq = lax.axis_size("seq")
    dp = lax.axis_size("dp")
    rows = seq * chunk
    ff = w_up.shape[1]
    count = prompts.shape[0]
    if images > seq or seq & (seq - 1) or dp & (dp - 1):
        raise ValueError("unsupported mesh")
    nkeys = up(rows + count, 16)
    pad = up(count, 8)
    gain_one, shift_one, b_qkv, b_out, gain_two, shift_two, b_up, b_down = (
        v.reshape(1, -1)
        for v in (gain_one, shift_one, b_qkv, b_out, gain_two, shift_two, b_up, b_down)
    )

    piece = ((chunk, width), BF16)
    picked = call(
        functools.partial(pick_kernel, seq, images),
        [piece] * (2 * seq),
        (tokens, cotangent),
        [pltpu.SemaphoreType.DMA((2 * seq,))],
        in_specs=[ANY] * 2,
        name="pick",
    )
    toks, cots = [picked[0]], [picked[1]]
    for k in range(1, seq):
        pairs = [(a, b) for a, b in flip(k, seq) if b < images]
        toks.append(lax.ppermute(picked[2 * k], "seq", pairs))
    for k in range(1, seq):
        pairs = [(a, b) for a, b in flip(k, seq) if b < images]
        cots.append(lax.ppermute(picked[2 * k + 1], "seq", pairs))

    (pkv,) = call(
        prompt_kernel,
        [((up(count, 16), 2 * width), BF16)],
        (prompts, gain_one, shift_one, w_qkv, b_qkv, w_out, w_up, w_down),
        flops=2 * count * width * 2 * width,
        name="prompt_kv",
    )

    outs = [
        ((pad, width), F32),
        ((rows, ff), BF16),
        ((rows, width), F32),
        ((rows, width), F32),
        ((HEADS, nkeys, rows), BF16),
        ((HEADS, nkeys, rows), BF16),
        ((rows, width), BF16),
        ((rows, width), BF16),
        ((width, nkeys), BF16),
        ((rows, width), F32),
    ]
    pgrad, act, resid, dres, p_bf, ds_bf, query, dmix, k_t, x = call(
        functools.partial(main_kernel, seq, images),
        outs,
        (
            *toks, *cots, key_mask, pkv, prompts, gain_one, shift_one, w_qkv, b_qkv, w_out, b_out,
            gain_two, shift_two, w_up, b_up, w_down,
        ),
        [
            pltpu.VMEM((rows, width), F32),
            pltpu.VMEM((seq, chunk, width), BF16),
            pltpu.VMEM((nkeys, width), BF16),
            pltpu.VMEM((nkeys, width), BF16),
            pltpu.VMEM((width, nkeys), BF16),
            pltpu.VMEM((width, rows), BF16),
            pltpu.VMEM((HEADS, nkeys, rows), F32),
            pltpu.VMEM((rows, ff), BF16),
            pltpu.VMEM((rows, width), BF16),
        ],
        flops=2 * rows * width * (4 * width + 3 * ff),
        vmem=24 * MIB,
        name="layer",
    )

    combined = pgrad
    for k in range(1, seq):
        combined = combined + lax.ppermute(pgrad, "seq", flip(k, seq))
    padded_error = jnp.pad(error_buffer[0], ((0, pad - count), (0, 0)))
    combined = combined + padded_error
    half = width // 2
    core = lax.rem(lax.axis_index("dp"), 2)
    keep = lax.dynamic_slice(combined, (0, core * half), (pad, half))
    give = lax.dynamic_slice(combined, (0, (1 - core) * half), (pad, half))
    mine = keep + lax.ppermute(give, "dp", flip(1, dp))
    bit = 2
    while bit < dp:
        steps = [bit, 2 * bit, 3 * bit] if 2 * bit < dp else [bit]
        mine = mine + sum(lax.ppermute(mine, "dp", flip(k, dp)) for k in steps)
        bit *= 4 if 2 * bit < dp else 2
    other = lax.ppermute(mine, "dp", flip(1, dp))

    low_chunks = call(
        functools.partial(down_kernel, seq),
        [piece] * seq,
        (act, resid, w_down, b_down),
        [pltpu.VMEM((rows, width), F32), pltpu.VMEM((seq, chunk, width), BF16)],
        flops=2 * rows * width * ff,
        name="down",
    )
    (dqkv,) = call(
        attn_back_kernel,
        [((rows, 3 * width), BF16)],
        (p_bf, ds_bf, query, dmix, k_t),
        [pltpu.VMEM((width, rows), BF16)],
        flops=6 * rows * width * nkeys,
        name="attn_back",
    )
    grad_chunks = call(
        functools.partial(input_kernel, seq),
        [piece] * seq,
        (dqkv, w_qkv, x, dres, gain_one),
        [pltpu.VMEM((rows, width), F32), pltpu.VMEM((seq, chunk, width), BF16)],
        flops=6 * rows * width * width,
        name="input_grad",
    )
    results = []
    for chunks in (low_chunks, grad_chunks):
        back = [chunks[0]]
        for k in range(1, seq):
            pairs = [(a, b) for a, b in flip(k, seq) if a < images]
            back.append(lax.ppermute(chunks[k], "seq", pairs))
        (placed,) = call(
            functools.partial(place_kernel, seq, images),
            [((images, chunk, width), BF16)],
            back,
            [pltpu.SemaphoreType.DMA((seq,))],
            in_specs=[ANY] * seq,
            out_specs=[ANY],
            name="place",
        )
        results.append(placed)
    layer_out, input_grad = results

    rank = start_factor.shape[1]
    basis_t, right_t, error, new_momentum, new_prompts, prompt_copy = call(
        functools.partial(final_kernel, images * dp),
        [
            ((rank, count), F32),
            ((rank, width), F32),
            ((count, 1, width), F32),
            ((count, width), F32),
            ((count, width), F32),
            ((count, width), BF16),
        ],
        (mine, other, combined, start_factor.T, prompts, momentum),
        [pltpu.VMEM((pad, width), F32)],
        name="final",
    )
    return (
        layer_out,
        input_grad,
        basis_t.T,
        right_t.T,
        error.transpose(1, 0, 2),
        new_momentum,
        new_prompts,
        prompt_copy,
    )


def solution(mesh):
    rep = P()
    rows = P("dp", "seq", None)
    placed = (rows, P("dp", None), *([rep] * 13), rows, rep, P("dp", None, None), rep)
    return jax.shard_map(
        body,
        mesh=mesh,
        in_specs=placed,
        out_specs=(rows, rows, rep, rep, P("dp", None, None), rep, rep, rep),
        check_vma=False,
    )
```

time: 413 us -> 119 us (0.29)
  the two profiles are of different devices: /device:TPU:0 before, /device:TPU:28 now
where the time goes in v1:
time: 119 us; the launch traced here: 118 us
  starting transfers between devices  42.5 us (36%)
  local copies, waits for them, and re-layouts  34.3 us (29%)
  Pallas kernels  26.2 us (22%)
  waiting for transfers between devices  11.7 us (10%)
  other arithmetic  2.27 us (2%)
    unnamed x81, local copies, waits for them, and re-layouts  29.5 us
    pallas_call x9, Pallas kernels, call(): pl.pallas_call(kernel, out_shape=[jax.ShapeDtypeStruct(s, d) for s, d in...  26.2 us
    ppermute x6, starting transfers between devices, body(): back.append(lax.ppermute(chunks[k], 'seq', pairs))  17.6 us
    ppermute x3, starting transfers between devices, body(): cots.append(lax.ppermute(picked[2 * k + 1], 'seq', pairs))  9.21 us
    ppermute x3, starting transfers between devices, body(): toks.append(lax.ppermute(picked[2 * k], 'seq', pairs))  7.73 us
    ppermute x3, waiting for transfers between devices, body(): combined = combined + lax.ppermute(pgrad, 'seq', flip(k, seq))  5.46 us
    ppermute x6, waiting for transfers between devices, body(): back.append(lax.ppermute(chunks[k], 'seq', pairs))  4.59 us
    ppermute x3, starting transfers between devices, body(): mine = mine + sum((lax.ppermute(mine, 'dp', flip(k, dp)) for k in steps))  4.45 us
  transfers between devices with their start and end apart: 20, of which 5 were waited for; matrix products, arithmetic and copies ran while one was open for 4% of the time, Pallas kernels for 5%

profile of v1, /device:TPU:28, one launch (start us, length us, event | category | flops | bytes accessed | tf_op | source)
XLA Modules:
  0.0 118.2 jit_solution(12590382800191200761)
XLA Ops:
  0.6 0.9 copy-done.32
  1.6 0.9 copy-done.33
  2.5 0.9 pick.1
  3.5 1.3 %collective-permute-start = (bf16[52,768]{1,0:T(8,128)(2,1)S(1)}, bf16[52,768]{1,0:T(8,128)(2,1)S(1)}, u32[]{:S(2)}, u32[]{:S(2)}) collective-permute-start(bf16[52,768]{1,0:T(8,128)(2,1)S(1)} %get-tuple-element.41), channel_id=1, source_target_pairs={{0,8},{8,0},{24,16},{1,9},{9,1},{25,17},{2,10},{10,2},{26,18},{3,1... | collective-permute-start | bytes 239624 | tf_op jit(solution)/shard_map/ppermute | solution.py:404
  4.8 4.5 %collective-permute-start.1 = (bf16[52,768]{1,0:T(8,128)(2,1)S(1)}, bf16[52,768]{1,0:T(8,128)(2,1)S(1)}, u32[]{:S(2)}, u32[]{:S(2)}) collective-permute-start(bf16[52,768]{1,0:T(8,128)(2,1)S(1)} %get-tuple-element.42), channel_id=1, source_target_pairs={{0,16},{16,0},{24,8},{1,17},{17,1},{25,9},{2,18},{18,2},{26,10},{3... | collective-permute-start | bytes 239624 | tf_op jit(solution)/shard_map/ppermute | solution.py:404
  9.3 1.9 %collective-permute-start.2 = (bf16[52,768]{1,0:T(8,128)(2,1)S(1)}, bf16[52,768]{1,0:T(8,128)(2,1)S(1)}, u32[]{:S(2)}, u32[]{:S(2)}) collective-permute-start(bf16[52,768]{1,0:T(8,128)(2,1)S(1)} %get-tuple-element.43), channel_id=1, source_target_pairs={{8,16},{16,8},{24,0},{9,17},{17,9},{25,1},{10,18},{18,10},{26,2},{... | collective-permute-start | bytes 239624 | tf_op jit(solution)/shard_map/ppermute | solution.py:404
  11.2 1.3 %collective-permute-start.3 = (bf16[52,768]{1,0:T(8,128)(2,1)S(1)}, bf16[52,768]{1,0:T(8,128)(2,1)S(1)}, u32[]{:S(2)}, u32[]{:S(2)}) collective-permute-start(bf16[52,768]{1,0:T(8,128)(2,1)S(1)} %get-tuple-element.45), channel_id=1, source_target_pairs={{0,8},{8,0},{24,16},{1,9},{9,1},{25,17},{2,10},{10,2},{26,18},{3,1... | collective-permute-start | bytes 239624 | tf_op jit(solution)/shard_map/ppermute | solution.py:407
  12.5 6.0 %collective-permute-start.4 = (bf16[52,768]{1,0:T(8,128)(2,1)S(1)}, bf16[52,768]{1,0:T(8,128)(2,1)S(1)}, u32[]{:S(2)}, u32[]{:S(2)}) collective-permute-start(bf16[52,768]{1,0:T(8,128)(2,1)S(1)} %get-tuple-element.46), channel_id=1, source_target_pairs={{0,16},{16,0},{24,8},{1,17},{17,1},{25,9},{2,18},{18,2},{26,10},{3... | collective-permute-start | bytes 239624 | tf_op jit(solution)/shard_map/ppermute | solution.py:407
  18.6 1.9 %collective-permute-start.5 = (bf16[52,768]{1,0:T(8,128)(2,1)S(1)}, bf16[52,768]{1,0:T(8,128)(2,1)S(1)}, u32[]{:S(2)}, u32[]{:S(2)}) collective-permute-start(bf16[52,768]{1,0:T(8,128)(2,1)S(1)} %get-tuple-element.47), channel_id=1, source_target_pairs={{8,16},{16,8},{24,0},{9,17},{17,9},{25,1},{10,18},{18,10},{26,2},{... | collective-permute-start | bytes 239624 | tf_op jit(solution)/shard_map/ppermute | solution.py:407
  24.6 2.3 %copy-done = bf16[3072,768]{1,0:T(8,128)(2,1)S(1)} copy-done((bf16[3072,768]{1,0:T(8,128)(2,1)S(1)}, bf16[3072,768]{1,0:T(8,128)(2,1)}, u32[]{:S(2)}) %copy-start) | copy-done | bytes 4718616
  27.0 2.0 %copy-done.3 = bf16[768,2304]{1,0:T(8,128)(2,1)S(1)} copy-done((bf16[768,2304]{1,0:T(8,128)(2,1)S(1)}, bf16[768,2304]{1,0:T(8,128)(2,1)}, u32[]{:S(2)}) %copy-start.3) | copy-done | bytes 3538968
  29.0 2.3 %copy-done.5 = bf16[768,3072]{1,0:T(8,128)(2,1)S(1)} copy-done((bf16[768,3072]{1,0:T(8,128)(2,1)S(1)}, bf16[768,3072]{1,0:T(8,128)(2,1)}, u32[]{:S(2)}) %copy-start.5) | copy-done | bytes 4718616
  31.3 1.3 %copy-done.7 = bf16[768,768]{1,0:T(8,128)(2,1)S(1)} copy-done((bf16[768,768]{1,0:T(8,128)(2,1)S(1)}, bf16[768,768]{1,0:T(8,128)(2,1)}, u32[]{:S(2)}) %copy-start.7) | copy-done | bytes 1179672
  32.6 0.9 copy-done.15
  34.3 1.5 %copy-done.1 = bf16[3072,768]{1,0:T(8,128)(2,1)S(1)} copy-done((bf16[3072,768]{1,0:T(8,128)(2,1)S(1)}, bf16[3072,768]{1,0:T(8,128)(2,1)}, u32[]{:S(2)}) %copy-start.1) | copy-done | bytes 4718616
  35.8 1.1 copy-done.4
  37.0 1.3 %copy-done.6 = bf16[768,3072]{1,0:T(8,128)(2,1)S(1)} copy-done((bf16[768,3072]{1,0:T(8,128)(2,1)S(1)}, bf16[768,3072]{1,0:T(8,128)(2,1)}, u32[]{:S(2)}) %copy-start.6) | copy-done | bytes 4718616
  38.6 16.0 %layer.1 = (f32[56,768]{1,0:T(8,128)}, bf16[208,3072]{1,0:T(8,128)(2,1)S(1)}, f32[208,768]{1,0:T(8,128)S(1)}, f32[208,768]{1,0:T(8,128)S(1)}, bf16[12,272,208]{2...) custom-call(bf16[52,768]{1,0:T(8,128)(2,1)S(1)} %get-tuple-element.4, ...), custom_call_target="tpu_custom_call" | custom-call | flops 3925868544 | bytes 15184320 | tf_op jit(solution)/shard_map/layer/pallas_call | solution.py:59
  54.5 1.2 %copy-done.9 = bf16[12,272,208]{2,1,0:T(8,128)(2,1)} copy-done((bf16[12,272,208]{2,1,0:T(8,128)(2,1)}, bf16[12,272,208]{2,1,0:T(8,128)(2,1)S(1)}, u32[]{:S(2)}) %copy-start.9) | copy-done | bytes 1357848
  55.8 1.2 %copy-done.11 = bf16[12,272,208]{2,1,0:T(8,128)(2,1)} copy-done((bf16[12,272,208]{2,1,0:T(8,128)(2,1)}, bf16[12,272,208]{2,1,0:T(8,128)(2,1)S(1)}, u32[]{:S(2)}) %copy-start.11) | copy-done | bytes 1357848
  57.0 1.1 copy-done.18
  58.0 0.8 copy-done.20
  58.9 0.8 copy-done.22
  59.7 0.8 copy-done.24
  60.6 0.8 copy-done.26
  61.4 0.8 copy-done.28
  62.1 0.8 copy-done.30
  62.9 2.9 %collective-permute-start.14 = (f32[56,768]{1,0:T(8,128)}, f32[56,768]{1,0:T(8,128)}, u32[]{:S(2)}, u32[]{:S(2)}) collective-permute-start(f32[56,768]{1,0:T(8,128)} %get-tuple-element.65), channel_id=1, source_target_pairs={{0,24},{8,16},{16,8},{24,0},{1,25},{9,17},{17,9},{25,1},{2,26},{10... | collective-permute-start | bytes 516104 | tf_op jit(solution)/shard_map/ppermute | solution.py:454
  67.1 4.2 %collective-permute-done.14 = f32[56,768]{1,0:T(8,128)} collective-permute-done((f32[56,768]{1,0:T(8,128)}, f32[56,768]{1,0:T(8,128)}, u32[]{:S(2)}, u32[]{:S(2)}) %collective-permute-start.14) | collective-permute-done | bytes 172064 | tf_op jit(solution)/shard_map/ppermute | solution.py:454
  71.3 1.3 %collective-permute-done.13 = f32[56,768]{1,0:T(8,128)} collective-permute-done((f32[56,768]{1,0:T(8,128)}, f32[56,768]{1,0:T(8,128)}, u32[]{:S(2)}, u32[]{:S(2)}) %collective-permute-start.13) | collective-permute-done | bytes 172064 | tf_op jit(solution)/shard_map/ppermute | solution.py:454
  72.5 1.3 %pad_add_fusion.combined = f32[56,768]{1,0:T(8,128)S(1)} fusion(f32[50,768]{1,0:T(8,128)} %bitcast.10, f32[56,768]{1,0:T(8,128)} %collective-permute-done.14, f32[56,768]{1,0:T(8,128)} %collective-permute-done.13, f32[56,768]{1,0:T(8,128)} %get-tuple-element.65, f32[56,768]{1,0:T(8,128)} %collective-permute-done.12), kind=kLoop, calls=%fused_computation.1 | loop fusion | flops 172032 | bytes 1013760 | tf_op jit(solution)/shard_map/add | solution.py:456
  75.2 1.6 %collective-permute-done.15 = f32[56,384]{1,0:T(8,128)} collective-permute-done((f32[56,384]{1,0:T(8,128)}, f32[56,384]{1,0:T(8,128)}, u32[]{:S(2)}, u32[]{:S(2)}) %collective-permute-start.15) | collective-permute-done | bytes 86048 | tf_op jit(solution)/shard_map/ppermute | solution.py:461
  76.8 0.9 dynamic-slice_add_fusion
  78.7 3.5 %collective-permute-start.17 = (f32[56,384]{1,0:T(8,128)S(1)}, f32[56,384]{1,0:T(8,128)S(1)}, u32[]{:S(2)}, u32[]{:S(2)}) collective-permute-start(f32[56,384]{1,0:T(8,128)S(1)} %dynamic-slice_add_fusion), channel_id=1, source_target_pairs={{0,4},{1,5},{2,6},{3,7},{4,0},{5,1},{6,2},{7,3},{8,12},{9,13},{10,... | collective-permute-start | bytes 258056 | tf_op jit(solution)/shard_map/ppermute | solution.py:465
  82.2 2.3 %copy-done.2 = bf16[3072,768]{1,0:T(8,128)(2,1)S(1)} copy-done((bf16[3072,768]{1,0:T(8,128)(2,1)S(1)}, bf16[3072,768]{1,0:T(8,128)(2,1)}, u32[]{:S(2)}) %copy-start.2) | copy-done | bytes 4718616
  84.5 1.3 %copy-done.19 = bf16[208,3072]{1,0:T(8,128)(2,1)S(1)} copy-done((bf16[208,3072]{1,0:T(8,128)(2,1)S(1)}, bf16[208,3072]{1,0:T(8,128)(2,1)}, u32[]{:S(2)}) %copy-start.19) | copy-done | bytes 1277976
  85.8 1.1 copy-done.25
  86.9 1.2 %down.1 = (bf16[52,768]{1,0:T(8,128)(2,1)S(1)}, bf16[52,768]{1,0:T(8,128)(2,1)S(1)}, bf16[52,768]{1,0:T(8,128)(2,1)S(1)}, bf16[52,768]{1,0:T(8,128)(2,1)S(1)}) custom-call(bf16[208,3072]{1,0:T(8,128)(2,1)S(1)} %copy-done.19, f32[208,768]{1,0:T(8,128)S(1)} %copy-done.25, bf16[3072,768]{1,0:T(8,128)(2,1)S(1)} %copy-done.2, f32[1,768]{1,0:T(1,128)S(1)} %reshape.47.b_down), custom_call_target="tpu_custom_call" | custom-call | flops 981467136 | bytes 6638592 | tf_op jit(solution)/shard_map/down/pallas_call | solution.py:59
  88.1 3.9 %collective-permute-start.6 = (bf16[52,768]{1,0:T(8,128)(2,1)S(1)}, bf16[52,768]{1,0:T(8,128)(2,1)S(1)}, u32[]{:S(2)}, u32[]{:S(2)}) collective-permute-start(bf16[52,768]{1,0:T(8,128)(2,1)S(1)} %get-tuple-element.51), channel_id=1, source_target_pairs={{0,8},{8,0},{16,24},{1,9},{9,1},{17,25},{2,10},{10,2},{18,26},{3,1... | collective-permute-start | bytes 239624 | tf_op jit(solution)/shard_map/ppermute | solution.py:498
  92.0 2.6 %collective-permute-start.7 = (bf16[52,768]{1,0:T(8,128)(2,1)S(1)}, bf16[52,768]{1,0:T(8,128)(2,1)S(1)}, u32[]{:S(2)}, u32[]{:S(2)}) collective-permute-start(bf16[52,768]{1,0:T(8,128)(2,1)S(1)} %get-tuple-element.52), channel_id=1, source_target_pairs={{0,16},{8,24},{16,0},{1,17},{9,25},{17,1},{2,18},{10,26},{18,2},{3... | collective-permute-start | bytes 239624 | tf_op jit(solution)/shard_map/ppermute | solution.py:498
  94.7 1.3 %attn_back.1.dqkv = bf16[208,2304]{1,0:T(8,128)(2,1)S(1)} custom-call(bf16[12,272,208]{2,1,0:T(8,128)(2,1)S(1)} %copy-done.10, bf16[12,272,208]{2,1,0:T(8,128)(2,1)S(1)} %copy-done.12, bf16[208,768]{1,0:T(8,128)(2,1)S(1)} %copy-done.29, bf16[208,768]{1,0:T(8,128)(2,1)S(1)} %copy-done.31, bf16[768,272]{1,0:T(8,128)(2,1)S(1)} %copy-done.27), custom_call_target="tpu_custom_call" | custom-call | flops 260702208 | bytes 3772416 | tf_op jit(solution)/shard_map/attn_back/pallas_call | solution.py:59
  95.9 2.3 %collective-permute-start.8 = (bf16[52,768]{1,0:T(8,128)(2,1)S(1)}, bf16[52,768]{1,0:T(8,128)(2,1)S(1)}, u32[]{:S(2)}, u32[]{:S(2)}) collective-permute-start(bf16[52,768]{1,0:T(8,128)(2,1)S(1)} %get-tuple-element.53), channel_id=1, source_target_pairs={{0,24},{8,16},{16,8},{1,25},{9,17},{17,9},{2,26},{10,18},{18,10},{... | collective-permute-start | bytes 239624 | tf_op jit(solution)/shard_map/ppermute | solution.py:498
  98.4 1.6 %input_grad.1 = (bf16[52,768]{1,0:T(8,128)(2,1)S(1)}, bf16[52,768]{1,0:T(8,128)(2,1)S(1)}, bf16[52,768]{1,0:T(8,128)(2,1)S(1)}, bf16[52,768]{1,0:T(8,128)(2,1)S(1)}) custom-call(bf16[208,2304]{1,0:T(8,128)(2,1)S(1)} %attn_back.1.dqkv, bf16[768,2304]{1,0:T(8,128)(2,1)S(1)} %copy-done.4, f32[208,768]{1,0:T(8,128)S(1)} %copy-done.23, ...), custom_call_target="tpu_custom_call" | custom-call | flops 736100352 | bytes 5778432 | tf_op jit(solution)/shard_map/input_grad/pallas_call | solution.py:59
  100.0 1.3 %collective-permute-start.9 = (bf16[52,768]{1,0:T(8,128)(2,1)S(1)}, bf16[52,768]{1,0:T(8,128)(2,1)S(1)}, u32[]{:S(2)}, u32[]{:S(2)}) collective-permute-start(bf16[52,768]{1,0:T(8,128)(2,1)S(1)} %get-tuple-element.62), channel_id=1, source_target_pairs={{0,8},{8,0},{16,24},{1,9},{9,1},{17,25},{2,10},{10,2},{18,26},{3,1... | collective-permute-start | bytes 239624 | tf_op jit(solution)/shard_map/ppermute | solution.py:498
  101.3 5.7 %collective-permute-start.10 = (bf16[52,768]{1,0:T(8,128)(2,1)S(1)}, bf16[52,768]{1,0:T(8,128)(2,1)S(1)}, u32[]{:S(2)}, u32[]{:S(2)}) collective-permute-start(bf16[52,768]{1,0:T(8,128)(2,1)S(1)} %get-tuple-element.63), channel_id=1, source_target_pairs={{0,16},{8,24},{16,0},{1,17},{9,25},{17,1},{2,18},{10,26},{18,2},{3... | collective-permute-start | bytes 239624 | tf_op jit(solution)/shard_map/ppermute | solution.py:498
  107.0 1.9 %collective-permute-start.11 = (bf16[52,768]{1,0:T(8,128)(2,1)S(1)}, bf16[52,768]{1,0:T(8,128)(2,1)S(1)}, u32[]{:S(2)}, u32[]{:S(2)}) collective-permute-start(bf16[52,768]{1,0:T(8,128)(2,1)S(1)} %get-tuple-element.64), channel_id=1, source_target_pairs={{0,24},{8,16},{16,8},{1,25},{9,17},{17,9},{2,26},{10,18},{18,10},{... | collective-permute-start | bytes 239624 | tf_op jit(solution)/shard_map/ppermute | solution.py:498
  109.8 4.4 %collective-permute-done.11.refs_3_ = bf16[52,768]{1,0:T(8,128)(2,1)S(1)} collective-permute-done((bf16[52,768]{1,0:T(8,128)(2,1)S(1)}, bf16[52,768]{1,0:T(8,128)(2,1)S(1)}, u32[]{:S(2)}, u32[]{:S(2)}) %collective-permute-start.11) | collective-permute-done | bytes 79904 | tf_op jit(solution)/shard_map/ppermute | solution.py:498
  115.1 3.1 %final.1 = (f32[8,50]{1,0:T(8,128)}, f32[8,768]{1,0:T(8,128)}, f32[50,1,768]{2,1,0:T(1,128)}, f32[50,768]{1,0:T(8,128)}, f32[50,768]{1,0:T(8,128)}, /*index=5*/bf16[50,768]{1,0:T(8,128)(2,1)}) custom-call(f32[56,384]{1,0:T(8,128)S(1)} %add_add_fusion.mine, f32[56,384]{1,0:T(8,128)S(1)} %collective-permute-done.19.other, f32[56,768]{1,0:T(8,128)S(1)} %copy-done.14, ...), custom_call_target="tpu_custom_call" | custom-call | bytes 675840 | tf_op jit(solution)/shard_map/final/pallas_call | solution.py:59
  (93 shorter events, 10.5 us)
Async XLA Ops:
  3.5 15.1 %collective-permute-start = (bf16[52,768]{1,0:T(8,128)(2,1)S(1)}, bf16[52,768]{1,0:T(8,128)(2,1)S(1)}, u32[]{:S(2)}, u32[]{:S(2)}) collective-permute-start(bf16[52,768]{1,0:T(8,128)(2,1)S(1)} %get-tuple-element.41), channel_id=1, source_target_pairs={{0,8},{8,0},{24,16},{1,9},{9,1},{25,17},{2,10},{10,2},{26,18},{3,1... | collective-permute-start | bytes 239624 | tf_op jit(solution)/shard_map/ppermute | solution.py:404
  4.8 29.5 %collective-permute-start.1 = (bf16[52,768]{1,0:T(8,128)(2,1)S(1)}, bf16[52,768]{1,0:T(8,128)(2,1)S(1)}, u32[]{:S(2)}, u32[]{:S(2)}) collective-permute-start(bf16[52,768]{1,0:T(8,128)(2,1)S(1)} %get-tuple-element.42), channel_id=1, source_target_pairs={{0,16},{16,0},{24,8},{1,17},{17,1},{25,9},{2,18},{18,2},{26,10},{3... | collective-permute-start | bytes 239624 | tf_op jit(solution)/shard_map/ppermute | solution.py:404
  9.3 25.0 %collective-permute-start.2 = (bf16[52,768]{1,0:T(8,128)(2,1)S(1)}, bf16[52,768]{1,0:T(8,128)(2,1)S(1)}, u32[]{:S(2)}, u32[]{:S(2)}) collective-permute-start(bf16[52,768]{1,0:T(8,128)(2,1)S(1)} %get-tuple-element.43), channel_id=1, source_target_pairs={{8,16},{16,8},{24,0},{9,17},{17,9},{25,1},{10,18},{18,10},{26,2},{... | collective-permute-start | bytes 239624 | tf_op jit(solution)/shard_map/ppermute | solution.py:404
  11.2 23.0 %collective-permute-start.3 = (bf16[52,768]{1,0:T(8,128)(2,1)S(1)}, bf16[52,768]{1,0:T(8,128)(2,1)S(1)}, u32[]{:S(2)}, u32[]{:S(2)}) collective-permute-start(bf16[52,768]{1,0:T(8,128)(2,1)S(1)} %get-tuple-element.45), channel_id=1, source_target_pairs={{0,8},{8,0},{24,16},{1,9},{9,1},{25,17},{2,10},{10,2},{26,18},{3,1... | collective-permute-start | bytes 239624 | tf_op jit(solution)/shard_map/ppermute | solution.py:407
  12.5 21.7 %collective-permute-start.4 = (bf16[52,768]{1,0:T(8,128)(2,1)S(1)}, bf16[52,768]{1,0:T(8,128)(2,1)S(1)}, u32[]{:S(2)}, u32[]{:S(2)}) collective-permute-start(bf16[52,768]{1,0:T(8,128)(2,1)S(1)} %get-tuple-element.46), channel_id=1, source_target_pairs={{0,16},{16,0},{24,8},{1,17},{17,1},{25,9},{2,18},{18,2},{26,10},{3... | collective-permute-start | bytes 239624 | tf_op jit(solution)/shard_map/ppermute | solution.py:407
  18.6 15.7 %collective-permute-start.5 = (bf16[52,768]{1,0:T(8,128)(2,1)S(1)}, bf16[52,768]{1,0:T(8,128)(2,1)S(1)}, u32[]{:S(2)}, u32[]{:S(2)}) collective-permute-start(bf16[52,768]{1,0:T(8,128)(2,1)S(1)} %get-tuple-element.47), channel_id=1, source_target_pairs={{8,16},{16,8},{24,0},{9,17},{17,9},{25,1},{10,18},{18,10},{26,2},{... | collective-permute-start | bytes 239624 | tf_op jit(solution)/shard_map/ppermute | solution.py:407
  24.6 2.3 %copy-start = (bf16[3072,768]{1,0:T(8,128)(2,1)S(1)}, bf16[3072,768]{1,0:T(8,128)(2,1)}, u32[]{:S(2)}) copy-start(bf16[3072,768]{1,0:T(8,128)(2,1)} %w_down.3) | copy-start | bytes 14155780
  27.0 2.0 %copy-start.3 = (bf16[768,2304]{1,0:T(8,128)(2,1)S(1)}, bf16[768,2304]{1,0:T(8,128)(2,1)}, u32[]{:S(2)}) copy-start(bf16[768,2304]{1,0:T(8,128)(2,1)} %w_qkv.3) | copy-start | bytes 10616836
  29.0 2.3 %copy-start.5 = (bf16[768,3072]{1,0:T(8,128)(2,1)S(1)}, bf16[768,3072]{1,0:T(8,128)(2,1)}, u32[]{:S(2)}) copy-start(bf16[768,3072]{1,0:T(8,128)(2,1)} %refs_19_.1) | copy-start | bytes 14155780
  31.3 1.3 %copy-start.7 = (bf16[768,768]{1,0:T(8,128)(2,1)S(1)}, bf16[768,768]{1,0:T(8,128)(2,1)}, u32[]{:S(2)}) copy-start(bf16[768,768]{1,0:T(8,128)(2,1)} %refs_15_.1) | copy-start | bytes 3538948
  33.5 2.3 %copy-start.1 = (bf16[3072,768]{1,0:T(8,128)(2,1)S(1)}, bf16[3072,768]{1,0:T(8,128)(2,1)}, u32[]{:S(2)}) copy-start(bf16[3072,768]{1,0:T(8,128)(2,1)} %w_down.3) | copy-start | bytes 14155780
  33.5 3.4 %copy-start.4 = (bf16[768,2304]{1,0:T(8,128)(2,1)S(1)}, bf16[768,2304]{1,0:T(8,128)(2,1)}, u32[]{:S(2)}) copy-start(bf16[768,2304]{1,0:T(8,128)(2,1)} %w_qkv.3) | copy-start | bytes 10616836
  33.5 4.8 %copy-start.6 = (bf16[768,3072]{1,0:T(8,128)(2,1)S(1)}, bf16[768,3072]{1,0:T(8,128)(2,1)}, u32[]{:S(2)}) copy-start(bf16[768,3072]{1,0:T(8,128)(2,1)} %refs_19_.1) | copy-start | bytes 14155780
  33.5 5.0 %copy-start.8 = (bf16[768,768]{1,0:T(8,128)(2,1)S(1)}, bf16[768,768]{1,0:T(8,128)(2,1)}, u32[]{:S(2)}) copy-start(bf16[768,768]{1,0:T(8,128)(2,1)} %refs_15_.1) | copy-start | bytes 3538948
  33.5 5.0 %copy-start.16 = (f32[50,768]{1,0:T(8,128)S(1)}, f32[50,768]{1,0:T(8,128)}, u32[]{:S(2)}) copy-start(f32[50,768]{1,0:T(8,128)} %prompts.3) | copy-start | bytes 460804
  33.5 5.0 %copy-start.36 = (f32[3072]{0:T(1024)S(1)}, f32[3072]{0:T(1024)}, u32[]{:S(2)}) copy-start(f32[3072]{0:T(1024)} %param.31) | copy-start | bytes 36868
  33.5 5.0 %copy-start.37 = (s32[3,208]{1,0:T(4,128)S(1)}, s32[3,208]{1,0:T(4,128)}, u32[]{:S(2)}) copy-start(s32[3,208]{1,0:T(4,128)} %refs_8_.1) | copy-start | bytes 7492
  38.6 27.8 %copy-start.38 = (f32[1,50,768]{2,0,1:T(1,128)S(1)}, f32[1,50,768]{2,0,1:T(1,128)}, u32[]{:S(2)}) copy-start(f32[1,50,768]{2,0,1:T(1,128)} %param.36) | copy-start | bytes 460804
  38.6 36.6 %copy-start.39 = (f32[768]{0:T(1024)S(1)}, f32[768]{0:T(1024)}, u32[]{:S(2)}) copy-start(f32[768]{0:T(1024)} %param.33) | copy-start | bytes 9220
  54.5 1.2 %copy-start.9 = (bf16[12,272,208]{2,1,0:T(8,128)(2,1)}, bf16[12,272,208]{2,1,0:T(8,128)(2,1)S(1)}, u32[]{:S(2)}) copy-start(bf16[12,272,208]{2,1,0:T(8,128)(2,1)S(1)} %get-tuple-element.54.p_bf) | copy-start | bytes 4073476
  55.8 1.2 %copy-start.11 = (bf16[12,272,208]{2,1,0:T(8,128)(2,1)}, bf16[12,272,208]{2,1,0:T(8,128)(2,1)S(1)}, u32[]{:S(2)}) copy-start(bf16[12,272,208]{2,1,0:T(8,128)(2,1)S(1)} %get-tuple-element.55.ds_bf) | copy-start | bytes 4073476
  62.9 8.4 %collective-permute-start.14 = (f32[56,768]{1,0:T(8,128)}, f32[56,768]{1,0:T(8,128)}, u32[]{:S(2)}, u32[]{:S(2)}) collective-permute-start(f32[56,768]{1,0:T(8,128)} %get-tuple-element.65), channel_id=1, source_target_pairs={{0,24},{8,16},{16,8},{24,0},{1,25},{9,17},{17,9},{25,1},{2,26},{10... | collective-permute-start | bytes 516104 | tf_op jit(solution)/shard_map/ppermute | solution.py:454
  65.8 6.7 %collective-permute-start.13 = (f32[56,768]{1,0:T(8,128)}, f32[56,768]{1,0:T(8,128)}, u32[]{:S(2)}, u32[]{:S(2)}) collective-permute-start(f32[56,768]{1,0:T(8,128)} %get-tuple-element.65), channel_id=1, source_target_pairs={{0,16},{8,24},{16,0},{24,8},{1,17},{9,25},{17,1},{25,9},{2,18},{10... | collective-permute-start | bytes 516104 | tf_op jit(solution)/shard_map/ppermute | solution.py:454
  65.8 6.7 %collective-permute-start.12 = (f32[56,768]{1,0:T(8,128)}, f32[56,768]{1,0:T(8,128)}, u32[]{:S(2)}, u32[]{:S(2)}) collective-permute-start(f32[56,768]{1,0:T(8,128)} %get-tuple-element.65), channel_id=1, source_target_pairs={{0,8},{8,0},{16,24},{24,16},{1,9},{9,1},{17,25},{25,17},{2,10},{10... | collective-permute-start | bytes 516104 | tf_op jit(solution)/shard_map/ppermute | solution.py:454
  75.2 1.6 %collective-permute-start.15 = (f32[56,384]{1,0:T(8,128)}, f32[56,384]{1,0:T(8,128)}, u32[]{:S(2)}, u32[]{:S(2)}) collective-permute-start(f32[56,384]{1,0:T(8,128)} %constant_dynamic-slice_fusion), channel_id=1, source_target_pairs={{0,1},{1,0},{2,3},{3,2},{4,5},{5,4},{6,7},{7,6},{8,9},{9,8},{10,11... | collective-permute-start | bytes 258056 | tf_op jit(solution)/shard_map/ppermute | solution.py:461
  77.7 18.2 %collective-permute-start.18 = (f32[56,384]{1,0:T(8,128)S(1)}, f32[56,384]{1,0:T(8,128)S(1)}, u32[]{:S(2)}, u32[]{:S(2)}) collective-permute-start(f32[56,384]{1,0:T(8,128)S(1)} %dynamic-slice_add_fusion), channel_id=1, source_target_pairs={{0,6},{1,7},{2,4},{3,5},{4,2},{5,3},{6,0},{7,1},{8,14},{9,15},{10,... | collective-permute-start | bytes 258056 | tf_op jit(solution)/shard_map/ppermute | solution.py:465
  78.0 20.2 %collective-permute-start.16 = (f32[56,384]{1,0:T(8,128)S(1)}, f32[56,384]{1,0:T(8,128)S(1)}, u32[]{:S(2)}, u32[]{:S(2)}) collective-permute-start(f32[56,384]{1,0:T(8,128)S(1)} %dynamic-slice_add_fusion), channel_id=1, source_target_pairs={{0,2},{1,3},{2,0},{3,1},{4,6},{5,7},{6,4},{7,5},{8,10},{9,11},{10,... | collective-permute-start | bytes 258056 | tf_op jit(solution)/shard_map/ppermute | solution.py:465
  78.7 19.6 %collective-permute-start.17 = (f32[56,384]{1,0:T(8,128)S(1)}, f32[56,384]{1,0:T(8,128)S(1)}, u32[]{:S(2)}, u32[]{:S(2)}) collective-permute-start(f32[56,384]{1,0:T(8,128)S(1)} %dynamic-slice_add_fusion), channel_id=1, source_target_pairs={{0,4},{1,5},{2,6},{3,7},{4,0},{5,1},{6,2},{7,3},{8,12},{9,13},{10,... | collective-permute-start | bytes 258056 | tf_op jit(solution)/shard_map/ppermute | solution.py:465
  82.2 2.3 %copy-start.2 = (bf16[3072,768]{1,0:T(8,128)(2,1)S(1)}, bf16[3072,768]{1,0:T(8,128)(2,1)}, u32[]{:S(2)}) copy-start(bf16[3072,768]{1,0:T(8,128)(2,1)} %w_down.3) | copy-start | bytes 14155780
  84.5 1.3 %copy-start.19 = (bf16[208,3072]{1,0:T(8,128)(2,1)S(1)}, bf16[208,3072]{1,0:T(8,128)(2,1)}, u32[]{:S(2)}) copy-start(bf16[208,3072]{1,0:T(8,128)(2,1)} %copy-done.18) | copy-start | bytes 3833860
  86.9 7.7 %copy-start.10 = (bf16[12,272,208]{2,1,0:T(8,128)(2,1)S(1)}, bf16[12,272,208]{2,1,0:T(8,128)(2,1)}, u32[]{:S(2)}) copy-start(bf16[12,272,208]{2,1,0:T(8,128)(2,1)} %copy-done.9) | copy-start | bytes 4073476
  86.9 7.7 %copy-start.12 = (bf16[12,272,208]{2,1,0:T(8,128)(2,1)S(1)}, bf16[12,272,208]{2,1,0:T(8,128)(2,1)}, u32[]{:S(2)}) copy-start(bf16[12,272,208]{2,1,0:T(8,128)(2,1)} %copy-done.11) | copy-start | bytes 4073476
  86.9 7.7 %copy-start.27 = (bf16[768,272]{1,0:T(8,128)(2,1)S(1)}, bf16[768,272]{1,0:T(8,128)(2,1)}, u32[]{:S(2)}) copy-start(bf16[768,272]{1,0:T(8,128)(2,1)} %copy-done.26) | copy-start | bytes 1253380
  86.9 7.7 %copy-start.29 = (bf16[208,768]{1,0:T(8,128)(2,1)S(1)}, bf16[208,768]{1,0:T(8,128)(2,1)}, u32[]{:S(2)}) copy-start(bf16[208,768]{1,0:T(8,128)(2,1)} %copy-done.28) | copy-start | bytes 958468
  86.9 7.7 %copy-start.31 = (bf16[208,768]{1,0:T(8,128)(2,1)S(1)}, bf16[208,768]{1,0:T(8,128)(2,1)}, u32[]{:S(2)}) copy-start(bf16[208,768]{1,0:T(8,128)(2,1)} %copy-done.30) | copy-start | bytes 958468
  88.1 13.1 %collective-permute-start.6 = (bf16[52,768]{1,0:T(8,128)(2,1)S(1)}, bf16[52,768]{1,0:T(8,128)(2,1)S(1)}, u32[]{:S(2)}, u32[]{:S(2)}) collective-permute-start(bf16[52,768]{1,0:T(8,128)(2,1)S(1)} %get-tuple-element.51), channel_id=1, source_target_pairs={{0,8},{8,0},{16,24},{1,9},{9,1},{17,25},{2,10},{10,2},{18,26},{3,1... | collective-permute-start | bytes 239624 | tf_op jit(solution)/shard_map/ppermute | solution.py:498
  92.0 15.0 %collective-permute-start.7 = (bf16[52,768]{1,0:T(8,128)(2,1)S(1)}, bf16[52,768]{1,0:T(8,128)(2,1)S(1)}, u32[]{:S(2)}, u32[]{:S(2)}) collective-permute-start(bf16[52,768]{1,0:T(8,128)(2,1)S(1)} %get-tuple-element.52), channel_id=1, source_target_pairs={{0,16},{8,24},{16,0},{1,17},{9,25},{17,1},{2,18},{10,26},{18,2},{3... | collective-permute-start | bytes 239624 | tf_op jit(solution)/shard_map/ppermute | solution.py:498
  94.6 3.7 %copy-start.21 = (f32[208,768]{1,0:T(8,128)S(1)}, f32[208,768]{1,0:T(8,128)}, u32[]{:S(2)}) copy-start(f32[208,768]{1,0:T(8,128)} %copy-done.20) | copy-start | bytes 1916932
  94.7 3.7 %copy-start.23 = (f32[208,768]{1,0:T(8,128)S(1)}, f32[208,768]{1,0:T(8,128)}, u32[]{:S(2)}) copy-start(f32[208,768]{1,0:T(8,128)} %copy-done.22) | copy-start | bytes 1916932
  95.9 13.0 %collective-permute-start.8 = (bf16[52,768]{1,0:T(8,128)(2,1)S(1)}, bf16[52,768]{1,0:T(8,128)(2,1)S(1)}, u32[]{:S(2)}, u32[]{:S(2)}) collective-permute-start(bf16[52,768]{1,0:T(8,128)(2,1)S(1)} %get-tuple-element.53), channel_id=1, source_target_pairs={{0,24},{8,16},{16,8},{1,25},{9,17},{17,9},{2,26},{10,18},{18,10},{... | collective-permute-start | bytes 239624 | tf_op jit(solution)/shard_map/ppermute | solution.py:498
  98.3 16.7 %collective-permute-start.19 = (f32[56,384]{1,0:T(8,128)S(1)}, f32[56,384]{1,0:T(8,128)S(1)}, u32[]{:S(2)}, u32[]{:S(2)}) collective-permute-start(f32[56,384]{1,0:T(8,128)S(1)} %add_add_fusion.mine), channel_id=1, source_target_pairs={{0,1},{1,0},{2,3},{3,2},{4,5},{5,4},{6,7},{7,6},{8,9},{9,8},{10,11... | collective-permute-start | bytes 258056 | tf_op jit(solution)/shard_map/ppermute | solution.py:467
  98.4 16.6 %copy-start.14 = (f32[56,768]{1,0:T(8,128)S(1)}, f32[56,768]{1,0:T(8,128)}, u32[]{:S(2)}) copy-start(f32[56,768]{1,0:T(8,128)} %copy-done.13) | copy-start | bytes 516100
  98.4 16.6 %copy-start.17 = (f32[50,768]{1,0:T(8,128)S(1)}, f32[50,768]{1,0:T(8,128)}, u32[]{:S(2)}) copy-start(f32[50,768]{1,0:T(8,128)} %prompts.3) | copy-start | bytes 460804
  98.4 16.6 %copy-start.34 = (f32[50,768]{1,0:T(8,128)S(1)}, f32[50,768]{1,0:T(8,128)}, u32[]{:S(2)}) copy-start(f32[50,768]{1,0:T(8,128)} %momentum.1) | copy-start | bytes 460804
  98.4 16.6 %copy-start.35 = (f32[768,8]{0,1:T(8,128)S(1)}, f32[768,8]{0,1:T(8,128)}, u32[]{:S(2)}) copy-start(f32[768,8]{0,1:T(8,128)} %param.35) | copy-start | bytes 73732
  100.0 9.7 %collective-permute-start.9 = (bf16[52,768]{1,0:T(8,128)(2,1)S(1)}, bf16[52,768]{1,0:T(8,128)(2,1)S(1)}, u32[]{:S(2)}, u32[]{:S(2)}) collective-permute-start(bf16[52,768]{1,0:T(8,128)(2,1)S(1)} %get-tuple-element.62), channel_id=1, source_target_pairs={{0,8},{8,0},{16,24},{1,9},{9,1},{17,25},{2,10},{10,2},{18,26},{3,1... | collective-permute-start | bytes 239624 | tf_op jit(solution)/shard_map/ppermute | solution.py:498
  101.3 8.5 %collective-permute-start.10 = (bf16[52,768]{1,0:T(8,128)(2,1)S(1)}, bf16[52,768]{1,0:T(8,128)(2,1)S(1)}, u32[]{:S(2)}, u32[]{:S(2)}) collective-permute-start(bf16[52,768]{1,0:T(8,128)(2,1)S(1)} %get-tuple-element.63), channel_id=1, source_target_pairs={{0,16},{8,24},{16,0},{1,17},{9,25},{17,1},{2,18},{10,26},{18,2},{3... | collective-permute-start | bytes 239624 | tf_op jit(solution)/shard_map/ppermute | solution.py:498
  107.0 7.3 %collective-permute-start.11 = (bf16[52,768]{1,0:T(8,128)(2,1)S(1)}, bf16[52,768]{1,0:T(8,128)(2,1)S(1)}, u32[]{:S(2)}, u32[]{:S(2)}) collective-permute-start(bf16[52,768]{1,0:T(8,128)(2,1)S(1)} %get-tuple-element.64), channel_id=1, source_target_pairs={{0,24},{8,16},{16,8},{1,25},{9,17},{17,9},{2,26},{10,18},{18,10},{... | collective-permute-start | bytes 239624 | tf_op jit(solution)/shard_map/ppermute | solution.py:498
  (12 other events, 10.5 us)

commit v2 on v1

v2 whole, which is shorter than its diff:
```python
import functools
import math

import jax
import jax.numpy as jnp
from jax import lax
from jax.experimental import pallas as pl
from jax.experimental.pallas import tpu as pltpu
from jax.sharding import PartitionSpec as P

HEADS = 12
EPS = 1e-06
MOMENTUM_DECAY = 0.5
RATE_SCALE = 3.0
HIGHEST = lax.Precision.HIGHEST
F32 = jnp.float32
BF16 = jnp.bfloat16
VMEM = pl.BlockSpec(memory_space=pltpu.VMEM)
ANY = pl.BlockSpec(memory_space=pl.ANY)
HBM = pl.BlockSpec(memory_space=pltpu.HBM)
MIB = 1 << 20
LOG2E = 1.4426950408889634


def up(value, unit):
    return -(-value // unit) * unit


def dot(a, b):
    return jnp.dot(a, b, preferred_element_type=F32)


def dot_nt(a, b, precision=None):
    return lax.dot_general(
        a, b, (((1,), (1,)), ((), ())), precision=precision, preferred_element_type=F32
    )


def dot_tn(a, b, precision=None):
    return lax.dot_general(
        a, b, (((0,), (0,)), ((), ())), precision=precision, preferred_element_type=F32
    )


def normalize(values):
    center = values - jnp.mean(values, axis=-1, keepdims=True)
    rstd = lax.rsqrt(jnp.mean(center * center, axis=-1, keepdims=True) + EPS)
    return center * rstd, rstd


def norm_back(hat, rstd, gain, grad):
    inner = grad * gain
    mean = jnp.mean(inner, axis=-1, keepdims=True)
    along = jnp.mean(inner * hat, axis=-1, keepdims=True)
    return rstd * (inner - mean - hat * along)


def call(kernel, outs, ins, scratch=(), in_specs=None, out_specs=None, flops=0, vmem=8 * MIB, name=None):
    in_specs = in_specs or [VMEM] * len(ins)
    out_specs = out_specs or [VMEM] * len(outs)
    ins = [
        pltpu.with_memory_space_constraint(x, pltpu.HBM) if spec is HBM else x
        for x, spec in zip(ins, in_specs)
    ]
    held = {id(VMEM): pltpu.VMEM, id(HBM): pltpu.HBM}
    return pl.pallas_call(
        kernel,
        out_shape=[
            held.get(id(spec), jax.ShapeDtypeStruct)(s, d) for (s, d), spec in zip(outs, out_specs)
        ],
        in_specs=in_specs,
        out_specs=out_specs,
        scratch_shapes=list(scratch),
        compiler_params=pltpu.CompilerParams(vmem_limit_bytes=vmem),
        cost_estimate=pl.CostEstimate(
            flops=flops,
            bytes_accessed=sum(x.size * x.dtype.itemsize for x in ins),
            transcendentals=0,
        ),
        name=name,
    )(*ins)


class Copies:
    def __init__(self, sems):
        self.sems = sems
        self.used = 0

    def __call__(self, source, target):
        copy = pltpu.make_async_copy(source, target, self.sems.at[self.used])
        self.used += 1
        copy.start()
        return copy


def wait(*copies):
    for copy in copies:
        copy.wait()


def pick_kernel(seq, images, tok, cot, *refs):
    outs, sems = refs[:-1], refs[-1]
    me = lax.axis_index("seq")
    start = Copies(sems)
    copies = []
    for k in range(seq):
        index = jnp.minimum(me ^ k, images - 1)
        copies.append(start(tok.at[index], outs[k].at[0]))
        copies.append(start(cot.at[index], outs[k].at[1]))
    wait(*copies)


def prepare_kernel(count_in, *refs):
    sources, targets = refs[:count_in], refs[count_in : 2 * count_in]
    pkv, sems = refs[2 * count_in :]
    start = Copies(sems)
    copies = [
        start(a, b if len(a.shape) == len(b.shape) else b.at[0]) for a, b in zip(sources, targets)
    ]
    prompts, gain, shift, b_qkv, w_qkv = targets[:5]
    count, width = prompts.shape
    cols = pl.ds(width, 2 * width)
    pkv[...] = jnp.zeros_like(pkv)
    wait(*copies[:4])
    hat, _ = normalize(prompts[...].astype(BF16).astype(F32))
    normed = (hat * gain[...] + shift[...]).astype(BF16)
    wait(copies[4])
    pkv[:count, :] = (dot(normed, w_qkv[:, cols]) + b_qkv[:, cols]).astype(BF16)
    wait(*copies[5:])


def layer_kernel(seq, images, *refs):
    packs = refs[:seq]
    (
        mask, pkv, prompts, gain_one, shift_one, b_qkv, w_qkv, w_out, b_out, gain_two, shift_two,
        w_up, b_up, w_down, error,
        pgrad, base, act, resid, dres, p_bf, ds_bf, query, dmix, k_t, x_bf,
        x, gbuf, tbuf, keys, values, v_t, mix_t, p_f, dhid, normed,
    ) = refs[seq:]
    me = lax.axis_index("seq")
    chunk = packs[0].shape[1]
    rows, width = x.shape
    head = width // HEADS
    ff = act.shape[1]
    nkeys = keys.shape[0]
    count = prompts.shape[0]
    scale = head ** (-0.5)
    parts = [pl.ds(part * width, width) for part in range(3)]

    live = jnp.where(me < images, 1.0, 0.0)
    for k in range(seq):
        tbuf[k] = packs[k][...]
    for c in range(seq):
        span = pl.ds(c * chunk, chunk)
        x[span, :] = tbuf[me ^ c, 0].astype(F32) * live
        gbuf[span, :] = tbuf[me ^ c, 1].astype(F32) * live
    x_bf[...] = x[...].astype(BF16)
    hat, _ = normalize(x[...])
    normed[...] = (hat * gain_one[...] + shift_one[...]).astype(BF16)
    query[...] = (dot(normed[...], w_qkv[:, parts[0]]) + b_qkv[:, parts[0]]).astype(BF16)
    for index, dest in ((1, keys), (2, values)):
        part = parts[index]
        dest[:rows, :] = (dot(normed[...], w_qkv[:, part]) + b_qkv[:, part]).astype(BF16)
        dest[rows:, :] = pkv[: nkeys - rows, parts[index - 1]]
    k_t[...] = keys[...].T
    v_t[...] = values[...].T

    mrow = mask[pl.ds(jnp.minimum(me, images - 1), 1), :].astype(F32)
    mcol = dot_tn(
        jnp.broadcast_to(mrow, (8, rows)).astype(BF16), jnp.full((8, rows), 0.125, BF16)
    )
    rest = lax.broadcasted_iota(jnp.int32, (nkeys - rows, rows), 0)
    bias = jnp.concatenate(
        [jnp.where(mcol > 0.5, 0.0, -jnp.inf), jnp.where(rest < count, 0.0, -jnp.inf)], 0
    )

    lane = lax.broadcasted_iota(jnp.int32, (rows, 2 * head), 1) // head
    for pair in range(HEADS // 2):
        cols = pl.ds(pair * 2 * head, 2 * head)
        qp = query[:, cols]
        kp = keys[:, cols]
        for side in range(2):
            h = pair * 2 + side
            qm = jnp.where(lane == side, qp, jnp.zeros_like(qp))
            score = dot_nt(kp, qm) * (scale * LOG2E) + bias
            top = jnp.max(score, axis=0, keepdims=True)
            ex = jnp.exp2(score - top)
            total = jnp.sum(ex, axis=0, keepdims=True)
            prob = ex * (1.0 / total)
            p_f[h] = prob
            weight = prob.astype(BF16)
            p_bf[h] = weight
            part = pl.ds(h * head, head)
            mix_t[part, :] = dot(v_t[part, :], weight).astype(BF16)

    resid[...] = x[...] + dot_tn(mix_t[...], w_out[...]) + b_out[...]
    hat_two, _ = normalize(resid[...])
    normed[...] = (hat_two * gain_two[...] + shift_two[...]).astype(BF16)
    grad_out = gbuf[...].astype(BF16)
    step = 256

    def mlp(c, carry):
        cols = pl.ds(pl.multiple_of(c * step, step), step)
        hidden = dot(normed[...], w_up[:, cols]) + b_up[:, cols]
        grad = dot_nt(grad_out, w_down[cols, :])
        cdf = 0.5 * (1.0 + lax.erf(hidden * math.sqrt(0.5)))
        act[:, cols] = (hidden * cdf).astype(BF16)
        pdf = jnp.exp(-0.5 * hidden * hidden) * (1.0 / math.sqrt(2.0 * math.pi))
        dhid[:, cols] = (grad * (cdf + hidden * pdf)).astype(BF16)
        return carry

    lax.fori_loop(0, ff // step, mlp, 0)
    hat_two, rstd_two = normalize(resid[...])
    grad_resid = gbuf[...] + norm_back(
        hat_two, rstd_two, gain_two[...], dot_nt(dhid[...], w_up[...])
    )
    dres[...] = grad_resid
    dmix[...] = dot_nt(grad_resid.astype(BF16), w_out[...]).astype(BF16)

    gk = []
    gv = []
    for pair in range(HEADS // 2):
        cols = pl.ds(pair * 2 * head, 2 * head)
        qp = query[:, cols]
        gp = dmix[:, cols]
        vp = values[:, cols]
        gkp = jnp.zeros((nkeys - rows, 2 * head), F32)
        gvp = jnp.zeros((nkeys - rows, 2 * head), F32)
        for side in range(2):
            h = pair * 2 + side
            qm = jnp.where(lane == side, qp, jnp.zeros_like(qp))
            gm = jnp.where(lane == side, gp, jnp.zeros_like(gp))
            dprob = dot_nt(vp, gm)
            prob = p_f[h]
            both = prob * dprob
            inner = jnp.sum(both, axis=0, keepdims=True)
            draw = ((both - prob * inner) * scale).astype(BF16)
            ds_bf[h] = draw
            gkp = gkp + dot(draw[rows:, :], qm)
            gvp = gvp + dot(p_bf[h, rows:, :], gm)
        gk.append(gkp)
        gv.append(gvp)
    pad = pgrad.shape[0]
    grad_kv = jnp.concatenate(gk + gv, 1)[:pad, :]
    first = grad_kv.astype(BF16)
    left = grad_kv - first.astype(F32)
    second = left.astype(BF16)
    third = (left - second.astype(F32)).astype(BF16)
    w_kv = w_qkv[:, pl.ds(width, 2 * width)]
    three = dot_nt(jnp.concatenate([first, second, third], 0), w_kv)
    grad_normed = three[:pad] + three[pad : 2 * pad] + three[2 * pad :]
    hat_p, rstd_p = normalize(prompts[...].astype(BF16).astype(F32))
    part = norm_back(hat_p, rstd_p, gain_one[...], grad_normed[:count, :]).astype(pgrad.dtype)
    pgrad[...] = jnp.zeros_like(pgrad)
    pgrad[:count, :] = part
    base[...] = jnp.zeros_like(base)
    base[:count, :] = error[:, 0, :]


def rest_kernel(
    seq, act, resid, dres, p_bf, ds_bf, query, dmix, k_t, x_bf, w_down, w_qkv, b_down, gain,
    out, grad, dqkv, q_t, wide,
):
    rows, width = query.shape
    head = width // HEADS
    chunk = out.shape[1]
    lane = lax.broadcasted_iota(jnp.int32, (rows, 2 * head), 1) // head
    for pair in range(HEADS // 2):
        cols = pl.ds(pair * 2 * head, 2 * head)
        qp = query[:, cols]
        gp = dmix[:, cols]
        gk = jnp.zeros((rows, 2 * head), F32)
        gv = jnp.zeros((rows, 2 * head), F32)
        for side in range(2):
            h = pair * 2 + side
            part = pl.ds(h * head, head)
            q_t[part, :] = dot(k_t[part, :], ds_bf[h]).astype(BF16)
            gk = gk + dot(ds_bf[h, :rows, :], jnp.where(lane == side, qp, jnp.zeros_like(qp)))
            gv = gv + dot(p_bf[h, :rows, :], jnp.where(lane == side, gp, jnp.zeros_like(gp)))
        dqkv[:, pl.ds(width + pair * 2 * head, 2 * head)] = gk.astype(BF16)
        dqkv[:, pl.ds(2 * width + pair * 2 * head, 2 * head)] = gv.astype(BF16)
    dqkv[:, :width] = q_t[...].T
    wide[...] = resid[...] + dot(act[...], w_down[...]) + b_down[...]
    for c in range(seq):
        out[c] = wide[pl.ds(c * chunk, chunk), :].astype(BF16)
    hat, rstd = normalize(x_bf[...].astype(F32))
    wide[...] = dres[...] + norm_back(hat, rstd, gain[...], dot_nt(dqkv[...], w_qkv[...]))
    for c in range(seq):
        grad[c] = wide[pl.ds(c * chunk, chunk), :].astype(BF16)


def pack_kernel(seq, out, grad, after, *packs):
    me = lax.axis_index("seq")
    for k in range(seq):
        packs[k][0] = out[me ^ k]
        packs[k][1] = grad[me ^ k]


def place_kernel(seq, images, *refs):
    ins, (out, grad, sems) = refs[:seq], refs[seq:]
    me = lax.axis_index("seq")

    def copies(k):
        return (
            pltpu.make_async_copy(ins[k].at[0], out.at[me ^ k], sems.at[2 * k]),
            pltpu.make_async_copy(ins[k].at[1], grad.at[me ^ k], sems.at[2 * k + 1]),
        )

    for k in range(seq):
        @pl.when((me ^ k) < images)
        def _():
            for copy in copies(k):
                copy.start()

    for k in range(seq):
        @pl.when((me ^ k) < images)
        def _():
            for copy in copies(k):
                copy.wait()


def tree(values):
    while len(values) > 1:
        values = [
            values[i] + values[i + 1] if i + 1 < len(values) else values[i]
            for i in range(0, len(values), 2)
        ]
    return values[0]


def combine_kernel(*refs):
    base, parts, (combined, keep, give) = refs[0], refs[1:-4], refs[-3:]
    half = keep.shape[1]
    core = lax.rem(lax.axis_index("dp"), 2)
    combined[...] = tree([part[...].astype(F32) for part in parts]) + base[...]
    low, high = combined[:, :half], combined[:, half:]
    keep[...] = jnp.where(core == 0, low, high)
    give[...] = jnp.where(core == 0, high, low)


def add_kernel(*refs):
    parts, out = refs[:-1], refs[-1]
    out[...] = tree([part[...].astype(F32) for part in parts]).astype(out.dtype)


def final_kernel(
    total, mine, other, combined, start_t, prompts, momentum,
    basis_t, right_t, error, new_momentum, new_prompts, prompt_copy, whole,
):
    half = mine.shape[1]
    count, width = prompts.shape
    rank = start_t.shape[0]
    core = lax.rem(lax.axis_index("dp"), 2)
    whole[:, :half] = jnp.where(core == 0, mine[...], other[...])
    whole[:, half:] = jnp.where(core == 0, other[...], mine[...])
    summed = whole[...]
    left = dot_nt(start_t[...], summed, HIGHEST)
    row = lax.broadcasted_iota(jnp.int32, left.shape, 0)
    for j in range(rank):
        pivot = left[j : j + 1, :]
        pivot = pivot * lax.rsqrt(jnp.sum(pivot * pivot, axis=1, keepdims=True) + 1e-12)
        along = jnp.sum(left * pivot, axis=1, keepdims=True)
        left = jnp.where(row > j, left - along * pivot, jnp.where(row == j, pivot, left))
    right = jnp.dot(left, summed, precision=HIGHEST, preferred_element_type=F32)
    mine_w = combined[...]
    right_w = jnp.dot(left, mine_w, precision=HIGHEST, preferred_element_type=F32)
    error[:, 0, :] = (mine_w - dot_tn(left, right_w, HIGHEST))[:count, :]
    update = dot_tn(left, right, HIGHEST)[:count, :] / total
    moved = MOMENTUM_DECAY * momentum[...] + update
    fresh = prompts[...] - RATE_SCALE * math.sqrt(total) * moved
    basis_t[...] = left[:, :count]
    right_t[...] = right
    new_momentum[...] = moved
    new_prompts[...] = fresh
    prompt_copy[...] = fresh.astype(BF16)


def flip(k, n):
    return [(i, i ^ k) for i in range(n)]


def body(
    tokens,
    key_mask,
    prompts,
    gain_one,
    shift_one,
    w_qkv,
    b_qkv,
    w_out,
    b_out,
    gain_two,
    shift_two,
    w_up,
    b_up,
    w_down,
    b_down,
    cotangent,
    start_factor,
    error_buffer,
    momentum,
):
    images, chunk, width = tokens.shape
    seq = lax.axis_size("seq")
    dp = lax.axis_size("dp")
    rows = seq * chunk
    ff = w_up.shape[1]
    count = prompts.shape[0]
    if images > seq or seq & (seq - 1) or dp & (dp - 1):
        raise ValueError("unsupported mesh")
    nkeys = up(rows + count, 16)
    pad = up(count, 8)
    dma = pltpu.SemaphoreType.DMA

    piece = ((2, chunk, width), BF16)
    packs = call(
        functools.partial(pick_kernel, seq, images),
        [piece] * seq,
        (tokens, cotangent),
        [dma((2 * seq,))],
        in_specs=[HBM] * 2,
        name="pick",
    )
    packs = [packs[0]] + [
        lax.ppermute(packs[k], "seq", flip(k, seq)) for k in range(1, seq)
    ]

    loads = (
        prompts, gain_one, shift_one, b_qkv, w_qkv, w_out, b_out, gain_two, shift_two, w_up, b_up,
        w_down, error_buffer.transpose(1, 0, 2), b_down,
    )
    *held, pkv = call(
        functools.partial(prepare_kernel, len(loads)),
        [((1, v.size) if v.ndim == 1 else v.shape, v.dtype) for v in loads]
        + [((up(count, 16), 2 * width), BF16)],
        loads,
        [dma((len(loads),))],
        in_specs=[HBM] * len(loads),
        flops=2 * count * width * 2 * width,
        name="prepare",
    )
    held, b_down_row = held[:-1], held[-1]
    gain_row, w_qkv_held, w_down_held = held[1], held[4], held[11]

    wire = BF16
    saved = [
        ((rows, ff), BF16),
        ((rows, width), F32),
        ((rows, width), F32),
        ((HEADS, nkeys, rows), BF16),
        ((HEADS, nkeys, rows), BF16),
        ((rows, width), BF16),
        ((rows, width), BF16),
        ((width, nkeys), BF16),
        ((rows, width), BF16),
    ]
    pgrad, base, *kept = call(
        functools.partial(layer_kernel, seq, images),
        [((pad, width), wire), ((pad, width), F32)] + saved,
        (*packs, key_mask, pkv, *held),
        [
            pltpu.VMEM((rows, width), F32),
            pltpu.VMEM((rows, width), F32),
            pltpu.VMEM((seq, 2, chunk, width), BF16),
            pltpu.VMEM((nkeys, width), BF16),
            pltpu.VMEM((nkeys, width), BF16),
            pltpu.VMEM((width, nkeys), BF16),
            pltpu.VMEM((width, rows), BF16),
            pltpu.VMEM((HEADS, nkeys, rows), F32),
            pltpu.VMEM((rows, ff), BF16),
            pltpu.VMEM((rows, width), BF16),
        ],
        flops=2 * rows * width * (4 * width + 3 * ff),
        vmem=20 * MIB,
        name="layer",
    )

    out_chunks, grad_chunks = call(
        functools.partial(rest_kernel, seq),
        [((seq, chunk, width), BF16)] * 2,
        (*kept, w_down_held, w_qkv_held, b_down_row, gain_row),
        [
            pltpu.VMEM((rows, 3 * width), BF16),
            pltpu.VMEM((width, rows), BF16),
            pltpu.VMEM((rows, width), F32),
        ],
        flops=2 * rows * width * (3 * width + ff),
        vmem=8 * MIB,
        name="rest",
    )

    parts = [pgrad] + [lax.ppermute(pgrad, "seq", flip(k, seq)) for k in range(1, seq)]
    half = width // 2
    combined, keep, give = call(
        combine_kernel,
        [((pad, width), F32), ((pad, half), F32), ((pad, half), F32)],
        (base, *parts, out_chunks),
        in_specs=[VMEM] * (1 + seq) + [ANY],
        name="combine",
    )
    parts = [keep, lax.ppermute(give, "dp", flip(1, dp))]
    bit = 2
    first = None
    while bit < dp:
        (mine,) = call(add_kernel, [((pad, half), F32)], parts, name="add")
        first = mine if first is None else first
        steps = [bit, 2 * bit, 3 * bit] if 2 * bit < dp else [bit]
        parts = [mine] + [lax.ppermute(mine, "dp", flip(k, dp)) for k in steps]
        bit *= 4 if 2 * bit < dp else 2
    (mine,) = call(add_kernel, [((pad, half), F32)], parts, name="add")
    other = lax.ppermute(mine, "dp", flip(1, dp))

    packs = call(
        functools.partial(pack_kernel, seq),
        [piece] * seq,
        (out_chunks, grad_chunks, first),
        in_specs=[VMEM] * 2 + [ANY],
        name="pack",
    )
    back = [packs[0]] + [
        lax.ppermute(packs[k], "seq", flip(k, seq)) for k in range(1, seq)
    ]
    layer_out, input_grad = call(
        functools.partial(place_kernel, seq, images),
        [((images, chunk, width), BF16)] * 2,
        back,
        [dma((2 * seq,))],
        in_specs=[ANY] * seq,
        out_specs=[ANY] * 2,
        name="place",
    )

    rank = start_factor.shape[1]
    basis_t, right_t, error, new_momentum, new_prompts, prompt_copy = call(
        functools.partial(final_kernel, images * dp),
        [
            ((rank, count), F32),
            ((rank, width), F32),
            ((count, 1, width), F32),
            ((count, width), F32),
            ((count, width), F32),
            ((count, width), BF16),
        ],
        (mine, other, combined, start_factor.T, prompts, momentum),
        [pltpu.VMEM((pad, width), F32)],
        out_specs=[pl.BlockSpec(memory_space=pltpu.VMEM) for _ in range(6)],
        name="final",
    )
    return (
        layer_out,
        input_grad,
        basis_t.T,
        right_t.T,
        error.transpose(1, 0, 2),
        new_momentum,
        new_prompts,
        prompt_copy,
    )


def solution(mesh):
    rep = P()
    rows = P("dp", "seq", None)
    placed = (rows, P("dp", None), *([rep] * 13), rows, rep, P("dp", None, None), rep)
    return jax.shard_map(
        body,
        mesh=mesh,
        in_specs=placed,
        out_specs=(rows, rows, rep, rep, P("dp", None, None), rep, rep, rep),
        check_vma=False,
    )
```

time: 119 us -> 57.5 us (0.48)
  the two profiles are of different devices: /device:TPU:28 before, /device:TPU:0 now
where the time goes in v2:
time: 57.5 us; the launch traced here: 57.4 us
  Pallas kernels  29.7 us (52%)
  starting transfers between devices  16.8 us (29%)
  waiting for transfers between devices  10 us (17%)
  between operations  0.78 us (1%)
    pallas_call x10, Pallas kernels, call(): pl.pallas_call(kernel, out_shape=[held.get(id(spec), jax.ShapeDtypeStruct...  29.7 us
    ppermute x6, starting transfers between devices, body(): lax.ppermute(packs[k], 'seq', flip(k, seq))  8.66 us
    ppermute x6, waiting for transfers between devices, body(): lax.ppermute(packs[k], 'seq', flip(k, seq))  6.06 us
    ppermute x3, starting transfers between devices, body(): parts = [mine] + [lax.ppermute(mine, 'dp', flip(k, dp)) for k in steps]  4.45 us
    ppermute x3, starting transfers between devices, body(): lax.ppermute(pgrad, 'seq', flip(k, seq))  3.55 us
    ppermute x3, waiting for transfers between devices, body(): parts = [mine] + [lax.ppermute(mine, 'dp', flip(k, dp)) for k in steps]  2.58 us
    ppermute x1, waiting for transfers between devices, body(): parts = [keep, lax.ppermute(give, 'dp', flip(1, dp))]  1.27 us
  transfers between devices with their start and end apart: 14, of which 7 were waited for; matrix products, arithmetic and copies ran while one was open for 0% of the time, Pallas kernels for 17%

profile of v2, /device:TPU:0, one launch (start us, length us, event | category | flops | bytes accessed | tf_op | source)
XLA Modules:
  0.0 57.4 jit_solution(13020484827141496747)
XLA Ops:
  0.6 1.3 %pick.1 = (bf16[2,52,768]{2,1,0:T(8,128)(2,1)S(1)}, bf16[2,52,768]{2,1,0:T(8,128)(2,1)S(1)}, bf16[2,52,768]{2,1,0:T(8,128)(2,1)S(1)}, bf16[2,52,768]{2,1,0:T(8,128)(2,1)S(1)}) custom-call(bf16[3,52,768]{2,1,0:T(8,128)(2,1)} %tok.1, bf16[3,52,768]{2,1,0:T(8,128)(2,1)} %cot.1), custom_call_target="tpu_custom_call" | custom-call | bytes 479232 | tf_op jit(solution)/shard_map/pick/pallas_call | solution.py:66
  1.9 3.0 %collective-permute-start = (bf16[2,52,768]{2,1,0:T(8,128)(2,1)S(1)}, bf16[2,52,768]{2,1,0:T(8,128)(2,1)S(1)}, u32[]{:S(2)}, u32[]{:S(2)}) collective-permute-start(bf16[2,52,768]{2,1,0:T(8,128)(2,1)S(1)} %get-tuple-element.56), channel_id=1, source_target_pairs={{0,8},{8,0},{16,24},{24,16},{1,9},{9,1},{17,25},{25,17},{2,10},{10... | collective-permute-start | bytes 479240 | tf_op jit(solution)/shard_map/ppermute | solution.py:425
  4.9 1.5 %collective-permute-start.1 = (bf16[2,52,768]{2,1,0:T(8,128)(2,1)S(1)}, bf16[2,52,768]{2,1,0:T(8,128)(2,1)S(1)}, u32[]{:S(2)}, u32[]{:S(2)}) collective-permute-start(bf16[2,52,768]{2,1,0:T(8,128)(2,1)S(1)} %get-tuple-element.57), channel_id=1, source_target_pairs={{0,16},{8,24},{16,0},{24,8},{1,17},{9,25},{17,1},{25,9},{2,18},{10... | collective-permute-start | bytes 479240 | tf_op jit(solution)/shard_map/ppermute | solution.py:425
  6.4 0.0 collective-permute-start.2
  6.5 0.0 copy-start.3
  6.5 5.4 %prepare.1 = (f32[50,768]{1,0:T(8,128)S(1)}, f32[1,768]{1,0:T(1,128)S(1)}, f32[1,768]{1,0:T(1,128)S(1)}, f32[1,2304]{1,0:T(1,128)S(1)}, bf16[768,2304]{1,0:T(8,1...) custom-call(f32[50,768]{1,0:T(8,128)} %prompts.1, ...), custom_call_target="tpu_custom_call" | custom-call | flops 117964800 | bytes 14502912 | tf_op jit(solution)/shard_map/prepare/pallas_call | solution.py:66
  11.9 0.0 collective-permute-done.refs_1_
  11.9 2.5 %collective-permute-done.1.refs_2_ = bf16[2,52,768]{2,1,0:T(8,128)(2,1)S(1)} collective-permute-done((bf16[2,52,768]{2,1,0:T(8,128)(2,1)S(1)}, bf16[2,52,768]{2,1,0:T(8,128)(2,1)S(1)}, u32[]{:S(2)}, u32[]{:S(2)}) %collective-permute-start.1) | collective-permute-done | bytes 159776 | tf_op jit(solution)/shard_map/ppermute | solution.py:425
  14.4 0.0 collective-permute-done.2.refs_3_
  14.4 0.0 copy-done.3
  14.4 15.4 %layer.1 = (bf16[56,768]{1,0:T(8,128)(2,1)S(1)}, f32[56,768]{1,0:T(8,128)S(1)}, bf16[208,3072]{1,0:T(8,128)(2,1)S(1)}, f32[208,768]{1,0:T(8,128)S(1)}, f32[208,7...) custom-call(bf16[2,52,768]{2,1,0:T(8,128)(2,1)S(1)} %get-tuple-eleme, ...), custom_call_target="tpu_custom_call" | custom-call | flops 3925868544 | bytes 15337920 | tf_op jit(solution)/shard_map/layer/pallas_call | solution.py:66
  29.8 1.6 %collective-permute-start.5 = (bf16[56,768]{1,0:T(8,128)(2,1)S(1)}, bf16[56,768]{1,0:T(8,128)(2,1)S(1)}, u32[]{:S(2)}, u32[]{:S(2)}) collective-permute-start(bf16[56,768]{1,0:T(8,128)(2,1)S(1)} %get-tuple-element.86.refs_1_), channel_id=1, source_target_pairs={{0,24},{8,16},{16,8},{24,0},{1,25},{9,17},{17,9},{25,1},{2,26},{10... | collective-permute-start | bytes 258056 | tf_op jit(solution)/shard_map/ppermute | solution.py:492
  31.4 1.2 %collective-permute-start.4 = (bf16[56,768]{1,0:T(8,128)(2,1)S(1)}, bf16[56,768]{1,0:T(8,128)(2,1)S(1)}, u32[]{:S(2)}, u32[]{:S(2)}) collective-permute-start(bf16[56,768]{1,0:T(8,128)(2,1)S(1)} %get-tuple-element.86.refs_1_), channel_id=1, source_target_pairs={{0,16},{8,24},{16,0},{24,8},{1,17},{9,25},{17,1},{25,9},{2,18},{10... | collective-permute-start | bytes 258056 | tf_op jit(solution)/shard_map/ppermute | solution.py:492
  32.6 0.8 %collective-permute-start.3 = (bf16[56,768]{1,0:T(8,128)(2,1)S(1)}, bf16[56,768]{1,0:T(8,128)(2,1)S(1)}, u32[]{:S(2)}, u32[]{:S(2)}) collective-permute-start(bf16[56,768]{1,0:T(8,128)(2,1)S(1)} %get-tuple-element.86.refs_1_), channel_id=1, source_target_pairs={{0,8},{8,0},{16,24},{24,16},{1,9},{9,1},{17,25},{25,17},{2,10},{10... | collective-permute-start | bytes 258056 | tf_op jit(solution)/shard_map/ppermute | solution.py:492
  33.4 0.0 copy-start
  33.4 0.0 copy-start.1
  33.4 0.0 copy-start.2
  33.4 3.5 %rest.1 = (bf16[4,52,768]{2,1,0:T(8,128)(2,1)S(1)}, bf16[4,52,768]{2,1,0:T(8,128)(2,1)S(1)}) custom-call(bf16[208,3072]{1,0:T(8,128)(2,1)S(1)} %get-tuple-element.73.act, f32[208,768]{1,0:T(8,128)S(1)} %get-tuple-element.74.resid, f32[208,768]{1,0:T(8,128)S(1)} %get-tuple-element.75.dres, bf16[12,272,208]{2,1,0:T(8,128)(2,1)S(1)} %get-tuple-element.76.p_bf, ...), custom_call_target="tpu_custom_call" | custom-call | flops 1717567488 | bytes 14911488 | tf_op jit(solution)/shard_map/rest/pallas_call | solution.py:66
  36.9 0.0 collective-permute-done.5.refs_4_
  36.9 0.0 collective-permute-done.4.refs_3_
  37.0 0.1 collective-permute-done.3.refs_2_
  37.1 0.1 combine.1
  37.2 0.1 collective-permute-start.6
  37.2 1.3 %collective-permute-done.6.refs_1_ = f32[56,384]{1,0:T(8,128)S(1)} collective-permute-done((f32[56,384]{1,0:T(8,128)S(1)}, f32[56,384]{1,0:T(8,128)S(1)}, u32[]{:S(2)}, u32[]{:S(2)}) %collective-permute-start.6) | collective-permute-done | bytes 86048 | tf_op jit(solution)/shard_map/ppermute | solution.py:501
  38.5 3.7 %collective-permute-start.12 = (f32[56,384]{1,0:T(8,128)S(1)}, f32[56,384]{1,0:T(8,128)S(1)}, u32[]{:S(2)}, u32[]{:S(2)}) collective-permute-start(f32[56,384]{1,0:T(8,128)S(1)} %add.2.after.refs_0_), channel_id=1, source_target_pairs={{0,6},{1,7},{2,4},{3,5},{4,2},{5,3},{6,0},{7,1},{8,14},{9,15},{10,... | collective-permute-start | bytes 258056 | tf_op jit(solution)/shard_map/ppermute | solution.py:508
  42.2 0.0 collective-permute-start.11
  42.2 0.8 %collective-permute-start.10 = (f32[56,384]{1,0:T(8,128)S(1)}, f32[56,384]{1,0:T(8,128)S(1)}, u32[]{:S(2)}, u32[]{:S(2)}) collective-permute-start(f32[56,384]{1,0:T(8,128)S(1)} %add.2.after.refs_0_), channel_id=1, source_target_pairs={{0,2},{1,3},{2,0},{3,1},{4,6},{5,7},{6,4},{7,5},{8,10},{9,11},{10,... | collective-permute-start | bytes 258056 | tf_op jit(solution)/shard_map/ppermute | solution.py:508
  43.0 1.2 %collective-permute-start.7 = (bf16[2,52,768]{2,1,0:T(8,128)(2,1)S(1)}, bf16[2,52,768]{2,1,0:T(8,128)(2,1)S(1)}, u32[]{:S(2)}, u32[]{:S(2)}) collective-permute-start(bf16[2,52,768]{2,1,0:T(8,128)(2,1)S(1)} %get-tuple-element.90), channel_id=1, source_target_pairs={{0,8},{8,0},{16,24},{24,16},{1,9},{9,1},{17,25},{25,17},{2,10},{10... | collective-permute-start | bytes 479240 | tf_op jit(solution)/shard_map/ppermute | solution.py:521
  44.2 1.2 %collective-permute-start.8 = (bf16[2,52,768]{2,1,0:T(8,128)(2,1)S(1)}, bf16[2,52,768]{2,1,0:T(8,128)(2,1)S(1)}, u32[]{:S(2)}, u32[]{:S(2)}) collective-permute-start(bf16[2,52,768]{2,1,0:T(8,128)(2,1)S(1)} %get-tuple-element.91), channel_id=1, source_target_pairs={{0,16},{8,24},{16,0},{24,8},{1,17},{9,25},{17,1},{25,9},{2,18},{10... | collective-permute-start | bytes 479240 | tf_op jit(solution)/shard_map/ppermute | solution.py:521
  45.4 0.4 collective-permute-done.12.refs_3_
  45.8 1.7 %collective-permute-start.9 = (bf16[2,52,768]{2,1,0:T(8,128)(2,1)S(1)}, bf16[2,52,768]{2,1,0:T(8,128)(2,1)S(1)}, u32[]{:S(2)}, u32[]{:S(2)}) collective-permute-start(bf16[2,52,768]{2,1,0:T(8,128)(2,1)S(1)} %get-tuple-element.92), channel_id=1, source_target_pairs={{0,24},{8,16},{16,8},{24,0},{1,25},{9,17},{17,9},{25,1},{2,26},{10... | collective-permute-start | bytes 479240 | tf_op jit(solution)/shard_map/ppermute | solution.py:521
  47.5 2.2 %collective-permute-done.11.refs_2_ = f32[56,384]{1,0:T(8,128)S(1)} collective-permute-done((f32[56,384]{1,0:T(8,128)S(1)}, f32[56,384]{1,0:T(8,128)S(1)}, u32[]{:S(2)}, u32[]{:S(2)}) %collective-permute-start.11) | collective-permute-done | bytes 86048 | tf_op jit(solution)/shard_map/ppermute | solution.py:508
  49.7 0.0 collective-permute-done.10.refs_1_
  49.7 0.1 collective-permute-start.13
  49.8 0.0 collective-permute-done.7.refs_1_
  49.8 2.2 %collective-permute-done.8.refs_2_ = bf16[2,52,768]{2,1,0:T(8,128)(2,1)S(1)} collective-permute-done((bf16[2,52,768]{2,1,0:T(8,128)(2,1)S(1)}, bf16[2,52,768]{2,1,0:T(8,128)(2,1)S(1)}, u32[]{:S(2)}, u32[]{:S(2)}) %collective-permute-start.8) | collective-permute-done | bytes 159776 | tf_op jit(solution)/shard_map/ppermute | solution.py:521
  52.1 1.3 %collective-permute-done.9.refs_3_ = bf16[2,52,768]{2,1,0:T(8,128)(2,1)S(1)} collective-permute-done((bf16[2,52,768]{2,1,0:T(8,128)(2,1)S(1)}, bf16[2,52,768]{2,1,0:T(8,128)(2,1)S(1)}, u32[]{:S(2)}, u32[]{:S(2)}) %collective-permute-start.9) | collective-permute-done | bytes 159776 | tf_op jit(solution)/shard_map/ppermute | solution.py:521
  53.4 0.8 %place.1 = (bf16[3,52,768]{2,1,0:T(8,128)(2,1)}, bf16[3,52,768]{2,1,0:T(8,128)(2,1)}) custom-call(bf16[2,52,768]{2,1,0:T(8,128)(2,1)S(1)} %get-tuple-element.89.refs_0_, bf16[2,52,768]{2,1,0:T(8,128)(2,1)S(1)} %collective-permute-done.7.refs_1_, bf16[2,52,768]{2,1,0:T(8,128)(2,1)S(1)} %collective-permute-done.8.refs_2_, ...), custom_call_target="tpu_custom_call" | custom-call | bytes 638976 | tf_op jit(solution)/shard_map/place/pallas_call | solution.py:66
  54.2 0.0 collective-permute-done.13.other
  54.2 0.0 copy-done
  54.2 0.0 copy-done.1
  54.2 0.0 copy-done.2
  54.3 3.1 %final.1 = (f32[8,50]{1,0:T(8,128)}, f32[8,768]{1,0:T(8,128)}, f32[50,1,768]{2,1,0:T(1,128)}, f32[50,768]{1,0:T(8,128)}, f32[50,768]{1,0:T(8,128)}, /*index=5*/bf16[50,768]{1,0:T(8,128)(2,1)}) custom-call(f32[56,384]{1,0:T(8,128)S(1)} %add.3.mine, f32[56,384]{1,0:T(8,128)S(1)} %collective-permute-done.13.other, f32[56,768]{1,0:T(8,128)S(1)} %get-tuple-element.95.combined, ...), custom_call_target="tpu_custom_call" | custom-call | bytes 675840 | tf_op jit(solution)/shard_map/final/pallas_call | solution.py:66
  (3 shorter events, 0.1 us)
Async XLA Ops:
  1.9 10.0 %collective-permute-start = (bf16[2,52,768]{2,1,0:T(8,128)(2,1)S(1)}, bf16[2,52,768]{2,1,0:T(8,128)(2,1)S(1)}, u32[]{:S(2)}, u32[]{:S(2)}) collective-permute-start(bf16[2,52,768]{2,1,0:T(8,128)(2,1)S(1)} %get-tuple-element.56), channel_id=1, source_target_pairs={{0,8},{8,0},{16,24},{24,16},{1,9},{9,1},{17,25},{25,17},{2,10},{10... | collective-permute-start | bytes 479240 | tf_op jit(solution)/shard_map/ppermute | solution.py:425
  4.9 9.5 %collective-permute-start.1 = (bf16[2,52,768]{2,1,0:T(8,128)(2,1)S(1)}, bf16[2,52,768]{2,1,0:T(8,128)(2,1)S(1)}, u32[]{:S(2)}, u32[]{:S(2)}) collective-permute-start(bf16[2,52,768]{2,1,0:T(8,128)(2,1)S(1)} %get-tuple-element.57), channel_id=1, source_target_pairs={{0,16},{8,24},{16,0},{24,8},{1,17},{9,25},{17,1},{25,9},{2,18},{10... | collective-permute-start | bytes 479240 | tf_op jit(solution)/shard_map/ppermute | solution.py:425
  6.4 8.0 %collective-permute-start.2 = (bf16[2,52,768]{2,1,0:T(8,128)(2,1)S(1)}, bf16[2,52,768]{2,1,0:T(8,128)(2,1)S(1)}, u32[]{:S(2)}, u32[]{:S(2)}) collective-permute-start(bf16[2,52,768]{2,1,0:T(8,128)(2,1)S(1)} %get-tuple-element.58), channel_id=1, source_target_pairs={{0,24},{8,16},{16,8},{24,0},{1,25},{9,17},{17,9},{25,1},{2,26},{10... | collective-permute-start | bytes 479240 | tf_op jit(solution)/shard_map/ppermute | solution.py:425
  6.5 8.0 %copy-start.3 = (s32[3,208]{1,0:T(4,128)S(1)}, s32[3,208]{1,0:T(4,128)}, u32[]{:S(2)}) copy-start(s32[3,208]{1,0:T(4,128)} %refs_4_.3) | copy-start | bytes 7492
  29.8 7.1 %collective-permute-start.5 = (bf16[56,768]{1,0:T(8,128)(2,1)S(1)}, bf16[56,768]{1,0:T(8,128)(2,1)S(1)}, u32[]{:S(2)}, u32[]{:S(2)}) collective-permute-start(bf16[56,768]{1,0:T(8,128)(2,1)S(1)} %get-tuple-element.86.refs_1_), channel_id=1, source_target_pairs={{0,24},{8,16},{16,8},{24,0},{1,25},{9,17},{17,9},{25,1},{2,26},{10... | collective-permute-start | bytes 258056 | tf_op jit(solution)/shard_map/ppermute | solution.py:492
  31.4 5.6 %collective-permute-start.4 = (bf16[56,768]{1,0:T(8,128)(2,1)S(1)}, bf16[56,768]{1,0:T(8,128)(2,1)S(1)}, u32[]{:S(2)}, u32[]{:S(2)}) collective-permute-start(bf16[56,768]{1,0:T(8,128)(2,1)S(1)} %get-tuple-element.86.refs_1_), channel_id=1, source_target_pairs={{0,16},{8,24},{16,0},{24,8},{1,17},{9,25},{17,1},{25,9},{2,18},{10... | collective-permute-start | bytes 258056 | tf_op jit(solution)/shard_map/ppermute | solution.py:492
  32.6 4.5 %collective-permute-start.3 = (bf16[56,768]{1,0:T(8,128)(2,1)S(1)}, bf16[56,768]{1,0:T(8,128)(2,1)S(1)}, u32[]{:S(2)}, u32[]{:S(2)}) collective-permute-start(bf16[56,768]{1,0:T(8,128)(2,1)S(1)} %get-tuple-element.86.refs_1_), channel_id=1, source_target_pairs={{0,8},{8,0},{16,24},{24,16},{1,9},{9,1},{17,25},{25,17},{2,10},{10... | collective-permute-start | bytes 258056 | tf_op jit(solution)/shard_map/ppermute | solution.py:492
  33.4 20.9 %copy-start = (f32[50,768]{1,0:T(8,128)S(1)}, f32[50,768]{1,0:T(8,128)}, u32[]{:S(2)}) copy-start(f32[50,768]{1,0:T(8,128)} %prompts.1) | copy-start | bytes 460804
  33.4 20.9 %copy-start.1 = (f32[50,768]{1,0:T(8,128)S(1)}, f32[50,768]{1,0:T(8,128)}, u32[]{:S(2)}) copy-start(f32[50,768]{1,0:T(8,128)} %momentum.1) | copy-start | bytes 460804
  33.4 20.9 %copy-start.2 = (f32[768,8]{0,1:T(8,128)S(1)}, f32[768,8]{0,1:T(8,128)}, u32[]{:S(2)}) copy-start(f32[768,8]{0,1:T(8,128)} %param.35) | copy-start | bytes 73732
  37.2 1.3 %collective-permute-start.6 = (f32[56,384]{1,0:T(8,128)S(1)}, f32[56,384]{1,0:T(8,128)S(1)}, u32[]{:S(2)}, u32[]{:S(2)}) collective-permute-start(f32[56,384]{1,0:T(8,128)S(1)} %get-tuple-element.88), channel_id=1, source_target_pairs={{0,1},{1,0},{2,3},{3,2},{4,5},{5,4},{6,7},{7,6},{8,9},{9,8},{10,11... | collective-permute-start | bytes 258056 | tf_op jit(solution)/shard_map/ppermute | solution.py:501
  38.5 7.2 %collective-permute-start.12 = (f32[56,384]{1,0:T(8,128)S(1)}, f32[56,384]{1,0:T(8,128)S(1)}, u32[]{:S(2)}, u32[]{:S(2)}) collective-permute-start(f32[56,384]{1,0:T(8,128)S(1)} %add.2.after.refs_0_), channel_id=1, source_target_pairs={{0,6},{1,7},{2,4},{3,5},{4,2},{5,3},{6,0},{7,1},{8,14},{9,15},{10,... | collective-permute-start | bytes 258056 | tf_op jit(solution)/shard_map/ppermute | solution.py:508
  42.2 7.5 %collective-permute-start.11 = (f32[56,384]{1,0:T(8,128)S(1)}, f32[56,384]{1,0:T(8,128)S(1)}, u32[]{:S(2)}, u32[]{:S(2)}) collective-permute-start(f32[56,384]{1,0:T(8,128)S(1)} %add.2.after.refs_0_), channel_id=1, source_target_pairs={{0,4},{1,5},{2,6},{3,7},{4,0},{5,1},{6,2},{7,3},{8,12},{9,13},{10,... | collective-permute-start | bytes 258056 | tf_op jit(solution)/shard_map/ppermute | solution.py:508
  42.2 7.5 %collective-permute-start.10 = (f32[56,384]{1,0:T(8,128)S(1)}, f32[56,384]{1,0:T(8,128)S(1)}, u32[]{:S(2)}, u32[]{:S(2)}) collective-permute-start(f32[56,384]{1,0:T(8,128)S(1)} %add.2.after.refs_0_), channel_id=1, source_target_pairs={{0,2},{1,3},{2,0},{3,1},{4,6},{5,7},{6,4},{7,5},{8,10},{9,11},{10,... | collective-permute-start | bytes 258056 | tf_op jit(solution)/shard_map/ppermute | solution.py:508
  43.0 6.8 %collective-permute-start.7 = (bf16[2,52,768]{2,1,0:T(8,128)(2,1)S(1)}, bf16[2,52,768]{2,1,0:T(8,128)(2,1)S(1)}, u32[]{:S(2)}, u32[]{:S(2)}) collective-permute-start(bf16[2,52,768]{2,1,0:T(8,128)(2,1)S(1)} %get-tuple-element.90), channel_id=1, source_target_pairs={{0,8},{8,0},{16,24},{24,16},{1,9},{9,1},{17,25},{25,17},{2,10},{10... | collective-permute-start | bytes 479240 | tf_op jit(solution)/shard_map/ppermute | solution.py:521
  44.2 7.9 %collective-permute-start.8 = (bf16[2,52,768]{2,1,0:T(8,128)(2,1)S(1)}, bf16[2,52,768]{2,1,0:T(8,128)(2,1)S(1)}, u32[]{:S(2)}, u32[]{:S(2)}) collective-permute-start(bf16[2,52,768]{2,1,0:T(8,128)(2,1)S(1)} %get-tuple-element.91), channel_id=1, source_target_pairs={{0,16},{8,24},{16,0},{24,8},{1,17},{9,25},{17,1},{25,9},{2,18},{10... | collective-permute-start | bytes 479240 | tf_op jit(solution)/shard_map/ppermute | solution.py:521
  45.8 7.6 %collective-permute-start.9 = (bf16[2,52,768]{2,1,0:T(8,128)(2,1)S(1)}, bf16[2,52,768]{2,1,0:T(8,128)(2,1)S(1)}, u32[]{:S(2)}, u32[]{:S(2)}) collective-permute-start(bf16[2,52,768]{2,1,0:T(8,128)(2,1)S(1)} %get-tuple-element.92), channel_id=1, source_target_pairs={{0,24},{8,16},{16,8},{24,0},{1,25},{9,17},{17,9},{25,1},{2,26},{10... | collective-permute-start | bytes 479240 | tf_op jit(solution)/shard_map/ppermute | solution.py:521
  49.7 4.5 %collective-permute-start.13 = (f32[56,384]{1,0:T(8,128)S(1)}, f32[56,384]{1,0:T(8,128)S(1)}, u32[]{:S(2)}, u32[]{:S(2)}) collective-permute-start(f32[56,384]{1,0:T(8,128)S(1)} %add.3.mine), channel_id=1, source_target_pairs={{0,1},{1,0},{2,3},{3,2},{4,5},{5,4},{6,7},{7,6},{8,9},{9,8},{10,11... | collective-permute-start | bytes 258056 | tf_op jit(solution)/shard_map/ppermute | solution.py:511

commit v3 on v2

v3 whole, which is shorter than its diff:
```python
import functools
import math

import jax
import jax.numpy as jnp
from jax import lax
from jax.experimental import pallas as pl
from jax.experimental.pallas import tpu as pltpu
from jax.sharding import PartitionSpec as P

HEADS = 12
EPS = 1e-06
MOMENTUM_DECAY = 0.5
RATE_SCALE = 3.0
HIGH = lax.Precision.HIGH
F32 = jnp.float32
BF16 = jnp.bfloat16
VMEM = pl.BlockSpec(memory_space=pltpu.VMEM)
ANY = pl.BlockSpec(memory_space=pl.ANY)
HBM = pl.BlockSpec(memory_space=pltpu.HBM)
MIB = 1 << 20
LOG2E = 1.4426950408889634


def up(value, unit):
    return -(-value // unit) * unit


def dot(a, b):
    return jnp.dot(a, b, preferred_element_type=F32)


def dot_nt(a, b, precision=None):
    return lax.dot_general(
        a, b, (((1,), (1,)), ((), ())), precision=precision, preferred_element_type=F32
    )


def dot_tn(a, b, precision=None):
    return lax.dot_general(
        a, b, (((0,), (0,)), ((), ())), precision=precision, preferred_element_type=F32
    )


def normalize(values):
    center = values - jnp.mean(values, axis=-1, keepdims=True)
    rstd = lax.rsqrt(jnp.mean(center * center, axis=-1, keepdims=True) + EPS)
    return center * rstd, rstd


def norm_back(hat, rstd, gain, grad):
    inner = grad * gain
    mean = jnp.mean(inner, axis=-1, keepdims=True)
    along = jnp.mean(inner * hat, axis=-1, keepdims=True)
    return rstd * (inner - mean - hat * along)


def call(kernel, outs, ins, scratch=(), in_specs=None, out_specs=None, flops=0, vmem=8 * MIB, name=None):
    in_specs = in_specs or [VMEM] * len(ins)
    out_specs = out_specs or [VMEM] * len(outs)
    ins = [
        pltpu.with_memory_space_constraint(x, pltpu.HBM) if spec is HBM else x
        for x, spec in zip(ins, in_specs)
    ]
    held = {id(VMEM): pltpu.VMEM, id(HBM): pltpu.HBM}
    return pl.pallas_call(
        kernel,
        out_shape=[
            held.get(id(spec), jax.ShapeDtypeStruct)(s, d) for (s, d), spec in zip(outs, out_specs)
        ],
        in_specs=in_specs,
        out_specs=out_specs,
        scratch_shapes=list(scratch),
        compiler_params=pltpu.CompilerParams(vmem_limit_bytes=vmem),
        cost_estimate=pl.CostEstimate(
            flops=flops,
            bytes_accessed=sum(x.size * x.dtype.itemsize for x in ins),
            transcendentals=0,
        ),
        name=name,
    )(*ins)


class Copies:
    def __init__(self, sems):
        self.sems = sems
        self.used = 0

    def __call__(self, source, target):
        copy = pltpu.make_async_copy(source, target, self.sems.at[self.used])
        self.used += 1
        copy.start()
        return copy


def wait(*copies):
    for copy in copies:
        copy.wait()


def pick_kernel(seq, images, small, source, *refs):
    sources, refs = refs[:small], refs[small:]
    chunks, targets, sems = refs[:seq], refs[seq:-1], refs[-1]
    me = lax.axis_index("seq")
    start = Copies(sems)
    copies = [
        start(source.at[jnp.minimum(me ^ k, images - 1)], chunks[k]) for k in range(seq)
    ]
    for a, b in zip(sources, targets):
        copies.append(start(a, b if len(a.shape) > 1 else b.at[0]))
    wait(*copies)


def forward_kernel(seq, images, *refs):
    toks, refs = refs[:seq], refs[seq:]
    (
        mask, prompts, gain_one, shift_one, b_qkv, b_out, gain_two, shift_two, w_qkv, w_out,
        x_bf, query, keys, values, p_f, p_bf, resid, normed_two,
        x, tbuf, normed, bias, mix_t,
    ) = refs
    me = lax.axis_index("seq")
    rows, width = x.shape
    chunk = rows // seq
    head = width // HEADS
    nkeys = keys.shape[0]
    count = prompts.shape[0]
    scale = head ** (-0.5)
    parts = [pl.ds(part * width, width) for part in range(3)]
    for k in range(seq):
        tbuf[k] = toks[k][...]
    live = jnp.where(me < images, 1.0, 0.0)
    for c in range(seq):
        x[pl.ds(c * chunk, chunk), :] = tbuf[me ^ c].astype(F32) * live
    x_bf[...] = x[...].astype(BF16)
    mrow = mask[pl.ds(jnp.minimum(me, images - 1), 1), :].astype(F32)
    mcol = dot_tn(
        jnp.broadcast_to(mrow, (8, rows)).astype(BF16), jnp.full((8, rows), 0.125, BF16)
    )
    rest = lax.broadcasted_iota(jnp.int32, (nkeys - rows, rows), 0)
    bias[:rows, :] = jnp.where(mcol > 0.5, 0.0, -jnp.inf)
    bias[rows:, :] = jnp.where(rest < count, 0.0, -jnp.inf)
    hat, _ = normalize(x[...])
    normed[:rows, :] = (hat * gain_one[...] + shift_one[...]).astype(BF16)
    hat, _ = normalize(prompts[...].astype(BF16).astype(F32))
    normed[rows:, :] = jnp.zeros((nkeys - rows, width), BF16)
    normed[rows : rows + count, :] = (hat * gain_one[...] + shift_one[...]).astype(BF16)
    query[...] = (dot(normed[:rows, :], w_qkv[:, parts[0]]) + b_qkv[:, parts[0]]).astype(BF16)
    for index, dest in ((1, keys), (2, values)):
        part = parts[index]
        dest[...] = (dot(normed[...], w_qkv[:, part]) + b_qkv[:, part]).astype(BF16)
    lane = lax.broadcasted_iota(jnp.int32, (rows, 2 * head), 1) // head
    for h in range(HEADS):
        cols = pl.ds(h // 2 * 2 * head, 2 * head)
        qp = query[:, cols]
        qm = jnp.where(lane == h % 2, qp, jnp.zeros_like(qp))
        score = dot_nt(keys[:, cols], qm) * (scale * LOG2E) + bias[...]
        ex = jnp.exp2(score - jnp.max(score, axis=0, keepdims=True))
        prob = ex * (1.0 / jnp.sum(ex, axis=0, keepdims=True))
        p_f[h] = prob
        p_bf[h] = prob.astype(BF16)
    for h in range(HEADS):
        both = dot_tn(values[:, pl.ds(h // 2 * 2 * head, 2 * head)], p_bf[h])
        mix_t[pl.ds(h * head, head), :] = both[h % 2 * head :][:head].astype(BF16)
    resid[...] = x[...] + dot_tn(mix_t[...], w_out[...]) + b_out[...]
    hat, _ = normalize(resid[...])
    normed_two[...] = (hat * gain_two[...] + shift_two[...]).astype(BF16)


def backward_kernel(seq, images, *refs):
    cots, refs = refs[:seq], refs[seq:]
    (
        query, values, p_f, p_bf, resid, normed_two, w_qkv, w_out, gain_two, w_up, b_up, w_down,
        prompts, gain_one,
        pgrad, act, dres, ds_bf, dmix,
        gbuf, tbuf, dhid, gkv,
    ) = refs
    me = lax.axis_index("seq")
    rows, width = resid.shape
    chunk = rows // seq
    head = width // HEADS
    ff = act.shape[1]
    nkeys = values.shape[0]
    count = prompts.shape[0]
    scale = head ** (-0.5)
    for k in range(seq):
        tbuf[k] = cots[k][...]
    live = jnp.where(me < images, 1.0, 0.0)
    for c in range(seq):
        gbuf[pl.ds(c * chunk, chunk), :] = tbuf[me ^ c].astype(F32) * live
    grad_out = gbuf[...].astype(BF16)
    step = 256
    for c in range(ff // step):
        cols = pl.ds(c * step, step)
        hidden = dot(normed_two[...], w_up[:, cols]) + b_up[:, cols]
        grad = dot_nt(grad_out, w_down[cols, :])
        cdf = 0.5 * (1.0 + lax.erf(hidden * math.sqrt(0.5)))
        act[:, cols] = (hidden * cdf).astype(BF16)
        pdf = jnp.exp(-0.5 * hidden * hidden) * (1.0 / math.sqrt(2.0 * math.pi))
        dhid[:, cols] = (grad * (cdf + hidden * pdf)).astype(BF16)
    hat_two, rstd_two = normalize(resid[...])
    grad_resid = gbuf[...] + norm_back(
        hat_two, rstd_two, gain_two[...], dot_nt(dhid[...], w_up[...])
    )
    dres[...] = grad_resid
    dmix[...] = dot_nt(dres[...].astype(BF16), w_out[...]).astype(BF16)
    lane = lax.broadcasted_iota(jnp.int32, (rows, 2 * head), 1) // head
    for h in range(HEADS):
        cols = pl.ds(h // 2 * 2 * head, 2 * head)
        gp = dmix[:, cols]
        dprob = dot_nt(values[:, cols], jnp.where(lane == h % 2, gp, jnp.zeros_like(gp)))
        prob = p_f[h]
        both = prob * dprob
        inner = jnp.sum(both, axis=0, keepdims=True)
        ds_bf[h] = ((both - prob * inner) * scale).astype(BF16)
    low = lax.broadcasted_iota(jnp.int32, (nkeys - rows, 2 * head), 1) < head
    for pair in range(HEADS // 2):
        cols = pl.ds(pair * 2 * head, 2 * head)
        for at, source, other in ((0, ds_bf, query), (width, p_bf, dmix)):
            two = jnp.concatenate([source[2 * pair, rows:, :], source[2 * pair + 1, rows:, :]], 0)
            both = dot(two, other[:, cols])
            gkv[:, pl.ds(at + pair * 2 * head, 2 * head)] = jnp.where(
                low, both[: nkeys - rows], both[nkeys - rows :]
            )
    pad = pgrad.shape[0]
    grad_kv = gkv[:pad, :]
    first = grad_kv.astype(BF16)
    left = grad_kv - first.astype(F32)
    second = left.astype(BF16)
    third = (left - second.astype(F32)).astype(BF16)
    w_kv = w_qkv[:, pl.ds(width, 2 * width)]
    three = dot_nt(jnp.concatenate([first, second, third], 0), w_kv)
    grad_normed = three[:pad] + three[pad : 2 * pad] + three[2 * pad :]
    hat_p, rstd_p = normalize(prompts[...].astype(BF16).astype(F32))
    part = norm_back(hat_p, rstd_p, gain_one[...], grad_normed[:count, :]).astype(pgrad.dtype)
    pgrad[...] = jnp.zeros_like(pgrad)
    pgrad[:count, :] = part


def rest_kernel(
    seq, act, resid, dres, p_bf, ds_bf, query, dmix, keys, x_bf, w_down, w_qkv, b_down, gain,
    out, grad, dqkv, q_t, wide, k_t,
):
    rows, width = query.shape
    head = width // HEADS
    chunk = out.shape[1]
    k_t[...] = keys[...].T
    low = lax.broadcasted_iota(jnp.int32, (rows, 2 * head), 1) < head
    for pair in range(HEADS // 2):
        cols = pl.ds(pair * 2 * head, 2 * head)
        for at, source, other in ((width, ds_bf, query), (2 * width, p_bf, dmix)):
            two = jnp.concatenate([source[2 * pair, :rows, :], source[2 * pair + 1, :rows, :]], 0)
            both = dot(two, other[:, cols])
            dqkv[:, pl.ds(at + pair * 2 * head, 2 * head)] = jnp.where(
                low, both[:rows], both[rows:]
            ).astype(BF16)
    for h in range(HEADS):
        part = pl.ds(h * head, head)
        q_t[part, :] = dot(k_t[part, :], ds_bf[h]).astype(BF16)
    dqkv[:, :width] = q_t[...].T
    wide[...] = resid[...] + dot(act[...], w_down[...]) + b_down[...]
    for c in range(seq):
        out[c] = wide[pl.ds(c * chunk, chunk), :].astype(BF16)
    hat, rstd = normalize(x_bf[...].astype(F32))
    wide[...] = dres[...] + norm_back(hat, rstd, gain[...], dot_nt(dqkv[...], w_qkv[...]))
    for c in range(seq):
        grad[c] = wide[pl.ds(c * chunk, chunk), :].astype(BF16)


def pack_kernel(seq, out, grad, after, *packs):
    me = lax.axis_index("seq")
    for k in range(seq):
        packs[k][0] = out[me ^ k]
        packs[k][1] = grad[me ^ k]


def tree(values):
    while len(values) > 1:
        values = [
            values[i] + values[i + 1] if i + 1 < len(values) else values[i]
            for i in range(0, len(values), 2)
        ]
    return values[0]


def combine_kernel(*refs):
    error, parts, (combined, keep, give) = refs[0], refs[1:-4], refs[-3:]
    half = keep.shape[1]
    count = error.shape[0]
    core = lax.rem(lax.axis_index("dp"), 2)
    combined[...] = tree([part[...].astype(F32) for part in parts])
    combined[:count, :] += error[:, 0, :]
    low, high = combined[:, :half], combined[:, half:]
    keep[...] = jnp.where(core == 0, low, high)
    give[...] = jnp.where(core == 0, high, low)


def add_kernel(*refs):
    parts, out = refs[:-1], refs[-1]
    out[...] = tree([part[...].astype(F32) for part in parts]).astype(out.dtype)


def final_kernel(seq, images, total, *refs):
    back, refs = refs[:seq], refs[seq:]
    (
        mine, other, combined, start_t, prompts, momentum,
        layer_out, input_grad, basis_t, right_t, error, new_momentum, new_prompts, prompt_copy,
        whole,
    ) = refs
    me = lax.axis_index("seq")
    for k in range(seq):
        @pl.when((me ^ k) < images)
        def _():
            layer_out[me ^ k] = back[k][0]
            input_grad[me ^ k] = back[k][1]
    half = mine.shape[1]
    count, width = prompts.shape
    rank = start_t.shape[0]
    core = lax.rem(lax.axis_index("dp"), 2)
    whole[:, :half] = jnp.where(core == 0, mine[...], other[...]).astype(F32)
    whole[:, half:width] = jnp.where(core == 0, other[...], mine[...]).astype(F32)
    whole[:, width:] = combined[...]
    left = dot_nt(start_t[...], whole[:, :width], HIGH)
    row = lax.broadcasted_iota(jnp.int32, left.shape, 0)
    for j in range(rank):
        pivot = left[j : j + 1, :]
        along = jnp.sum(left * pivot, axis=1, keepdims=True)
        inverse = lax.rsqrt(along[j : j + 1, :] + 1e-12)
        pivot = pivot * inverse
        left = jnp.where(
            row > j, left - (along * inverse) * pivot, jnp.where(row == j, pivot, left)
        )
    right = jnp.dot(left, whole[...], precision=HIGH, preferred_element_type=F32)
    outer = dot_tn(left, right, HIGH)[:count, :]
    error[:, 0, :] = combined[:count, :] - outer[:, width:]
    moved = MOMENTUM_DECAY * momentum[...] + outer[:, :width] / total
    fresh = prompts[...] - RATE_SCALE * math.sqrt(total) * moved
    basis_t[...] = left[:, :count]
    right_t[...] = right[:, :width]
    new_momentum[...] = moved
    new_prompts[...] = fresh
    prompt_copy[...] = fresh.astype(BF16)


def flip(k, n):
    return [(i, i ^ k) for i in range(n)]


def body(
    tokens,
    key_mask,
    prompts,
    gain_one,
    shift_one,
    w_qkv,
    b_qkv,
    w_out,
    b_out,
    gain_two,
    shift_two,
    w_up,
    b_up,
    w_down,
    b_down,
    cotangent,
    start_factor,
    error_buffer,
    momentum,
):
    images, chunk, width = tokens.shape
    seq = lax.axis_size("seq")
    dp = lax.axis_size("dp")
    rows = seq * chunk
    ff = w_up.shape[1]
    count = prompts.shape[0]
    if images > seq or seq & (seq - 1) or dp & (dp - 1):
        raise ValueError("unsupported mesh")
    nkeys = up(rows + count, 16)
    pad = up(count, 8)
    dma = pltpu.SemaphoreType.DMA

    piece = ((2, chunk, width), BF16)
    one = ((chunk, width), BF16)
    row = lambda v: ((1, v.size), v.dtype) if v.ndim == 1 else (v.shape, v.dtype)
    small = (
        key_mask, prompts, gain_one, shift_one, b_qkv, b_out, gain_two, shift_two, b_up, b_down,
        error_buffer.transpose(1, 0, 2),
    )

    def pick(source, small, flops):
        return call(
            functools.partial(pick_kernel, seq, images, len(small)),
            [one] * seq + [row(v) for v in small],
            (source, *small),
            [dma((seq + len(small),))],
            in_specs=[HBM] * (1 + len(small)),
            flops=flops,
            name="pick",
        )

    toks = pick(tokens, (), 0)
    picked = pick(cotangent, small, 1 << 34)
    cots, small = picked[:seq], picked[seq:]
    mask, prompts_held, gain_one, shift_one, b_qkv, b_out, gain_two, shift_two = small[:8]
    b_up, b_down, error_rows = small[8:]
    toks = [toks[0]] + [lax.ppermute(toks[k], "seq", flip(k, seq)) for k in range(1, seq)]
    cots = [cots[0]] + [lax.ppermute(cots[k], "seq", flip(k, seq)) for k in range(1, seq)]

    wide = ((rows, width), BF16)
    long = ((nkeys, width), BF16)
    probs = (HEADS, nkeys, rows)
    x_bf, query, keys, values, p_f, p_bf, resid, normed_two = call(
        functools.partial(forward_kernel, seq, images),
        [wide, wide, long, long, (probs, F32), (probs, BF16), ((rows, width), F32), wide],
        (
            *toks, mask, prompts_held, gain_one, shift_one, b_qkv, b_out, gain_two, shift_two,
            w_qkv, w_out,
        ),
        [
            pltpu.VMEM((rows, width), F32),
            pltpu.VMEM((seq, chunk, width), BF16),
            pltpu.VMEM((nkeys, width), BF16),
            pltpu.VMEM((nkeys, rows), F32),
            pltpu.VMEM((width, rows), BF16),
        ],
        flops=2 * rows * width * (4 * width + 2 * nkeys),
        vmem=8 * MIB,
        name="forward",
    )

    wire = BF16
    pgrad, act, dres, ds_bf, dmix = call(
        functools.partial(backward_kernel, seq, images),
        [
            ((pad, width), wire), ((rows, ff), BF16), ((rows, width), F32), (probs, BF16), wide,
        ],
        (
            *cots, query, values, p_f, p_bf, resid, normed_two, w_qkv, w_out, gain_two,
            w_up, b_up, w_down, prompts_held, gain_one,
        ),
        [
            pltpu.VMEM((rows, width), F32),
            pltpu.VMEM((seq, chunk, width), BF16),
            pltpu.VMEM((rows, ff), BF16),
            pltpu.VMEM((nkeys - rows, 2 * width), F32),
        ],
        flops=2 * rows * width * (3 * width + 3 * ff),
        vmem=8 * MIB,
        name="backward",
    )
    kept = (act, resid, dres, p_bf, ds_bf, query, dmix, keys, x_bf)

    out_chunks, grad_chunks = call(
        functools.partial(rest_kernel, seq),
        [((seq, chunk, width), BF16)] * 2,
        (*kept, w_down, w_qkv, b_down, gain_one),
        [
            pltpu.VMEM((rows, 3 * width), BF16),
            pltpu.VMEM((width, rows), BF16),
            pltpu.VMEM((rows, width), F32),
            pltpu.VMEM((width, nkeys), BF16),
        ],
        flops=2 * rows * width * (3 * width + ff),
        vmem=8 * MIB,
        name="rest",
    )

    parts = [pgrad] + [lax.ppermute(pgrad, "seq", flip(k, seq)) for k in range(1, seq)]
    half = width // 2
    combined, keep, give = call(
        combine_kernel,
        [((pad, width), F32), ((pad, half), F32), ((pad, half), F32)],
        (error_rows, *parts, out_chunks),
        in_specs=[VMEM] * (1 + seq) + [ANY],
        name="combine",
    )
    parts = [keep, lax.ppermute(give, "dp", flip(1, dp))]
    bit = 2
    first = None
    while bit < dp:
        (mine,) = call(add_kernel, [((pad, half), wire)], parts, name="add")
        first = mine if first is None else first
        parts = [mine, lax.ppermute(mine, "dp", flip(bit, dp))]
        bit *= 2
    (mine,) = call(add_kernel, [((pad, half), F32)], parts, name="add")
    other = lax.ppermute(mine, "dp", flip(1, dp))

    packs = call(
        functools.partial(pack_kernel, seq),
        [piece] * seq,
        (out_chunks, grad_chunks, first),
        in_specs=[VMEM] * 2 + [ANY],
        flops=1 << 32,
        name="pack",
    )
    back = [packs[0]] + [
        lax.ppermute(packs[k], "seq", flip(k, seq)) for k in range(1, seq)
    ]
    rank = start_factor.shape[1]
    layer_out, input_grad, basis_t, right_t, error, new_momentum, new_prompts, prompt_copy = call(
        functools.partial(final_kernel, seq, images, images * dp),
        [
            ((images, chunk, width), BF16),
            ((images, chunk, width), BF16),
            ((rank, count), F32),
            ((rank, width), F32),
            ((count, 1, width), F32),
            ((count, width), F32),
            ((count, width), F32),
            ((count, width), BF16),
        ],
        (*back, mine, other, combined, start_factor.T, prompts, momentum),
        [pltpu.VMEM((pad, 2 * width), F32)],
        out_specs=[pl.BlockSpec(memory_space=pltpu.VMEM) for _ in range(8)],
        name="final",
    )
    return (
        layer_out,
        input_grad,
        basis_t.T,
        right_t.T,
        error.transpose(1, 0, 2),
        new_momentum,
        new_prompts,
        prompt_copy,
    )


def solution(mesh):
    rep = P()
    rows = P("dp", "seq", None)
    placed = (rows, P("dp", None), *([rep] * 13), rows, rep, P("dp", None, None), rep)
    return jax.shard_map(
        body,
        mesh=mesh,
        in_specs=placed,
        out_specs=(rows, rows, rep, rep, P("dp", None, None), rep, rep, rep),
        check_vma=False,
    )
```

time: 57.5 us -> 47.5 us (0.83)
  Pallas kernels: 29.7 us -> 19.9 us
  waiting for transfers between devices: 10 us -> 6.93 us
  starting transfers between devices: 16.8 us -> 19.6 us
    pallas_call x10 -> x11, Pallas kernels: 29.7 us -> 19.9 us  [call(): pl.pallas_call(kernel, out_shape=[held.get(id(spec), jax.ShapeDtypeStruct...]
    ppermute x3 -> x8, starting transfers between devices: 4.45 us -> 12.4 us  [the longest x3 4.54 us: body(): lax.ppermute(toks[k], 'seq', flip(k, seq))]
    ppermute x6 -> x3, starting transfers between devices: 8.66 us -> 3.55 us  [body(): lax.ppermute(packs[k], 'seq', flip(k, seq))]
    ppermute x6 -> x3, waiting for transfers between devices: 6.06 us -> 1.46 us  [body(): lax.ppermute(packs[k], 'seq', flip(k, seq))]
    ppermute x3 -> x8, waiting for transfers between devices: 2.58 us -> 4.19 us  [the longest x2 2.69 us: body(): parts = [mine, lax.ppermute(mine, 'dp', flip(bit, dp))]]
  transfers between devices with their start and end apart: 14 -> 16, of which waited for: 7 -> 5; matrix products, arithmetic and copies ran while one was open for 0% -> 0% of each run, Pallas kernels for 17% -> 19%
where the time goes in v3:
time: 47.5 us; the launch traced here: 47.4 us
  Pallas kernels  19.9 us (42%)
  starting transfers between devices  19.6 us (41%)
  waiting for transfers between devices  6.93 us (15%)
  between operations  0.83 us (2%)
    pallas_call x11, Pallas kernels, call(): pl.pallas_call(kernel, out_shape=[held.get(id(spec), jax.ShapeDtypeStruct...  19.9 us
    ppermute x3, starting transfers between devices, body(): lax.ppermute(toks[k], 'seq', flip(k, seq))  4.54 us
    ppermute x2, starting transfers between devices, body(): parts = [mine, lax.ppermute(mine, 'dp', flip(bit, dp))]  4.29 us
    ppermute x3, starting transfers between devices, body(): lax.ppermute(cots[k], 'seq', flip(k, seq))  3.55 us
    ppermute x3, starting transfers between devices, body(): lax.ppermute(pgrad, 'seq', flip(k, seq))  3.55 us
    ppermute x3, starting transfers between devices, body(): lax.ppermute(packs[k], 'seq', flip(k, seq))  3.55 us
    ppermute x2, waiting for transfers between devices, body(): parts = [mine, lax.ppermute(mine, 'dp', flip(bit, dp))]  2.69 us
    ppermute x3, waiting for transfers between devices, body(): lax.ppermute(packs[k], 'seq', flip(k, seq))  1.46 us
  transfers between devices with their start and end apart: 16, of which 5 were waited for; matrix products, arithmetic and copies ran while one was open for 0% of the time, Pallas kernels for 19%

profile of v3, /device:TPU:0, one launch (start us, length us, event | category | flops | bytes accessed | tf_op | source)
XLA Modules:
  0.0 47.4 jit_solution(14547637087305028393)
XLA Ops:
  0.6 1.1 %pick.3 = (bf16[52,768]{1,0:T(8,128)(2,1)S(1)}, bf16[52,768]{1,0:T(8,128)(2,1)S(1)}, bf16[52,768]{1,0:T(8,128)(2,1)S(1)}, bf16[52,768]{1,0:T(8,128)(2,1)S(1)}) custom-call(bf16[3,52,768]{2,1,0:T(8,128)(2,1)} %source.3), custom_call_target="tpu_custom_call" | custom-call | bytes 239616 | tf_op jit(solution)/shard_map/pick/pallas_call | solution.py:66
  1.7 3.0 %collective-permute-start.3 = (bf16[52,768]{1,0:T(8,128)(2,1)S(1)}, bf16[52,768]{1,0:T(8,128)(2,1)S(1)}, u32[]{:S(2)}, u32[]{:S(2)}) collective-permute-start(bf16[52,768]{1,0:T(8,128)(2,1)S(1)} %get-tuple-element.62), channel_id=1, source_target_pairs={{0,8},{8,0},{16,24},{24,16},{1,9},{9,1},{17,25},{25,17},{2,10},{10... | collective-permute-start | bytes 239624 | tf_op jit(solution)/shard_map/ppermute | solution.py:405
  4.7 1.5 %collective-permute-start.4 = (bf16[52,768]{1,0:T(8,128)(2,1)S(1)}, bf16[52,768]{1,0:T(8,128)(2,1)S(1)}, u32[]{:S(2)}, u32[]{:S(2)}) collective-permute-start(bf16[52,768]{1,0:T(8,128)(2,1)S(1)} %get-tuple-element.63), channel_id=1, source_target_pairs={{0,16},{8,24},{16,0},{24,8},{1,17},{9,25},{17,1},{25,9},{2,18},{10... | collective-permute-start | bytes 239624 | tf_op jit(solution)/shard_map/ppermute | solution.py:405
  6.2 0.0 collective-permute-start.5
  6.3 0.0 slice-start.1
  6.3 0.0 slice-start.3
  6.3 1.5 %pick.2 = (bf16[52,768]{1,0:T(8,128)(2,1)S(1)}, bf16[52,768]{1,0:T(8,128)(2,1)S(1)}, bf16[52,768]{1,0:T(8,128)(2,1)S(1)}, bf16[52,768]{1,0:T(8,128)(2,1)S(1)}, s...) custom-call(bf16[3,52,768]{2,1,0:T(8,128)(2,1)} %source.2, ...), custom_call_target="tpu_custom_call" | custom-call | flops 17179869184 | bytes 589248 | tf_op jit(solution)/shard_map/pick/pallas_call | solution.py:66
  7.8 2.0 %collective-permute-start = (bf16[52,768]{1,0:T(8,128)(2,1)S(1)}, bf16[52,768]{1,0:T(8,128)(2,1)S(1)}, u32[]{:S(2)}, u32[]{:S(2)}) collective-permute-start(bf16[52,768]{1,0:T(8,128)(2,1)S(1)} %get-tuple-element.58), channel_id=1, source_target_pairs={{0,8},{8,0},{16,24},{24,16},{1,9},{9,1},{17,25},{25,17},{2,10},{10... | collective-permute-start | bytes 239624 | tf_op jit(solution)/shard_map/ppermute | solution.py:406
  9.8 1.5 %collective-permute-start.1 = (bf16[52,768]{1,0:T(8,128)(2,1)S(1)}, bf16[52,768]{1,0:T(8,128)(2,1)S(1)}, u32[]{:S(2)}, u32[]{:S(2)}) collective-permute-start(bf16[52,768]{1,0:T(8,128)(2,1)S(1)} %get-tuple-element.59), channel_id=1, source_target_pairs={{0,16},{8,24},{16,0},{24,8},{1,17},{9,25},{17,1},{25,9},{2,18},{10... | collective-permute-start | bytes 239624 | tf_op jit(solution)/shard_map/ppermute | solution.py:406
  11.3 0.0 collective-permute-done.3.refs_1_
  11.3 0.0 collective-permute-start.2
  11.4 0.0 collective-permute-done.4.refs_2_
  11.4 1.0 %collective-permute-done.5.refs_3_ = bf16[52,768]{1,0:T(8,128)(2,1)S(1)} collective-permute-done((bf16[52,768]{1,0:T(8,128)(2,1)S(1)}, bf16[52,768]{1,0:T(8,128)(2,1)S(1)}, u32[]{:S(2)}, u32[]{:S(2)}) %collective-permute-start.5) | collective-permute-done | bytes 79904 | tf_op jit(solution)/shard_map/ppermute | solution.py:405
  12.4 0.0 copy-done
  12.4 0.0 copy-done.1
  12.4 3.8 %forward.1 = (bf16[208,768]{1,0:T(8,128)(2,1)S(1)}, bf16[208,768]{1,0:T(8,128)(2,1)S(1)}, bf16[272,768]{1,0:T(8,128)(2,1)S(1)}, bf16[272,768]{1,0:T(8,128)(2,1)S...) custom-call(bf16[52,768]{1,0:T(8,128)(2,1)S(1)} %get-tuple-element.6, ...), custom_call_target="tpu_custom_call" | custom-call | flops 1155268608 | bytes 5218752 | tf_op jit(solution)/shard_map/forward/pallas_call | solution.py:66
  16.2 0.0 collective-permute-done.refs_1_
  16.2 0.0 collective-permute-done.1.refs_2_
  16.2 0.5 %collective-permute-done.2.refs_3_ = bf16[52,768]{1,0:T(8,128)(2,1)S(1)} collective-permute-done((bf16[52,768]{1,0:T(8,128)(2,1)S(1)}, bf16[52,768]{1,0:T(8,128)(2,1)S(1)}, u32[]{:S(2)}, u32[]{:S(2)}) %collective-permute-start.2) | collective-permute-done | bytes 79904 | tf_op jit(solution)/shard_map/ppermute | solution.py:406
  16.7 0.0 slice-done
  16.7 0.0 slice-done.2
  16.7 0.0 slice-done.1
  16.7 0.0 slice-done.3
  16.8 7.5 %backward.1 = (bf16[56,768]{1,0:T(8,128)(2,1)S(1)}, bf16[208,3072]{1,0:T(8,128)(2,1)S(1)}, f32[208,768]{1,0:T(8,128)S(1)}, bf16[12,272,208]{2,1,0:T(8,128)(2,1)S(1)}, bf16[208,768]{1,0:T(8,128)(2,1)S(1)}) custom-call(bf16[52,768]{1,0:T(8,128)(2,1)S(1)} %get-tuple-element.57.refs_0_, bf16[52,768]{1,0:T(8,128)(2,1)S(1)} %collective-permute-done.refs_1_, ...), custom_call_target="tpu_custom_call" | custom-call | flops 3680501760 | bytes 20416512 | tf_op jit(solution)/shard_map/backward/pallas_call | solution.py:66
  24.2 1.5 %collective-permute-start.8 = (bf16[56,768]{1,0:T(8,128)(2,1)S(1)}, bf16[56,768]{1,0:T(8,128)(2,1)S(1)}, u32[]{:S(2)}, u32[]{:S(2)}) collective-permute-start(bf16[56,768]{1,0:T(8,128)(2,1)S(1)} %get-tuple-element.90.refs_1_), channel_id=1, source_target_pairs={{0,24},{8,16},{16,8},{24,0},{1,25},{9,17},{17,9},{25,1},{2,26},{10... | collective-permute-start | bytes 258056 | tf_op jit(solution)/shard_map/ppermute | solution.py:467
  25.8 0.5 %collective-permute-start.7 = (bf16[56,768]{1,0:T(8,128)(2,1)S(1)}, bf16[56,768]{1,0:T(8,128)(2,1)S(1)}, u32[]{:S(2)}, u32[]{:S(2)}) collective-permute-start(bf16[56,768]{1,0:T(8,128)(2,1)S(1)} %get-tuple-element.90.refs_1_), channel_id=1, source_target_pairs={{0,16},{8,24},{16,0},{24,8},{1,17},{9,25},{17,1},{25,9},{2,18},{10... | collective-permute-start | bytes 258056 | tf_op jit(solution)/shard_map/ppermute | solution.py:467
  26.3 1.5 %collective-permute-start.6 = (bf16[56,768]{1,0:T(8,128)(2,1)S(1)}, bf16[56,768]{1,0:T(8,128)(2,1)S(1)}, u32[]{:S(2)}, u32[]{:S(2)}) collective-permute-start(bf16[56,768]{1,0:T(8,128)(2,1)S(1)} %get-tuple-element.90.refs_1_), channel_id=1, source_target_pairs={{0,8},{8,0},{16,24},{24,16},{1,9},{9,1},{17,25},{25,17},{2,10},{10... | collective-permute-start | bytes 258056 | tf_op jit(solution)/shard_map/ppermute | solution.py:467
  27.8 3.6 %rest.1 = (bf16[4,52,768]{2,1,0:T(8,128)(2,1)S(1)}, bf16[4,52,768]{2,1,0:T(8,128)(2,1)S(1)}) custom-call(bf16[208,3072]{1,0:T(8,128)(2,1)S(1)} %get-tuple-element.80.act, f32[208,768]{1,0:T(8,128)S(1)} %get-tuple-element.77.refs_8_.resid, f32[208,768]{1,0:T(8,128)S(1)} %get-tuple-element.81.dres, bf16[12,272,208]{2,1,0:T(8,128)(2,1)S(1)} %get-tuple-element.76.refs_7_.p_bf, ...), custom_call_target="tpu_custom_call" | custom-call | flops 1717567488 | bytes 14911488 | tf_op jit(solution)/shard_map/rest/pallas_call | solution.py:66
  31.4 0.0 collective-permute-done.8.refs_4_
  31.4 0.0 collective-permute-done.7.refs_3_
  31.4 0.0 collective-permute-done.6.refs_2_
  31.4 0.1 combine.1
  31.5 0.1 collective-permute-start.9
  31.6 1.3 %collective-permute-done.9.refs_1_ = f32[56,384]{1,0:T(8,128)S(1)} collective-permute-done((f32[56,384]{1,0:T(8,128)S(1)}, f32[56,384]{1,0:T(8,128)S(1)}, u32[]{:S(2)}, u32[]{:S(2)}) %collective-permute-start.9) | collective-permute-done | bytes 86048 | tf_op jit(solution)/shard_map/ppermute | solution.py:476
  32.9 1.6 %collective-permute-start.13 = (bf16[56,384]{1,0:T(8,128)(2,1)S(1)}, bf16[56,384]{1,0:T(8,128)(2,1)S(1)}, u32[]{:S(2)}, u32[]{:S(2)}) collective-permute-start(bf16[56,384]{1,0:T(8,128)(2,1)S(1)} %add.3.after.refs_0_), channel_id=1, source_target_pairs={{0,2},{1,3},{2,0},{3,1},{4,6},{5,7},{6,4},{7,5},{8,10},{9,11},{10,... | collective-permute-start | bytes 129032 | tf_op jit(solution)/shard_map/ppermute | solution.py:482
  34.6 0.9 %collective-permute-start.10 = (bf16[2,52,768]{2,1,0:T(8,128)(2,1)S(1)}, bf16[2,52,768]{2,1,0:T(8,128)(2,1)S(1)}, u32[]{:S(2)}, u32[]{:S(2)}) collective-permute-start(bf16[2,52,768]{2,1,0:T(8,128)(2,1)S(1)} %get-tuple-element.94), channel_id=1, source_target_pairs={{0,8},{8,0},{16,24},{24,16},{1,9},{9,1},{17,25},{25,17},{2,10},{10... | collective-permute-start | bytes 479240 | tf_op jit(solution)/shard_map/ppermute | solution.py:496
  35.5 1.2 %collective-permute-start.11 = (bf16[2,52,768]{2,1,0:T(8,128)(2,1)S(1)}, bf16[2,52,768]{2,1,0:T(8,128)(2,1)S(1)}, u32[]{:S(2)}, u32[]{:S(2)}) collective-permute-start(bf16[2,52,768]{2,1,0:T(8,128)(2,1)S(1)} %get-tuple-element.95), channel_id=1, source_target_pairs={{0,16},{8,24},{16,0},{24,8},{1,17},{9,25},{17,1},{25,9},{2,18},{10... | collective-permute-start | bytes 479240 | tf_op jit(solution)/shard_map/ppermute | solution.py:496
  36.7 1.5 %collective-permute-start.12 = (bf16[2,52,768]{2,1,0:T(8,128)(2,1)S(1)}, bf16[2,52,768]{2,1,0:T(8,128)(2,1)S(1)}, u32[]{:S(2)}, u32[]{:S(2)}) collective-permute-start(bf16[2,52,768]{2,1,0:T(8,128)(2,1)S(1)} %get-tuple-element.96), channel_id=1, source_target_pairs={{0,24},{8,16},{16,8},{24,0},{1,25},{9,17},{17,9},{25,1},{2,26},{10... | collective-permute-start | bytes 479240 | tf_op jit(solution)/shard_map/ppermute | solution.py:496
  38.2 0.0 collective-permute-done.13.refs_1_
  38.2 2.6 %collective-permute-start.14 = (bf16[56,384]{1,0:T(8,128)(2,1)S(1)}, bf16[56,384]{1,0:T(8,128)(2,1)S(1)}, u32[]{:S(2)}, u32[]{:S(2)}) collective-permute-start(bf16[56,384]{1,0:T(8,128)(2,1)S(1)} %add.4.refs_0_), channel_id=1, source_target_pairs={{0,4},{1,5},{2,6},{3,7},{4,0},{5,1},{6,2},{7,3},{8,12},{9,13},{10,... | collective-permute-start | bytes 129032 | tf_op jit(solution)/shard_map/ppermute | solution.py:482
  40.8 2.7 %collective-permute-done.14.refs_1_ = bf16[56,384]{1,0:T(8,128)(2,1)S(1)} collective-permute-done((bf16[56,384]{1,0:T(8,128)(2,1)S(1)}, bf16[56,384]{1,0:T(8,128)(2,1)S(1)}, u32[]{:S(2)}, u32[]{:S(2)}) %collective-permute-start.14) | collective-permute-done | bytes 43040 | tf_op jit(solution)/shard_map/ppermute | solution.py:482
  43.5 0.1 collective-permute-start.15
  43.6 0.0 collective-permute-done.10.refs_1_
  43.6 1.5 %collective-permute-done.11.refs_2_ = bf16[2,52,768]{2,1,0:T(8,128)(2,1)S(1)} collective-permute-done((bf16[2,52,768]{2,1,0:T(8,128)(2,1)S(1)}, bf16[2,52,768]{2,1,0:T(8,128)(2,1)S(1)}, u32[]{:S(2)}, u32[]{:S(2)}) %collective-permute-start.11) | collective-permute-done | bytes 159776 | tf_op jit(solution)/shard_map/ppermute | solution.py:496
  45.1 0.0 collective-permute-done.12.refs_3_
  45.1 0.0 collective-permute-done.15.refs_5_
  45.1 0.0 copy-done.2
  45.1 2.3 %final.1 = (bf16[3,52,768]{2,1,0:T(8,128)(2,1)}, bf16[3,52,768]{2,1,0:T(8,128)(2,1)}, f32[8,50]{1,0:T(8,128)}, f32[8,768]{1,0:T(8,128)}, f32[50,1,768]{2,1,0:T(1...) custom-call(bf16[2,52,768]{2,1,0:T(8,128)(2,1)S(1)} %get-tuple-element.93.refs_0_, ...), custom_call_target="tpu_custom_call" | custom-call | bytes 1314816 | tf_op jit(solution)/shard_map/final/pallas_call | solution.py:66
  (15 shorter events, 0.1 us)
Async XLA Ops:
  1.7 9.6 %collective-permute-start.3 = (bf16[52,768]{1,0:T(8,128)(2,1)S(1)}, bf16[52,768]{1,0:T(8,128)(2,1)S(1)}, u32[]{:S(2)}, u32[]{:S(2)}) collective-permute-start(bf16[52,768]{1,0:T(8,128)(2,1)S(1)} %get-tuple-element.62), channel_id=1, source_target_pairs={{0,8},{8,0},{16,24},{24,16},{1,9},{9,1},{17,25},{25,17},{2,10},{10... | collective-permute-start | bytes 239624 | tf_op jit(solution)/shard_map/ppermute | solution.py:405
  4.7 6.7 %collective-permute-start.4 = (bf16[52,768]{1,0:T(8,128)(2,1)S(1)}, bf16[52,768]{1,0:T(8,128)(2,1)S(1)}, u32[]{:S(2)}, u32[]{:S(2)}) collective-permute-start(bf16[52,768]{1,0:T(8,128)(2,1)S(1)} %get-tuple-element.63), channel_id=1, source_target_pairs={{0,16},{8,24},{16,0},{24,8},{1,17},{9,25},{17,1},{25,9},{2,18},{10... | collective-permute-start | bytes 239624 | tf_op jit(solution)/shard_map/ppermute | solution.py:405
  6.2 6.1 %collective-permute-start.5 = (bf16[52,768]{1,0:T(8,128)(2,1)S(1)}, bf16[52,768]{1,0:T(8,128)(2,1)S(1)}, u32[]{:S(2)}, u32[]{:S(2)}) collective-permute-start(bf16[52,768]{1,0:T(8,128)(2,1)S(1)} %get-tuple-element.64), channel_id=1, source_target_pairs={{0,24},{8,16},{16,8},{24,0},{1,25},{9,17},{17,9},{25,1},{2,26},{10... | collective-permute-start | bytes 239624 | tf_op jit(solution)/shard_map/ppermute | solution.py:405
  6.2 10.5 %slice-start = ((s8[4718592]{0:T(1024)(128)(4,1)}), s8[4194304]{0:T(1024)(128)(4,1)S(1)}, s32[]{:S(2)}) async-start(s8[4718592]{0:T(1024)(128)(4,1)} %bitcast.5), calls=%async_computation | async-start | bytes 8388608
  6.2 10.5 %slice-start.2 = ((s8[4718592]{0:T(1024)(128)(4,1)}), s8[4194304]{0:T(1024)(128)(4,1)S(1)}, s32[]{:S(2)}) async-start(s8[4718592]{0:T(1024)(128)(4,1)} %bitcast.7), calls=%async_computation.2 | async-start | bytes 8388608
  6.3 6.1 %copy-start = (bf16[768,2304]{1,0:T(8,128)(2,1)S(1)}, bf16[768,2304]{1,0:T(8,128)(2,1)}, u32[]{:S(2)}) copy-start(bf16[768,2304]{1,0:T(8,128)(2,1)} %w_qkv.1) | copy-start | bytes 10616836
  6.3 6.1 %copy-start.1 = (bf16[768,768]{1,0:T(8,128)(2,1)S(1)}, bf16[768,768]{1,0:T(8,128)(2,1)}, u32[]{:S(2)}) copy-start(bf16[768,768]{1,0:T(8,128)(2,1)} %refs_11_.1) | copy-start | bytes 3538948
  6.3 10.5 %slice-start.1 = ((s8[4718592]{0:T(1024)(128)(4,1)}), s8[524288]{0:T(1024)(128)(4,1)S(1)}, s32[]{:S(2)}) async-start(s8[4718592]{0:T(1024)(128)(4,1)} %bitcast.5), calls=%async_computation.1 | async-start | bytes 1048576
  6.3 10.5 %slice-start.3 = ((s8[4718592]{0:T(1024)(128)(4,1)}), s8[524288]{0:T(1024)(128)(4,1)S(1)}, s32[]{:S(2)}) async-start(s8[4718592]{0:T(1024)(128)(4,1)} %bitcast.7), calls=%async_computation.3 | async-start | bytes 1048576
  7.8 8.4 %collective-permute-start = (bf16[52,768]{1,0:T(8,128)(2,1)S(1)}, bf16[52,768]{1,0:T(8,128)(2,1)S(1)}, u32[]{:S(2)}, u32[]{:S(2)}) collective-permute-start(bf16[52,768]{1,0:T(8,128)(2,1)S(1)} %get-tuple-element.58), channel_id=1, source_target_pairs={{0,8},{8,0},{16,24},{24,16},{1,9},{9,1},{17,25},{25,17},{2,10},{10... | collective-permute-start | bytes 239624 | tf_op jit(solution)/shard_map/ppermute | solution.py:406
  9.8 6.4 %collective-permute-start.1 = (bf16[52,768]{1,0:T(8,128)(2,1)S(1)}, bf16[52,768]{1,0:T(8,128)(2,1)S(1)}, u32[]{:S(2)}, u32[]{:S(2)}) collective-permute-start(bf16[52,768]{1,0:T(8,128)(2,1)S(1)} %get-tuple-element.59), channel_id=1, source_target_pairs={{0,16},{8,24},{16,0},{24,8},{1,17},{9,25},{17,1},{25,9},{2,18},{10... | collective-permute-start | bytes 239624 | tf_op jit(solution)/shard_map/ppermute | solution.py:406
  11.3 5.4 %collective-permute-start.2 = (bf16[52,768]{1,0:T(8,128)(2,1)S(1)}, bf16[52,768]{1,0:T(8,128)(2,1)S(1)}, u32[]{:S(2)}, u32[]{:S(2)}) collective-permute-start(bf16[52,768]{1,0:T(8,128)(2,1)S(1)} %get-tuple-element.60), channel_id=1, source_target_pairs={{0,24},{8,16},{16,8},{24,0},{1,25},{9,17},{17,9},{25,1},{2,26},{10... | collective-permute-start | bytes 239624 | tf_op jit(solution)/shard_map/ppermute | solution.py:406
  24.2 7.2 %collective-permute-start.8 = (bf16[56,768]{1,0:T(8,128)(2,1)S(1)}, bf16[56,768]{1,0:T(8,128)(2,1)S(1)}, u32[]{:S(2)}, u32[]{:S(2)}) collective-permute-start(bf16[56,768]{1,0:T(8,128)(2,1)S(1)} %get-tuple-element.90.refs_1_), channel_id=1, source_target_pairs={{0,24},{8,16},{16,8},{24,0},{1,25},{9,17},{17,9},{25,1},{2,26},{10... | collective-permute-start | bytes 258056 | tf_op jit(solution)/shard_map/ppermute | solution.py:467
  25.8 5.6 %collective-permute-start.7 = (bf16[56,768]{1,0:T(8,128)(2,1)S(1)}, bf16[56,768]{1,0:T(8,128)(2,1)S(1)}, u32[]{:S(2)}, u32[]{:S(2)}) collective-permute-start(bf16[56,768]{1,0:T(8,128)(2,1)S(1)} %get-tuple-element.90.refs_1_), channel_id=1, source_target_pairs={{0,16},{8,24},{16,0},{24,8},{1,17},{9,25},{17,1},{25,9},{2,18},{10... | collective-permute-start | bytes 258056 | tf_op jit(solution)/shard_map/ppermute | solution.py:467
  26.3 5.1 %collective-permute-start.6 = (bf16[56,768]{1,0:T(8,128)(2,1)S(1)}, bf16[56,768]{1,0:T(8,128)(2,1)S(1)}, u32[]{:S(2)}, u32[]{:S(2)}) collective-permute-start(bf16[56,768]{1,0:T(8,128)(2,1)S(1)} %get-tuple-element.90.refs_1_), channel_id=1, source_target_pairs={{0,8},{8,0},{16,24},{24,16},{1,9},{9,1},{17,25},{25,17},{2,10},{10... | collective-permute-start | bytes 258056 | tf_op jit(solution)/shard_map/ppermute | solution.py:467
  31.5 1.3 %collective-permute-start.9 = (f32[56,384]{1,0:T(8,128)S(1)}, f32[56,384]{1,0:T(8,128)S(1)}, u32[]{:S(2)}, u32[]{:S(2)}) collective-permute-start(f32[56,384]{1,0:T(8,128)S(1)} %get-tuple-element.92), channel_id=1, source_target_pairs={{0,1},{1,0},{2,3},{3,2},{4,5},{5,4},{6,7},{7,6},{8,9},{9,8},{10,11... | collective-permute-start | bytes 258056 | tf_op jit(solution)/shard_map/ppermute | solution.py:476
  32.9 5.3 %collective-permute-start.13 = (bf16[56,384]{1,0:T(8,128)(2,1)S(1)}, bf16[56,384]{1,0:T(8,128)(2,1)S(1)}, u32[]{:S(2)}, u32[]{:S(2)}) collective-permute-start(bf16[56,384]{1,0:T(8,128)(2,1)S(1)} %add.3.after.refs_0_), channel_id=1, source_target_pairs={{0,2},{1,3},{2,0},{3,1},{4,6},{5,7},{6,4},{7,5},{8,10},{9,11},{10,... | collective-permute-start | bytes 129032 | tf_op jit(solution)/shard_map/ppermute | solution.py:482
  34.6 10.5 %copy-start.2 = (f32[50,768]{1,0:T(8,128)S(1)}, f32[50,768]{1,0:T(8,128)}, u32[]{:S(2)}) copy-start(f32[50,768]{1,0:T(8,128)} %refs_8_.3) | copy-start | bytes 460804
  34.6 10.5 %copy-start.3 = (f32[50,768]{1,0:T(8,128)S(1)}, f32[50,768]{1,0:T(8,128)}, u32[]{:S(2)}) copy-start(f32[50,768]{1,0:T(8,128)} %refs_9_.3) | copy-start | bytes 460804
  34.6 10.5 %copy-start.4 = (f32[768,8]{0,1:T(8,128)S(1)}, f32[768,8]{0,1:T(8,128)}, u32[]{:S(2)}) copy-start(f32[768,8]{0,1:T(8,128)} %param.35) | copy-start | bytes 73732
  34.6 9.0 %collective-permute-start.10 = (bf16[2,52,768]{2,1,0:T(8,128)(2,1)S(1)}, bf16[2,52,768]{2,1,0:T(8,128)(2,1)S(1)}, u32[]{:S(2)}, u32[]{:S(2)}) collective-permute-start(bf16[2,52,768]{2,1,0:T(8,128)(2,1)S(1)} %get-tuple-element.94), channel_id=1, source_target_pairs={{0,8},{8,0},{16,24},{24,16},{1,9},{9,1},{17,25},{25,17},{2,10},{10... | collective-permute-start | bytes 479240 | tf_op jit(solution)/shard_map/ppermute | solution.py:496
  35.5 9.6 %collective-permute-start.11 = (bf16[2,52,768]{2,1,0:T(8,128)(2,1)S(1)}, bf16[2,52,768]{2,1,0:T(8,128)(2,1)S(1)}, u32[]{:S(2)}, u32[]{:S(2)}) collective-permute-start(bf16[2,52,768]{2,1,0:T(8,128)(2,1)S(1)} %get-tuple-element.95), channel_id=1, source_target_pairs={{0,16},{8,24},{16,0},{24,8},{1,17},{9,25},{17,1},{25,9},{2,18},{10... | collective-permute-start | bytes 479240 | tf_op jit(solution)/shard_map/ppermute | solution.py:496
  36.7 8.4 %collective-permute-start.12 = (bf16[2,52,768]{2,1,0:T(8,128)(2,1)S(1)}, bf16[2,52,768]{2,1,0:T(8,128)(2,1)S(1)}, u32[]{:S(2)}, u32[]{:S(2)}) collective-permute-start(bf16[2,52,768]{2,1,0:T(8,128)(2,1)S(1)} %get-tuple-element.96), channel_id=1, source_target_pairs={{0,24},{8,16},{16,8},{24,0},{1,25},{9,17},{17,9},{25,1},{2,26},{10... | collective-permute-start | bytes 479240 | tf_op jit(solution)/shard_map/ppermute | solution.py:496
  38.2 5.3 %collective-permute-start.14 = (bf16[56,384]{1,0:T(8,128)(2,1)S(1)}, bf16[56,384]{1,0:T(8,128)(2,1)S(1)}, u32[]{:S(2)}, u32[]{:S(2)}) collective-permute-start(bf16[56,384]{1,0:T(8,128)(2,1)S(1)} %add.4.refs_0_), channel_id=1, source_target_pairs={{0,4},{1,5},{2,6},{3,7},{4,0},{5,1},{6,2},{7,3},{8,12},{9,13},{10,... | collective-permute-start | bytes 129032 | tf_op jit(solution)/shard_map/ppermute | solution.py:482
  43.5 1.5 %collective-permute-start.15 = (f32[56,384]{1,0:T(8,128)S(1)}, f32[56,384]{1,0:T(8,128)S(1)}, u32[]{:S(2)}, u32[]{:S(2)}) collective-permute-start(f32[56,384]{1,0:T(8,128)S(1)} %add.5.refs_4_), channel_id=1, source_target_pairs={{0,1},{1,0},{2,3},{3,2},{4,5},{5,4},{6,7},{7,6},{8,9},{9,8},{10,11... | collective-permute-start | bytes 258056 | tf_op jit(solution)/shard_map/ppermute | solution.py:485

commit v4 on v3

--- a/solution.py
+++ b/solution.py
@@ -98,27 +98,31 @@
         copy.wait()
 
 
-def pick_kernel(seq, images, small, source, *refs):
-    sources, refs = refs[:small], refs[small:]
-    chunks, targets, sems = refs[:seq], refs[seq:-1], refs[-1]
+def pick_kernel(seq, images, tok, cot, *refs):
+    outs, sems = refs[:-1], refs[-1]
     me = lax.axis_index("seq")
     start = Copies(sems)
-    copies = [
-        start(source.at[jnp.minimum(me ^ k, images - 1)], chunks[k]) for k in range(seq)
-    ]
-    for a, b in zip(sources, targets):
-        copies.append(start(a, b if len(a.shape) > 1 else b.at[0]))
+    copies = []
+    for part, source in enumerate((tok, cot)):
+        for k in range(seq):
+            index = jnp.minimum(me ^ k, images - 1)
+            copies.append(start(source.at[index], outs[part * seq + k]))
     wait(*copies)
+
+
+def line(ref):
+    return ref[...].reshape(1, -1)
 
 
 def forward_kernel(seq, images, *refs):
     toks, refs = refs[:seq], refs[seq:]
     (
-        mask, prompts, gain_one, shift_one, b_qkv, b_out, gain_two, shift_two, w_qkv, w_out,
-        x_bf, query, keys, values, p_f, p_bf, resid, normed_two,
+        mask, prompts, gain_one, shift_one, b_qkv, b_out, gain_two, shift_two, w_qkv, w_out, w_down,
+        x_bf, query, keys, values, p_f, p_bf, resid, normed_two, w_down_t,
         x, tbuf, normed, bias, mix_t,
     ) = refs
     me = lax.axis_index("seq")
+    gain, shift, bias_qkv = line(gain_one), line(shift_one), line(b_qkv)
     rows, width = x.shape
     chunk = rows // seq
     head = width // HEADS
@@ -127,7 +131,7 @@
     scale = head ** (-0.5)
     parts = [pl.ds(part * width, width) for part in range(3)]
     for k in range(seq):
-        tbuf[k] = toks[k][...]
+        tbuf[(seq - k) % seq] = toks[k][...]
     live = jnp.where(me < images, 1.0, 0.0)
     for c in range(seq):
         x[pl.ds(c * chunk, chunk), :] = tbuf[me ^ c].astype(F32) * live
@@ -140,14 +144,14 @@
     bias[:rows, :] = jnp.where(mcol > 0.5, 0.0, -jnp.inf)
     bias[rows:, :] = jnp.where(rest < count, 0.0, -jnp.inf)
     hat, _ = normalize(x[...])
-    normed[:rows, :] = (hat * gain_one[...] + shift_one[...]).astype(BF16)
+    normed[:rows, :] = (hat * gain + shift).astype(BF16)
     hat, _ = normalize(prompts[...].astype(BF16).astype(F32))
     normed[rows:, :] = jnp.zeros((nkeys - rows, width), BF16)
-    normed[rows : rows + count, :] = (hat * gain_one[...] + shift_one[...]).astype(BF16)
-    query[...] = (dot(normed[:rows, :], w_qkv[:, parts[0]]) + b_qkv[:, parts[0]]).astype(BF16)
+    normed[rows : rows + count, :] = (hat * gain + shift).astype(BF16)
+    query[...] = (dot(normed[:rows, :], w_qkv[:, parts[0]]) + bias_qkv[:, :width]).astype(BF16)
     for index, dest in ((1, keys), (2, values)):
         part = parts[index]
-        dest[...] = (dot(normed[...], w_qkv[:, part]) + b_qkv[:, part]).astype(BF16)
+        dest[...] = (dot(normed[...], w_qkv[:, part]) + bias_qkv[:, index * width : (index + 1) * width]).astype(BF16)
     lane = lax.broadcasted_iota(jnp.int32, (rows, 2 * head), 1) // head
     for h in range(HEADS):
         cols = pl.ds(h // 2 * 2 * head, 2 * head)
@@ -158,12 +162,14 @@
         prob = ex * (1.0 / jnp.sum(ex, axis=0, keepdims=True))
         p_f[h] = prob
         p_bf[h] = prob.astype(BF16)
+        slab = w_down.shape[0] // HEADS
+        w_down_t[:, pl.ds(h * slab, slab)] = w_down[pl.ds(h * slab, slab), :].T
     for h in range(HEADS):
         both = dot_tn(values[:, pl.ds(h // 2 * 2 * head, 2 * head)], p_bf[h])
         mix_t[pl.ds(h * head, head), :] = both[h % 2 * head :][:head].astype(BF16)
-    resid[...] = x[...] + dot_tn(mix_t[...], w_out[...]) + b_out[...]
+    resid[...] = x[...] + dot_tn(mix_t[...], w_out[...]) + line(b_out)
     hat, _ = normalize(resid[...])
-    normed_two[...] = (hat * gain_two[...] + shift_two[...]).astype(BF16)
+    normed_two[...] = (hat * line(gain_two) + line(shift_two)).astype(BF16)
 
 
 def backward_kernel(seq, images, *refs):
@@ -183,23 +189,24 @@
     count = prompts.shape[0]
     scale = head ** (-0.5)
     for k in range(seq):
-        tbuf[k] = cots[k][...]
+        tbuf[(seq - k) % seq] = cots[k][...]
     live = jnp.where(me < images, 1.0, 0.0)
     for c in range(seq):
         gbuf[pl.ds(c * chunk, chunk), :] = tbuf[me ^ c].astype(F32) * live
     grad_out = gbuf[...].astype(BF16)
+    bias_up = line(b_up)
     step = 256
     for c in range(ff // step):
         cols = pl.ds(c * step, step)
-        hidden = dot(normed_two[...], w_up[:, cols]) + b_up[:, cols]
-        grad = dot_nt(grad_out, w_down[cols, :])
+        hidden = dot(normed_two[...], w_up[:, cols]) + bias_up[:, c * step : (c + 1) * step]
+        grad = dot(grad_out, w_down[:, cols])
         cdf = 0.5 * (1.0 + lax.erf(hidden * math.sqrt(0.5)))
         act[:, cols] = (hidden * cdf).astype(BF16)
         pdf = jnp.exp(-0.5 * hidden * hidden) * (1.0 / math.sqrt(2.0 * math.pi))
         dhid[:, cols] = (grad * (cdf + hidden * pdf)).astype(BF16)
     hat_two, rstd_two = normalize(resid[...])
     grad_resid = gbuf[...] + norm_back(
-        hat_two, rstd_two, gain_two[...], dot_nt(dhid[...], w_up[...])
+        hat_two, rstd_two, line(gain_two), dot_nt(dhid[...], w_up[...])
     )
     dres[...] = grad_resid
     dmix[...] = dot_nt(dres[...].astype(BF16), w_out[...]).astype(BF16)
@@ -231,18 +238,24 @@
     three = dot_nt(jnp.concatenate([first, second, third], 0), w_kv)
     grad_normed = three[:pad] + three[pad : 2 * pad] + three[2 * pad :]
     hat_p, rstd_p = normalize(prompts[...].astype(BF16).astype(F32))
-    part = norm_back(hat_p, rstd_p, gain_one[...], grad_normed[:count, :]).astype(pgrad.dtype)
+    part = norm_back(hat_p, rstd_p, line(gain_one), grad_normed[:count, :]).astype(pgrad.dtype)
     pgrad[...] = jnp.zeros_like(pgrad)
     pgrad[:count, :] = part
 
 
+def spans(chunk):
+    full = chunk // 16 * 16
+    return ((0, full), (full, chunk)) if full < chunk else ((0, full),)
+
+
 def rest_kernel(
     seq, act, resid, dres, p_bf, ds_bf, query, dmix, keys, x_bf, w_down, w_qkv, b_down, gain,
-    out, grad, dqkv, q_t, wide, k_t,
+    pack, dqkv, q_t, wide, k_t,
 ):
     rows, width = query.shape
     head = width // HEADS
-    chunk = out.shape[1]
+    chunk = rows // seq
+    full = spans(chunk)[0][1]
     k_t[...] = keys[...].T
     low = lax.broadcasted_iota(jnp.int32, (rows, 2 * head), 1) < head
     for pair in range(HEADS // 2):
@@ -257,20 +270,25 @@
         part = pl.ds(h * head, head)
         q_t[part, :] = dot(k_t[part, :], ds_bf[h]).astype(BF16)
     dqkv[:, :width] = q_t[...].T
-    wide[...] = resid[...] + dot(act[...], w_down[...]) + b_down[...]
+    wide[...] = resid[...] + dot(act[...], w_down[...]) + line(b_down)
     for c in range(seq):
-        out[c] = wide[pl.ds(c * chunk, chunk), :].astype(BF16)
+        for (low, high), at in zip(spans(chunk), (0, 2 * full)):
+            pack[c, pl.ds(at, high - low), :] = wide[pl.ds(c * chunk + low, high - low), :].astype(
+                BF16
+            )
     hat, rstd = normalize(x_bf[...].astype(F32))
-    wide[...] = dres[...] + norm_back(hat, rstd, gain[...], dot_nt(dqkv[...], w_qkv[...]))
+    wide[...] = dres[...] + norm_back(hat, rstd, line(gain), dot_nt(dqkv[...], w_qkv[...]))
     for c in range(seq):
-        grad[c] = wide[pl.ds(c * chunk, chunk), :].astype(BF16)
-
-
-def pack_kernel(seq, out, grad, after, *packs):
+        for (low, high), at in zip(spans(chunk), (full, full + chunk)):
+            pack[c, pl.ds(at, high - low), :] = wide[pl.ds(c * chunk + low, high - low), :].astype(
+                BF16
+            )
+
+
+def pack_kernel(seq, pack, after, *packs):
     me = lax.axis_index("seq")
     for k in range(seq):
-        packs[k][0] = out[me ^ k]
-        packs[k][1] = grad[me ^ k]
+        packs[k][...] = pack[me ^ k]
 
 
 def tree(values):
@@ -307,11 +325,14 @@
         whole,
     ) = refs
     me = lax.axis_index("seq")
+    chunk = layer_out.shape[1]
+    full = spans(chunk)[0][1]
     for k in range(seq):
         @pl.when((me ^ k) < images)
         def _():
-            layer_out[me ^ k] = back[k][0]
-            input_grad[me ^ k] = back[k][1]
+            for target, places in ((layer_out, (0, 2 * full)), (input_grad, (full, full + chunk))):
+                for (low, high), at in zip(spans(chunk), places):
+                    target[me ^ k, pl.ds(low, high - low), :] = back[k][pl.ds(at, high - low), :]
     half = mine.shape[1]
     count, width = prompts.shape
     rank = start_t.shape[0]
@@ -378,42 +399,31 @@
     pad = up(count, 8)
     dma = pltpu.SemaphoreType.DMA
 
-    piece = ((2, chunk, width), BF16)
+    piece = ((2 * chunk, width), BF16)
     one = ((chunk, width), BF16)
-    row = lambda v: ((1, v.size), v.dtype) if v.ndim == 1 else (v.shape, v.dtype)
-    small = (
-        key_mask, prompts, gain_one, shift_one, b_qkv, b_out, gain_two, shift_two, b_up, b_down,
-        error_buffer.transpose(1, 0, 2),
-    )
-
-    def pick(source, small, flops):
-        return call(
-            functools.partial(pick_kernel, seq, images, len(small)),
-            [one] * seq + [row(v) for v in small],
-            (source, *small),
-            [dma((seq + len(small),))],
-            in_specs=[HBM] * (1 + len(small)),
-            flops=flops,
-            name="pick",
-        )
-
-    toks = pick(tokens, (), 0)
-    picked = pick(cotangent, small, 1 << 34)
-    cots, small = picked[:seq], picked[seq:]
-    mask, prompts_held, gain_one, shift_one, b_qkv, b_out, gain_two, shift_two = small[:8]
-    b_up, b_down, error_rows = small[8:]
-    toks = [toks[0]] + [lax.ppermute(toks[k], "seq", flip(k, seq)) for k in range(1, seq)]
-    cots = [cots[0]] + [lax.ppermute(cots[k], "seq", flip(k, seq)) for k in range(1, seq)]
+    picked = call(
+        functools.partial(pick_kernel, seq, images),
+        [one] * (2 * seq),
+        (tokens, cotangent),
+        [dma((2 * seq,))],
+        in_specs=[HBM] * 2,
+        flops=1 << 34,
+        name="pick",
+    )
+    toks, cots = picked[:seq], picked[seq:]
+    error_rows = error_buffer.transpose(1, 0, 2)
+    toks = [toks[0]] + [lax.ppermute(toks[k], "seq", flip(k, seq)) for k in range(seq - 1, 0, -1)]
+    cots = [cots[0]] + [lax.ppermute(cots[k], "seq", flip(k, seq)) for k in range(seq - 1, 0, -1)]
 
     wide = ((rows, width), BF16)
     long = ((nkeys, width), BF16)
     probs = (HEADS, nkeys, rows)
-    x_bf, query, keys, values, p_f, p_bf, resid, normed_two = call(
+    x_bf, query, keys, values, p_f, p_bf, resid, normed_two, w_down_t = call(
         functools.partial(forward_kernel, seq, images),
-        [wide, wide, long, long, (probs, F32), (probs, BF16), ((rows, width), F32), wide],
+        [wide, wide, long, long, (probs, F32), (probs, BF16), ((rows, width), F32), wide, ((width, ff), BF16)],
         (
-            *toks, mask, prompts_held, gain_one, shift_one, b_qkv, b_out, gain_two, shift_two,
-            w_qkv, w_out,
+            *toks, key_mask, prompts, gain_one, shift_one, b_qkv, b_out, gain_two, shift_two,
+            w_qkv, w_out, w_down,
         ),
         [
             pltpu.VMEM((rows, width), F32),
@@ -435,7 +445,7 @@
         ],
         (
             *cots, query, values, p_f, p_bf, resid, normed_two, w_qkv, w_out, gain_two,
-            w_up, b_up, w_down, prompts_held, gain_one,
+            w_up, b_up, w_down_t, prompts, gain_one,
         ),
         [
             pltpu.VMEM((rows, width), F32),
@@ -449,9 +459,9 @@
     )
     kept = (act, resid, dres, p_bf, ds_bf, query, dmix, keys, x_bf)
 
-    out_chunks, grad_chunks = call(
+    (chunks,) = call(
         functools.partial(rest_kernel, seq),
-        [((seq, chunk, width), BF16)] * 2,
+        [((seq, 2 * chunk, width), BF16)],
         (*kept, w_down, w_qkv, b_down, gain_one),
         [
             pltpu.VMEM((rows, 3 * width), BF16),
@@ -469,7 +479,7 @@
     combined, keep, give = call(
         combine_kernel,
         [((pad, width), F32), ((pad, half), F32), ((pad, half), F32)],
-        (error_rows, *parts, out_chunks),
+        (error_rows, *parts, chunks),
         in_specs=[VMEM] * (1 + seq) + [ANY],
         name="combine",
     )
@@ -487,8 +497,8 @@
     packs = call(
         functools.partial(pack_kernel, seq),
         [piece] * seq,
-        (out_chunks, grad_chunks, first),
-        in_specs=[VMEM] * 2 + [ANY],
+        (chunks, first),
+        in_specs=[VMEM, ANY],
         flops=1 << 32,
         name="pack",
     )

time: 47.5 us -> 47.1 us (level)
  starting transfers between devices: 19.6 us -> 20.7 us
  Pallas kernels: 19.9 us -> 18.9 us
  waiting for transfers between devices: 6.93 us -> 6.34 us
    pallas_call x11 -> x10, Pallas kernels: 19.9 us -> 18.9 us  [call(): pl.pallas_call(kernel, out_shape=[held.get(id(spec), jax.ShapeDtypeStruct...]
    ppermute x3, starting transfers between devices: 3.55 us -> 4.43 us  [body(): lax.ppermute(cots[k], 'seq', flip(k, seq))]
    ppermute x3, waiting for transfers between devices: 0.49 us -> 0.01 us  [body(): lax.ppermute(cots[k], 'seq', flip(k, seq))]
  transfers between devices with their start and end apart: 16 -> 16, of which waited for: 5 -> 6; matrix products, arithmetic and copies ran while one was open for 0% -> 0% of each run, Pallas kernels for 19% -> 17%
where the time goes in v4:
time: 47.1 us; the launch traced here: 47 us
  starting transfers between devices  20.7 us (44%)
  Pallas kernels  18.9 us (40%)
  waiting for transfers between devices  6.34 us (13%)
  between operations  0.98 us (2%)
    pallas_call x10, Pallas kernels, call(): pl.pallas_call(kernel, out_shape=[held.get(id(spec), jax.ShapeDtypeStruct...  18.9 us
    ppermute x3, starting transfers between devices, body(): lax.ppermute(toks[k], 'seq', flip(k, seq))  4.6 us
    ppermute x3, starting transfers between devices, body(): lax.ppermute(cots[k], 'seq', flip(k, seq))  4.43 us
    ppermute x2, starting transfers between devices, body(): parts = [mine, lax.ppermute(mine, 'dp', flip(bit, dp))]  4.38 us
    ppermute x3, starting transfers between devices, body(): lax.ppermute(pgrad, 'seq', flip(k, seq))  3.55 us
    ppermute x3, starting transfers between devices, body(): lax.ppermute(packs[k], 'seq', flip(k, seq))  3.55 us
    ppermute x2, waiting for transfers between devices, body(): parts = [mine, lax.ppermute(mine, 'dp', flip(bit, dp))]  2.65 us
    ppermute x3, waiting for transfers between devices, body(): lax.ppermute(packs[k], 'seq', flip(k, seq))  1.44 us
  transfers between devices with their start and end apart: 16, of which 6 were waited for; matrix products, arithmetic and copies ran while one was open for 0% of the time, Pallas kernels for 17%

profile of v4, /device:TPU:0, one launch (start us, length us, event | category | flops | bytes accessed | tf_op | source)
XLA Modules:
  0.0 47.0 jit_solution(17674371391468280264)
XLA Ops:
  0.6 0.0 copy-start
  0.6 0.0 copy-start.7
  0.7 0.0 copy-start.4
  0.7 0.0 copy-start.1
  0.7 0.0 copy-start.9
  0.7 1.4 %pick.1 = (bf16[52,768]{1,0:T(8,128)(2,1)S(1)}, bf16[52,768]{1,0:T(8,128)(2,1)S(1)}, bf16[52,768]{1,0:T(8,128)(2,1)S(1)}, bf16[52,768]{1,0:T(8,128)(2,1)S(1)}, b...) custom-call(bf16[3,52,768]{2,1,0:T(8,128)(2,1)} %tok.1, ...), custom_call_target="tpu_custom_call" | custom-call | flops 17179869184 | bytes 479232 | tf_op jit(solution)/shard_map/pick/pallas_call | solution.py:66
  2.2 4.0 %collective-permute-start.3 = (bf16[52,768]{1,0:T(8,128)(2,1)S(1)}, bf16[52,768]{1,0:T(8,128)(2,1)S(1)}, u32[]{:S(2)}, u32[]{:S(2)}) collective-permute-start(bf16[52,768]{1,0:T(8,128)(2,1)S(1)} %get-tuple-element.50), channel_id=1, source_target_pairs={{0,24},{8,16},{16,8},{24,0},{1,25},{9,17},{17,9},{25,1},{2,26},{10... | collective-permute-start | bytes 239624 | tf_op jit(solution)/shard_map/ppermute | solution.py:415
  6.1 0.5 %collective-permute-start.4 = (bf16[52,768]{1,0:T(8,128)(2,1)S(1)}, bf16[52,768]{1,0:T(8,128)(2,1)S(1)}, u32[]{:S(2)}, u32[]{:S(2)}) collective-permute-start(bf16[52,768]{1,0:T(8,128)(2,1)S(1)} %get-tuple-element.51), channel_id=1, source_target_pairs={{0,16},{8,24},{16,0},{24,8},{1,17},{9,25},{17,1},{25,9},{2,18},{10... | collective-permute-start | bytes 239624 | tf_op jit(solution)/shard_map/ppermute | solution.py:415
  6.6 0.1 collective-permute-start.5
  6.8 2.8 %collective-permute-start = (bf16[52,768]{1,0:T(8,128)(2,1)S(1)}, bf16[52,768]{1,0:T(8,128)(2,1)S(1)}, u32[]{:S(2)}, u32[]{:S(2)}) collective-permute-start(bf16[52,768]{1,0:T(8,128)(2,1)S(1)} %get-tuple-element.46), channel_id=1, source_target_pairs={{0,24},{8,16},{16,8},{24,0},{1,25},{9,17},{17,9},{25,1},{2,26},{10... | collective-permute-start | bytes 239624 | tf_op jit(solution)/shard_map/ppermute | solution.py:416
  9.6 0.5 %collective-permute-start.1 = (bf16[52,768]{1,0:T(8,128)(2,1)S(1)}, bf16[52,768]{1,0:T(8,128)(2,1)S(1)}, u32[]{:S(2)}, u32[]{:S(2)}) collective-permute-start(bf16[52,768]{1,0:T(8,128)(2,1)S(1)} %get-tuple-element.47), channel_id=1, source_target_pairs={{0,16},{8,24},{16,0},{24,8},{1,17},{9,25},{17,1},{25,9},{2,18},{10... | collective-permute-start | bytes 239624 | tf_op jit(solution)/shard_map/ppermute | solution.py:416
  10.1 0.0 collective-permute-done.3.refs_1_
  10.1 1.1 %collective-permute-start.2 = (bf16[52,768]{1,0:T(8,128)(2,1)S(1)}, bf16[52,768]{1,0:T(8,128)(2,1)S(1)}, u32[]{:S(2)}, u32[]{:S(2)}) collective-permute-start(bf16[52,768]{1,0:T(8,128)(2,1)S(1)} %get-tuple-element.48), channel_id=1, source_target_pairs={{0,8},{8,0},{16,24},{24,16},{1,9},{9,1},{17,25},{25,17},{2,10},{10... | collective-permute-start | bytes 239624 | tf_op jit(solution)/shard_map/ppermute | solution.py:416
  11.2 0.4 collective-permute-done.4.refs_2_
  11.6 0.5 %collective-permute-done.5.refs_3_ = bf16[52,768]{1,0:T(8,128)(2,1)S(1)} collective-permute-done((bf16[52,768]{1,0:T(8,128)(2,1)S(1)}, bf16[52,768]{1,0:T(8,128)(2,1)S(1)}, u32[]{:S(2)}, u32[]{:S(2)}) %collective-permute-start.5) | collective-permute-done | bytes 79904 | tf_op jit(solution)/shard_map/ppermute | solution.py:415
  12.2 0.0 copy-start.3
  12.2 0.0 copy-start.10
  12.2 4.0 %forward.1 = (bf16[208,768]{1,0:T(8,128)(2,1)S(1)}, bf16[208,768]{1,0:T(8,128)(2,1)S(1)}, bf16[272,768]{1,0:T(8,128)(2,1)S(1)}, bf16[272,768]{1,0:T(8,128)(2,1)S...) custom-call(bf16[52,768]{1,0:T(8,128)(2,1)S(1)} %get-tuple-element.4, ...), custom_call_target="tpu_custom_call" | custom-call | flops 1155268608 | bytes 9937344 | tf_op jit(solution)/shard_map/forward/pallas_call | solution.py:66
  16.2 0.0 collective-permute-done.refs_1_
  16.2 0.0 collective-permute-done.1.refs_2_
  16.2 0.0 collective-permute-done.2.refs_3_
  16.3 0.0 copy-start.16
  16.3 7.3 %backward.1 = (bf16[56,768]{1,0:T(8,128)(2,1)S(1)}, bf16[208,3072]{1,0:T(8,128)(2,1)S(1)}, f32[208,768]{1,0:T(8,128)S(1)}, bf16[12,272,208]{2,1,0:T(8,128)(2,1)S(1)}, bf16[208,768]{1,0:T(8,128)(2,1)S(1)}) custom-call(bf16[52,768]{1,0:T(8,128)(2,1)S(1)} %get-tuple-element.45.refs_0_, bf16[52,768]{1,0:T(8,128)(2,1)S(1)} %collective-permute-done.refs_1_, ...), custom_call_target="tpu_custom_call" | custom-call | flops 3680501760 | bytes 20416512 | tf_op jit(solution)/shard_map/backward/pallas_call | solution.py:66
  23.5 1.6 %collective-permute-start.8 = (bf16[56,768]{1,0:T(8,128)(2,1)S(1)}, bf16[56,768]{1,0:T(8,128)(2,1)S(1)}, u32[]{:S(2)}, u32[]{:S(2)}) collective-permute-start(bf16[56,768]{1,0:T(8,128)(2,1)S(1)} %get-tuple-element.66.refs_1_), channel_id=1, source_target_pairs={{0,24},{8,16},{16,8},{24,0},{1,25},{9,17},{17,9},{25,1},{2,26},{10... | collective-permute-start | bytes 258056 | tf_op jit(solution)/shard_map/ppermute | solution.py:477
  25.1 1.4 %collective-permute-start.7 = (bf16[56,768]{1,0:T(8,128)(2,1)S(1)}, bf16[56,768]{1,0:T(8,128)(2,1)S(1)}, u32[]{:S(2)}, u32[]{:S(2)}) collective-permute-start(bf16[56,768]{1,0:T(8,128)(2,1)S(1)} %get-tuple-element.66.refs_1_), channel_id=1, source_target_pairs={{0,16},{8,24},{16,0},{24,8},{1,17},{9,25},{17,1},{25,9},{2,18},{10... | collective-permute-start | bytes 258056 | tf_op jit(solution)/shard_map/ppermute | solution.py:477
  26.5 0.6 %collective-permute-start.6 = (bf16[56,768]{1,0:T(8,128)(2,1)S(1)}, bf16[56,768]{1,0:T(8,128)(2,1)S(1)}, u32[]{:S(2)}, u32[]{:S(2)}) collective-permute-start(bf16[56,768]{1,0:T(8,128)(2,1)S(1)} %get-tuple-element.66.refs_1_), channel_id=1, source_target_pairs={{0,8},{8,0},{16,24},{24,16},{1,9},{9,1},{17,25},{25,17},{2,10},{10... | collective-permute-start | bytes 258056 | tf_op jit(solution)/shard_map/ppermute | solution.py:477
  27.1 3.8 %rest.1.refs_5_.pack = bf16[4,104,768]{2,1,0:T(8,128)(2,1)S(1)} custom-call(bf16[208,3072]{1,0:T(8,128)(2,1)S(1)} %get-tuple-element.60.act, f32[208,768]{1,0:T(8,128)S(1)} %get-tuple-element.57.refs_8_.resid, f32[208,768]{1,0:T(8,128)S(1)} %get-tuple-element.61.dres, bf16[12,272,208]{2,1,0:T(8,128)(2,1)S(1)} %get-tuple-element.56.refs_7_.p_bf, ...), custom_call_target="tpu_custom_call" | custom-call | flops 1717567488 | bytes 14911488 | tf_op jit(solution)/shard_map/rest/pallas_call | solution.py:66
  30.9 0.0 collective-permute-done.8.refs_4_
  30.9 0.0 collective-permute-done.7.refs_3_
  30.9 0.1 collective-permute-done.6.refs_2_
  31.0 0.1 combine.1
  31.1 0.1 collective-permute-start.9
  31.2 1.3 %collective-permute-done.9.refs_1_ = f32[56,384]{1,0:T(8,128)S(1)} collective-permute-done((f32[56,384]{1,0:T(8,128)S(1)}, f32[56,384]{1,0:T(8,128)S(1)}, u32[]{:S(2)}, u32[]{:S(2)}) %collective-permute-start.9) | collective-permute-done | bytes 86048 | tf_op jit(solution)/shard_map/ppermute | solution.py:486
  32.5 0.0 copy-start.5
  32.5 0.0 copy-start.8
  32.5 1.7 %collective-permute-start.13 = (bf16[56,384]{1,0:T(8,128)(2,1)S(1)}, bf16[56,384]{1,0:T(8,128)(2,1)S(1)}, u32[]{:S(2)}, u32[]{:S(2)}) collective-permute-start(bf16[56,384]{1,0:T(8,128)(2,1)S(1)} %add.3.after.refs_0_), channel_id=1, source_target_pairs={{0,2},{1,3},{2,0},{3,1},{4,6},{5,7},{6,4},{7,5},{8,10},{9,11},{10,... | collective-permute-start | bytes 129032 | tf_op jit(solution)/shard_map/ppermute | solution.py:492
  34.3 1.4 %collective-permute-start.10 = (bf16[104,768]{1,0:T(8,128)(2,1)S(1)}, bf16[104,768]{1,0:T(8,128)(2,1)S(1)}, u32[]{:S(2)}, u32[]{:S(2)}) collective-permute-start(bf16[104,768]{1,0:T(8,128)(2,1)S(1)} %get-tuple-element.70), channel_id=1, source_target_pairs={{0,8},{8,0},{16,24},{24,16},{1,9},{9,1},{17,25},{25,17},{2,10},{10... | collective-permute-start | bytes 479240 | tf_op jit(solution)/shard_map/ppermute | solution.py:506
  35.7 0.7 %collective-permute-start.11 = (bf16[104,768]{1,0:T(8,128)(2,1)S(1)}, bf16[104,768]{1,0:T(8,128)(2,1)S(1)}, u32[]{:S(2)}, u32[]{:S(2)}) collective-permute-start(bf16[104,768]{1,0:T(8,128)(2,1)S(1)} %get-tuple-element.71), channel_id=1, source_target_pairs={{0,16},{8,24},{16,0},{24,8},{1,17},{9,25},{17,1},{25,9},{2,18},{10... | collective-permute-start | bytes 479240 | tf_op jit(solution)/shard_map/ppermute | solution.py:506
  36.3 1.5 %collective-permute-start.12 = (bf16[104,768]{1,0:T(8,128)(2,1)S(1)}, bf16[104,768]{1,0:T(8,128)(2,1)S(1)}, u32[]{:S(2)}, u32[]{:S(2)}) collective-permute-start(bf16[104,768]{1,0:T(8,128)(2,1)S(1)} %get-tuple-element.72), channel_id=1, source_target_pairs={{0,24},{8,16},{16,8},{24,0},{1,25},{9,17},{17,9},{25,1},{2,26},{10... | collective-permute-start | bytes 479240 | tf_op jit(solution)/shard_map/ppermute | solution.py:506
  37.8 0.0 collective-permute-done.13.refs_1_
  37.8 2.7 %collective-permute-start.14 = (bf16[56,384]{1,0:T(8,128)(2,1)S(1)}, bf16[56,384]{1,0:T(8,128)(2,1)S(1)}, u32[]{:S(2)}, u32[]{:S(2)}) collective-permute-start(bf16[56,384]{1,0:T(8,128)(2,1)S(1)} %add.4.refs_0_), channel_id=1, source_target_pairs={{0,4},{1,5},{2,6},{3,7},{4,0},{5,1},{6,2},{7,3},{8,12},{9,13},{10,... | collective-permute-start | bytes 129032 | tf_op jit(solution)/shard_map/ppermute | solution.py:492
  40.5 2.6 %collective-permute-done.14.refs_1_ = bf16[56,384]{1,0:T(8,128)(2,1)S(1)} collective-permute-done((bf16[56,384]{1,0:T(8,128)(2,1)S(1)}, bf16[56,384]{1,0:T(8,128)(2,1)S(1)}, u32[]{:S(2)}, u32[]{:S(2)}) %collective-permute-start.14) | collective-permute-done | bytes 43040 | tf_op jit(solution)/shard_map/ppermute | solution.py:492
  43.2 0.1 collective-permute-start.15
  43.2 0.0 collective-permute-done.10.refs_1_
  43.3 1.4 %collective-permute-done.11.refs_2_ = bf16[104,768]{1,0:T(8,128)(2,1)S(1)} collective-permute-done((bf16[104,768]{1,0:T(8,128)(2,1)S(1)}, bf16[104,768]{1,0:T(8,128)(2,1)S(1)}, u32[]{:S(2)}, u32[]{:S(2)}) %collective-permute-start.11) | collective-permute-done | bytes 159776 | tf_op jit(solution)/shard_map/ppermute | solution.py:506
  44.7 0.0 collective-permute-done.12.refs_3_
  44.7 0.0 collective-permute-done.15.refs_5_
  44.7 2.3 %final.1 = (bf16[3,52,768]{2,1,0:T(8,128)(2,1)}, bf16[3,52,768]{2,1,0:T(8,128)(2,1)}, f32[8,50]{1,0:T(8,128)}, f32[8,768]{1,0:T(8,128)}, f32[50,1,768]{2,1,0:T(1...) custom-call(bf16[104,768]{1,0:T(8,128)(2,1)S(1)} %get-tuple-element.69.refs_0_, ...), custom_call_target="tpu_custom_call" | custom-call | bytes 1314816 | tf_op jit(solution)/shard_map/final/pallas_call | solution.py:66
  (28 shorter events, 0.1 us)
Async XLA Ops:
  0.6 11.5 %copy-start = (bf16[768,2304]{1,0:T(8,128)(2,1)S(1)}, bf16[768,2304]{1,0:T(8,128)(2,1)}, u32[]{:S(2)}) copy-start(bf16[768,2304]{1,0:T(8,128)(2,1)} %w_qkv.1) | copy-start | bytes 10616836
  0.6 11.5 %copy-start.7 = (f32[768]{0:T(1024)S(1)}, f32[768]{0:T(1024)}, u32[]{:S(2)}) copy-start(f32[768]{0:T(1024)} %gain.1) | copy-start | bytes 9220
  0.7 11.5 %copy-start.4 = (f32[50,768]{1,0:T(8,128)S(1)}, f32[50,768]{1,0:T(8,128)}, u32[]{:S(2)}) copy-start(f32[50,768]{1,0:T(8,128)} %refs_8_.3) | copy-start | bytes 460804
  0.7 11.5 %copy-start.1 = (bf16[3072,768]{1,0:T(8,128)(2,1)S(1)}, bf16[3072,768]{1,0:T(8,128)(2,1)}, u32[]{:S(2)}) copy-start(bf16[3072,768]{1,0:T(8,128)(2,1)} %w_down.1) | copy-start | bytes 14155780
  0.7 11.5 %copy-start.9 = (f32[768]{0:T(1024)S(1)}, f32[768]{0:T(1024)}, u32[]{:S(2)}) copy-start(f32[768]{0:T(1024)} %refs_12_.3) | copy-start | bytes 9220
  0.7 11.5 %copy-start.2 = (bf16[768,768]{1,0:T(8,128)(2,1)S(1)}, bf16[768,768]{1,0:T(8,128)(2,1)}, u32[]{:S(2)}) copy-start(bf16[768,768]{1,0:T(8,128)(2,1)} %refs_11_.3) | copy-start | bytes 3538948
  0.7 11.5 %copy-start.15 = (f32[768]{0:T(1024)S(1)}, f32[768]{0:T(1024)}, u32[]{:S(2)}) copy-start(f32[768]{0:T(1024)} %refs_11_.2) | copy-start | bytes 9220
  0.7 11.5 %copy-start.14 = (f32[768]{0:T(1024)S(1)}, f32[768]{0:T(1024)}, u32[]{:S(2)}) copy-start(f32[768]{0:T(1024)} %refs_9_.2) | copy-start | bytes 9220
  0.7 11.5 %copy-start.11 = (f32[2304]{0:T(1024)S(1)}, f32[2304]{0:T(1024)}, u32[]{:S(2)}) copy-start(f32[2304]{0:T(1024)} %refs_8_.2) | copy-start | bytes 27652
  0.7 11.5 %copy-start.13 = (f32[768]{0:T(1024)S(1)}, f32[768]{0:T(1024)}, u32[]{:S(2)}) copy-start(f32[768]{0:T(1024)} %refs_7_.1) | copy-start | bytes 9220
  0.7 11.5 %copy-start.12 = (s32[3,208]{1,0:T(4,128)S(1)}, s32[3,208]{1,0:T(4,128)}, u32[]{:S(2)}) copy-start(s32[3,208]{1,0:T(4,128)} %refs_4_.1) | copy-start | bytes 7492
  2.2 8.0 %collective-permute-start.3 = (bf16[52,768]{1,0:T(8,128)(2,1)S(1)}, bf16[52,768]{1,0:T(8,128)(2,1)S(1)}, u32[]{:S(2)}, u32[]{:S(2)}) collective-permute-start(bf16[52,768]{1,0:T(8,128)(2,1)S(1)} %get-tuple-element.50), channel_id=1, source_target_pairs={{0,24},{8,16},{16,8},{24,0},{1,25},{9,17},{17,9},{25,1},{2,26},{10... | collective-permute-start | bytes 239624 | tf_op jit(solution)/shard_map/ppermute | solution.py:415
  6.1 5.5 %collective-permute-start.4 = (bf16[52,768]{1,0:T(8,128)(2,1)S(1)}, bf16[52,768]{1,0:T(8,128)(2,1)S(1)}, u32[]{:S(2)}, u32[]{:S(2)}) collective-permute-start(bf16[52,768]{1,0:T(8,128)(2,1)S(1)} %get-tuple-element.51), channel_id=1, source_target_pairs={{0,16},{8,24},{16,0},{24,8},{1,17},{9,25},{17,1},{25,9},{2,18},{10... | collective-permute-start | bytes 239624 | tf_op jit(solution)/shard_map/ppermute | solution.py:415
  6.6 5.5 %collective-permute-start.5 = (bf16[52,768]{1,0:T(8,128)(2,1)S(1)}, bf16[52,768]{1,0:T(8,128)(2,1)S(1)}, u32[]{:S(2)}, u32[]{:S(2)}) collective-permute-start(bf16[52,768]{1,0:T(8,128)(2,1)S(1)} %get-tuple-element.52), channel_id=1, source_target_pairs={{0,8},{8,0},{16,24},{24,16},{1,9},{9,1},{17,25},{25,17},{2,10},{10... | collective-permute-start | bytes 239624 | tf_op jit(solution)/shard_map/ppermute | solution.py:415
  6.8 9.4 %collective-permute-start = (bf16[52,768]{1,0:T(8,128)(2,1)S(1)}, bf16[52,768]{1,0:T(8,128)(2,1)S(1)}, u32[]{:S(2)}, u32[]{:S(2)}) collective-permute-start(bf16[52,768]{1,0:T(8,128)(2,1)S(1)} %get-tuple-element.46), channel_id=1, source_target_pairs={{0,24},{8,16},{16,8},{24,0},{1,25},{9,17},{17,9},{25,1},{2,26},{10... | collective-permute-start | bytes 239624 | tf_op jit(solution)/shard_map/ppermute | solution.py:416
  9.6 6.6 %collective-permute-start.1 = (bf16[52,768]{1,0:T(8,128)(2,1)S(1)}, bf16[52,768]{1,0:T(8,128)(2,1)S(1)}, u32[]{:S(2)}, u32[]{:S(2)}) collective-permute-start(bf16[52,768]{1,0:T(8,128)(2,1)S(1)} %get-tuple-element.47), channel_id=1, source_target_pairs={{0,16},{8,24},{16,0},{24,8},{1,17},{9,25},{17,1},{25,9},{2,18},{10... | collective-permute-start | bytes 239624 | tf_op jit(solution)/shard_map/ppermute | solution.py:416
  10.1 6.1 %collective-permute-start.2 = (bf16[52,768]{1,0:T(8,128)(2,1)S(1)}, bf16[52,768]{1,0:T(8,128)(2,1)S(1)}, u32[]{:S(2)}, u32[]{:S(2)}) collective-permute-start(bf16[52,768]{1,0:T(8,128)(2,1)S(1)} %get-tuple-element.48), channel_id=1, source_target_pairs={{0,8},{8,0},{16,24},{24,16},{1,9},{9,1},{17,25},{25,17},{2,10},{10... | collective-permute-start | bytes 239624 | tf_op jit(solution)/shard_map/ppermute | solution.py:416
  12.2 4.0 %copy-start.3 = (bf16[768,3072]{1,0:T(8,128)(2,1)S(1)}, bf16[768,3072]{1,0:T(8,128)(2,1)}, u32[]{:S(2)}) copy-start(bf16[768,3072]{1,0:T(8,128)(2,1)} %refs_13_.3) | copy-start | bytes 14155780
  12.2 4.0 %copy-start.10 = (f32[3072]{0:T(1024)S(1)}, f32[3072]{0:T(1024)}, u32[]{:S(2)}) copy-start(f32[3072]{0:T(1024)} %refs_14_.3) | copy-start | bytes 36868
  16.3 10.8 %copy-start.16 = (f32[768]{0:T(1024)S(1)}, f32[768]{0:T(1024)}, u32[]{:S(2)}) copy-start(f32[768]{0:T(1024)} %b_down.1) | copy-start | bytes 9220
  23.5 7.4 %collective-permute-start.8 = (bf16[56,768]{1,0:T(8,128)(2,1)S(1)}, bf16[56,768]{1,0:T(8,128)(2,1)S(1)}, u32[]{:S(2)}, u32[]{:S(2)}) collective-permute-start(bf16[56,768]{1,0:T(8,128)(2,1)S(1)} %get-tuple-element.66.refs_1_), channel_id=1, source_target_pairs={{0,24},{8,16},{16,8},{24,0},{1,25},{9,17},{17,9},{25,1},{2,26},{10... | collective-permute-start | bytes 258056 | tf_op jit(solution)/shard_map/ppermute | solution.py:477
  25.1 5.8 %collective-permute-start.7 = (bf16[56,768]{1,0:T(8,128)(2,1)S(1)}, bf16[56,768]{1,0:T(8,128)(2,1)S(1)}, u32[]{:S(2)}, u32[]{:S(2)}) collective-permute-start(bf16[56,768]{1,0:T(8,128)(2,1)S(1)} %get-tuple-element.66.refs_1_), channel_id=1, source_target_pairs={{0,16},{8,24},{16,0},{24,8},{1,17},{9,25},{17,1},{25,9},{2,18},{10... | collective-permute-start | bytes 258056 | tf_op jit(solution)/shard_map/ppermute | solution.py:477
  26.5 4.5 %collective-permute-start.6 = (bf16[56,768]{1,0:T(8,128)(2,1)S(1)}, bf16[56,768]{1,0:T(8,128)(2,1)S(1)}, u32[]{:S(2)}, u32[]{:S(2)}) collective-permute-start(bf16[56,768]{1,0:T(8,128)(2,1)S(1)} %get-tuple-element.66.refs_1_), channel_id=1, source_target_pairs={{0,8},{8,0},{16,24},{24,16},{1,9},{9,1},{17,25},{25,17},{2,10},{10... | collective-permute-start | bytes 258056 | tf_op jit(solution)/shard_map/ppermute | solution.py:477
  27.1 3.9 %copy-start.6 = (f32[1,50,768]{2,0,1:T(1,128)S(1)}, f32[1,50,768]{2,0,1:T(1,128)}, u32[]{:S(2)}) copy-start(f32[1,50,768]{2,0,1:T(1,128)} %param.36) | copy-start | bytes 460804
  31.1 1.3 %collective-permute-start.9 = (f32[56,384]{1,0:T(8,128)S(1)}, f32[56,384]{1,0:T(8,128)S(1)}, u32[]{:S(2)}, u32[]{:S(2)}) collective-permute-start(f32[56,384]{1,0:T(8,128)S(1)} %get-tuple-element.68), channel_id=1, source_target_pairs={{0,1},{1,0},{2,3},{3,2},{4,5},{5,4},{6,7},{7,6},{8,9},{9,8},{10,11... | collective-permute-start | bytes 258056 | tf_op jit(solution)/shard_map/ppermute | solution.py:486
  32.5 12.2 %copy-start.5 = (f32[50,768]{1,0:T(8,128)S(1)}, f32[50,768]{1,0:T(8,128)}, u32[]{:S(2)}) copy-start(f32[50,768]{1,0:T(8,128)} %refs_9_.3) | copy-start | bytes 460804
  32.5 12.2 %copy-start.8 = (f32[768,8]{0,1:T(8,128)S(1)}, f32[768,8]{0,1:T(8,128)}, u32[]{:S(2)}) copy-start(f32[768,8]{0,1:T(8,128)} %param.35) | copy-start | bytes 73732
  32.5 5.3 %collective-permute-start.13 = (bf16[56,384]{1,0:T(8,128)(2,1)S(1)}, bf16[56,384]{1,0:T(8,128)(2,1)S(1)}, u32[]{:S(2)}, u32[]{:S(2)}) collective-permute-start(bf16[56,384]{1,0:T(8,128)(2,1)S(1)} %add.3.after.refs_0_), channel_id=1, source_target_pairs={{0,2},{1,3},{2,0},{3,1},{4,6},{5,7},{6,4},{7,5},{8,10},{9,11},{10,... | collective-permute-start | bytes 129032 | tf_op jit(solution)/shard_map/ppermute | solution.py:492
  34.3 9.0 %collective-permute-start.10 = (bf16[104,768]{1,0:T(8,128)(2,1)S(1)}, bf16[104,768]{1,0:T(8,128)(2,1)S(1)}, u32[]{:S(2)}, u32[]{:S(2)}) collective-permute-start(bf16[104,768]{1,0:T(8,128)(2,1)S(1)} %get-tuple-element.70), channel_id=1, source_target_pairs={{0,8},{8,0},{16,24},{24,16},{1,9},{9,1},{17,25},{25,17},{2,10},{10... | collective-permute-start | bytes 479240 | tf_op jit(solution)/shard_map/ppermute | solution.py:506
  35.7 9.0 %collective-permute-start.11 = (bf16[104,768]{1,0:T(8,128)(2,1)S(1)}, bf16[104,768]{1,0:T(8,128)(2,1)S(1)}, u32[]{:S(2)}, u32[]{:S(2)}) collective-permute-start(bf16[104,768]{1,0:T(8,128)(2,1)S(1)} %get-tuple-element.71), channel_id=1, source_target_pairs={{0,16},{8,24},{16,0},{24,8},{1,17},{9,25},{17,1},{25,9},{2,18},{10... | collective-permute-start | bytes 479240 | tf_op jit(solution)/shard_map/ppermute | solution.py:506
  36.3 8.4 %collective-permute-start.12 = (bf16[104,768]{1,0:T(8,128)(2,1)S(1)}, bf16[104,768]{1,0:T(8,128)(2,1)S(1)}, u32[]{:S(2)}, u32[]{:S(2)}) collective-permute-start(bf16[104,768]{1,0:T(8,128)(2,1)S(1)} %get-tuple-element.72), channel_id=1, source_target_pairs={{0,24},{8,16},{16,8},{24,0},{1,25},{9,17},{17,9},{25,1},{2,26},{10... | collective-permute-start | bytes 479240 | tf_op jit(solution)/shard_map/ppermute | solution.py:506
  37.8 5.3 %collective-permute-start.14 = (bf16[56,384]{1,0:T(8,128)(2,1)S(1)}, bf16[56,384]{1,0:T(8,128)(2,1)S(1)}, u32[]{:S(2)}, u32[]{:S(2)}) collective-permute-start(bf16[56,384]{1,0:T(8,128)(2,1)S(1)} %add.4.refs_0_), channel_id=1, source_target_pairs={{0,4},{1,5},{2,6},{3,7},{4,0},{5,1},{6,2},{7,3},{8,12},{9,13},{10,... | collective-permute-start | bytes 129032 | tf_op jit(solution)/shard_map/ppermute | solution.py:492
  43.2 1.5 %collective-permute-start.15 = (f32[56,384]{1,0:T(8,128)S(1)}, f32[56,384]{1,0:T(8,128)S(1)}, u32[]{:S(2)}, u32[]{:S(2)}) collective-permute-start(f32[56,384]{1,0:T(8,128)S(1)} %add.5.refs_4_), channel_id=1, source_target_pairs={{0,1},{1,0},{2,3},{3,2},{4,5},{5,4},{6,7},{7,6},{8,9},{9,8},{10,11... | collective-permute-start | bytes 258056 | tf_op jit(solution)/shard_map/ppermute | solution.py:495

commit v5 on v4

--- a/solution.py
+++ b/solution.py
@@ -165,8 +165,8 @@
         slab = w_down.shape[0] // HEADS
         w_down_t[:, pl.ds(h * slab, slab)] = w_down[pl.ds(h * slab, slab), :].T
     for h in range(HEADS):
-        both = dot_tn(values[:, pl.ds(h // 2 * 2 * head, 2 * head)], p_bf[h])
-        mix_t[pl.ds(h * head, head), :] = both[h % 2 * head :][:head].astype(BF16)
+        part = pl.ds(h * head, head)
+        mix_t[part, :] = dot_tn(values[:, part], p_bf[h]).astype(BF16)
     resid[...] = x[...] + dot_tn(mix_t[...], w_out[...]) + line(b_out)
     hat, _ = normalize(resid[...])
     normed_two[...] = (hat * line(gain_two) + line(shift_two)).astype(BF16)
@@ -210,11 +210,15 @@
     )
     dres[...] = grad_resid
     dmix[...] = dot_nt(dres[...].astype(BF16), w_out[...]).astype(BF16)
-    lane = lax.broadcasted_iota(jnp.int32, (rows, 2 * head), 1) // head
+    lane = lax.broadcasted_iota(jnp.int32, (nkeys, 2 * head), 1) // head
     for h in range(HEADS):
         cols = pl.ds(h // 2 * 2 * head, 2 * head)
-        gp = dmix[:, cols]
-        dprob = dot_nt(values[:, cols], jnp.where(lane == h % 2, gp, jnp.zeros_like(gp)))
+        if h % 2 == 0:
+            vp = values[:, cols]
+            none = jnp.zeros_like(vp)
+            two = jnp.concatenate([jnp.where(lane == side, vp, none) for side in range(2)], 0)
+            dprobs = dot_nt(two, dmix[:, cols])
+        dprob = dprobs[h % 2 * nkeys :][:nkeys]
         prob = p_f[h]
         both = prob * dprob
         inner = jnp.sum(both, axis=0, keepdims=True)
@@ -285,10 +289,10 @@
             )
 
 
-def pack_kernel(seq, pack, after, *packs):
+def pack_kernel(ways, pack, after, *packs):
     me = lax.axis_index("seq")
-    for k in range(seq):
-        packs[k][...] = pack[me ^ k]
+    for k, out in zip(ways, packs):
+        out[...] = pack[me ^ k]
 
 
 def tree(values):
@@ -317,13 +321,8 @@
     out[...] = tree([part[...].astype(F32) for part in parts]).astype(out.dtype)
 
 
-def final_kernel(seq, images, total, *refs):
-    back, refs = refs[:seq], refs[seq:]
-    (
-        mine, other, combined, start_t, prompts, momentum,
-        layer_out, input_grad, basis_t, right_t, error, new_momentum, new_prompts, prompt_copy,
-        whole,
-    ) = refs
+def place_kernel(seq, images, *refs):
+    back, (after, layer_out, input_grad) = refs[:seq], refs[seq:]
     me = lax.axis_index("seq")
     chunk = layer_out.shape[1]
     full = spans(chunk)[0][1]
@@ -333,6 +332,13 @@
             for target, places in ((layer_out, (0, 2 * full)), (input_grad, (full, full + chunk))):
                 for (low, high), at in zip(spans(chunk), places):
                     target[me ^ k, pl.ds(low, high - low), :] = back[k][pl.ds(at, high - low), :]
+
+
+def final_kernel(total, *refs):
+    (
+        mine, other, combined, start_t, prompts, momentum,
+        basis_t, right_t, error, new_momentum, new_prompts, prompt_copy, done, whole,
+    ) = refs[:6] + refs[-8:]
     half = mine.shape[1]
     count, width = prompts.shape
     rank = start_t.shape[0]
@@ -360,6 +366,7 @@
     new_momentum[...] = moved
     new_prompts[...] = fresh
     prompt_copy[...] = fresh.astype(BF16)
+    done[...] = jnp.zeros_like(done)
 
 
 def flip(k, n):
@@ -485,43 +492,56 @@
     )
     parts = [keep, lax.ppermute(give, "dp", flip(1, dp))]
     bit = 2
-    first = None
+    sums = []
     while bit < dp:
         (mine,) = call(add_kernel, [((pad, half), wire)], parts, name="add")
-        first = mine if first is None else first
+        sums.append(mine)
         parts = [mine, lax.ppermute(mine, "dp", flip(bit, dp))]
         bit *= 2
     (mine,) = call(add_kernel, [((pad, half), F32)], parts, name="add")
     other = lax.ppermute(mine, "dp", flip(1, dp))
 
-    packs = call(
-        functools.partial(pack_kernel, seq),
-        [piece] * seq,
-        (chunks, first),
-        in_specs=[VMEM, ANY],
-        flops=1 << 32,
-        name="pack",
-    )
-    back = [packs[0]] + [
-        lax.ppermute(packs[k], "seq", flip(k, seq)) for k in range(1, seq)
-    ]
+    groups = ((0,1,2), (3,)) if seq == 4 and len(sums) > 1 else (tuple(range(seq)), ())
+    back = [None] * seq
+    for ways, after in zip(groups, sums):
+        packs = call(
+            functools.partial(pack_kernel, ways),
+            [piece] * len(ways),
+            (chunks, after),
+            in_specs=[VMEM, ANY],
+            name="pack",
+        )
+        for k, pack in zip(ways, packs):
+            back[k] = lax.ppermute(pack, "seq", flip(k, seq)) if k else pack
+
     rank = start_factor.shape[1]
-    layer_out, input_grad, basis_t, right_t, error, new_momentum, new_prompts, prompt_copy = call(
-        functools.partial(final_kernel, seq, images, images * dp),
+    free = pl.BlockSpec(memory_space=pltpu.VMEM)
+    early = [back[k] for k in groups[0] if k]
+    basis_t, right_t, error, new_momentum, new_prompts, prompt_copy, done = call(
+        functools.partial(final_kernel, images * dp),
         [
-            ((images, chunk, width), BF16),
-            ((images, chunk, width), BF16),
             ((rank, count), F32),
             ((rank, width), F32),
             ((count, 1, width), F32),
             ((count, width), F32),
             ((count, width), F32),
             ((count, width), BF16),
+            ((8, 128), F32),
         ],
-        (*back, mine, other, combined, start_factor.T, prompts, momentum),
+        (mine, other, combined, start_factor.T, prompts, momentum, *early),
         [pltpu.VMEM((pad, 2 * width), F32)],
-        out_specs=[pl.BlockSpec(memory_space=pltpu.VMEM) for _ in range(8)],
+        in_specs=[VMEM] * 6 + [ANY] * len(early),
+        out_specs=[free] * 6 + [VMEM],
+        flops=7 << 26,
         name="final",
+    )
+    layer_out, input_grad = call(
+        functools.partial(place_kernel, seq, images),
+        [((images, chunk, width), BF16)] * 2,
+        (*back, done),
+        in_specs=[VMEM] * seq + [ANY],
+        out_specs=[free] * 2,
+        name="place",
     )
     return (
         layer_out,

time: 47.1 us -> 46.2 us (0.981)
  waiting for transfers between devices: 6.34 us -> 5.38 us
    ppermute x2, waiting for transfers between devices: 2.65 us -> 1.28 us  [body(): parts = [mine, lax.ppermute(mine, 'dp', flip(bit, dp))]]
    ppermute x1, waiting for transfers between devices: 0.01 us -> 1.25 us  [body(): other = lax.ppermute(mine, 'dp', flip(1, dp))]
    ppermute x3, waiting for transfers between devices: 1.44 us -> 0.44 us  [body(): back[k] = lax.ppermute(pack, 'seq', flip(k, seq)) if k else pack]
    pallas_call x10 -> x12, Pallas kernels: 18.9 us -> 19.2 us  [call(): pl.pallas_call(kernel, out_shape=[held.get(id(spec), jax.ShapeDtypeStruct...]
  transfers between devices with their start and end apart: 16 -> 16, of which waited for: 6 -> 8; matrix products, arithmetic and copies ran while one was open for 0% -> 0% of each run, Pallas kernels for 17% -> 21%
where the time goes in v5:
time: 46.2 us; the launch traced here: 46.1 us
  starting transfers between devices  20.5 us (44%)
  Pallas kernels  19.2 us (42%)
  waiting for transfers between devices  5.38 us (12%)
  between operations  0.97 us (2%)
    pallas_call x12, Pallas kernels, call(): pl.pallas_call(kernel, out_shape=[held.get(id(spec), jax.ShapeDtypeStruct...  19.2 us
    ppermute x3, starting transfers between devices, body(): lax.ppermute(toks[k], 'seq', flip(k, seq))  4.6 us
    ppermute x3, starting transfers between devices, body(): lax.ppermute(cots[k], 'seq', flip(k, seq))  4.43 us
    ppermute x2, starting transfers between devices, body(): parts = [mine, lax.ppermute(mine, 'dp', flip(bit, dp))]  4.3 us
    ppermute x3, starting transfers between devices, body(): lax.ppermute(pgrad, 'seq', flip(k, seq))  3.55 us
    ppermute x3, starting transfers between devices, body(): back[k] = lax.ppermute(pack, 'seq', flip(k, seq)) if k else pack  3.45 us
    ppermute x2, waiting for transfers between devices, body(): parts = [mine, lax.ppermute(mine, 'dp', flip(bit, dp))]  1.28 us
    ppermute x1, waiting for transfers between devices, body(): parts = [keep, lax.ppermute(give, 'dp', flip(1, dp))]  1.27 us
  transfers between devices with their start and end apart: 16, of which 8 were waited for; matrix products, arithmetic and copies ran while one was open for 0% of the time, Pallas kernels for 21%

profile of v5, /device:TPU:0, one launch (start us, length us, event | category | flops | bytes accessed | tf_op | source)
XLA Modules:
  0.0 46.1 jit_solution(13031924118059972612)
XLA Ops:
  0.6 0.0 copy-start
  0.6 0.0 copy-start.6
  0.7 0.0 copy-start.4
  0.7 0.0 copy-start.1
  0.7 0.0 copy-start.7
  0.7 0.0 copy-start.2
  0.7 1.4 %pick.1 = (bf16[52,768]{1,0:T(8,128)(2,1)S(1)}, bf16[52,768]{1,0:T(8,128)(2,1)S(1)}, bf16[52,768]{1,0:T(8,128)(2,1)S(1)}, bf16[52,768]{1,0:T(8,128)(2,1)S(1)}, b...) custom-call(bf16[3,52,768]{2,1,0:T(8,128)(2,1)} %tok.1, ...), custom_call_target="tpu_custom_call" | custom-call | flops 17179869184 | bytes 479232 | tf_op jit(solution)/shard_map/pick/pallas_call | solution.py:66
  2.2 4.0 %collective-permute-start.3 = (bf16[52,768]{1,0:T(8,128)(2,1)S(1)}, bf16[52,768]{1,0:T(8,128)(2,1)S(1)}, u32[]{:S(2)}, u32[]{:S(2)}) collective-permute-start(bf16[52,768]{1,0:T(8,128)(2,1)S(1)} %get-tuple-element.50), channel_id=1, source_target_pairs={{0,24},{8,16},{16,8},{24,0},{1,25},{9,17},{17,9},{25,1},{2,26},{10... | collective-permute-start | bytes 239624 | tf_op jit(solution)/shard_map/ppermute | solution.py:422
  6.1 0.5 %collective-permute-start.4 = (bf16[52,768]{1,0:T(8,128)(2,1)S(1)}, bf16[52,768]{1,0:T(8,128)(2,1)S(1)}, u32[]{:S(2)}, u32[]{:S(2)}) collective-permute-start(bf16[52,768]{1,0:T(8,128)(2,1)S(1)} %get-tuple-element.51), channel_id=1, source_target_pairs={{0,16},{8,24},{16,0},{24,8},{1,17},{9,25},{17,1},{25,9},{2,18},{10... | collective-permute-start | bytes 239624 | tf_op jit(solution)/shard_map/ppermute | solution.py:422
  6.6 0.1 collective-permute-start.5
  6.8 2.8 %collective-permute-start = (bf16[52,768]{1,0:T(8,128)(2,1)S(1)}, bf16[52,768]{1,0:T(8,128)(2,1)S(1)}, u32[]{:S(2)}, u32[]{:S(2)}) collective-permute-start(bf16[52,768]{1,0:T(8,128)(2,1)S(1)} %get-tuple-element.46), channel_id=1, source_target_pairs={{0,24},{8,16},{16,8},{24,0},{1,25},{9,17},{17,9},{25,1},{2,26},{10... | collective-permute-start | bytes 239624 | tf_op jit(solution)/shard_map/ppermute | solution.py:423
  9.6 0.5 %collective-permute-start.1 = (bf16[52,768]{1,0:T(8,128)(2,1)S(1)}, bf16[52,768]{1,0:T(8,128)(2,1)S(1)}, u32[]{:S(2)}, u32[]{:S(2)}) collective-permute-start(bf16[52,768]{1,0:T(8,128)(2,1)S(1)} %get-tuple-element.47), channel_id=1, source_target_pairs={{0,16},{8,24},{16,0},{24,8},{1,17},{9,25},{17,1},{25,9},{2,18},{10... | collective-permute-start | bytes 239624 | tf_op jit(solution)/shard_map/ppermute | solution.py:423
  10.1 0.0 collective-permute-done.3.refs_1_
  10.1 1.1 %collective-permute-start.2 = (bf16[52,768]{1,0:T(8,128)(2,1)S(1)}, bf16[52,768]{1,0:T(8,128)(2,1)S(1)}, u32[]{:S(2)}, u32[]{:S(2)}) collective-permute-start(bf16[52,768]{1,0:T(8,128)(2,1)S(1)} %get-tuple-element.48), channel_id=1, source_target_pairs={{0,8},{8,0},{16,24},{24,16},{1,9},{9,1},{17,25},{25,17},{2,10},{10... | collective-permute-start | bytes 239624 | tf_op jit(solution)/shard_map/ppermute | solution.py:423
  11.2 0.4 collective-permute-done.4.refs_2_
  11.6 0.5 %collective-permute-done.5.refs_3_ = bf16[52,768]{1,0:T(8,128)(2,1)S(1)} collective-permute-done((bf16[52,768]{1,0:T(8,128)(2,1)S(1)}, bf16[52,768]{1,0:T(8,128)(2,1)S(1)}, u32[]{:S(2)}, u32[]{:S(2)}) %collective-permute-start.5) | collective-permute-done | bytes 79904 | tf_op jit(solution)/shard_map/ppermute | solution.py:422
  12.2 0.0 copy-start.3
  12.2 0.0 copy-start.8
  12.2 3.9 %forward.1 = (bf16[208,768]{1,0:T(8,128)(2,1)S(1)}, bf16[208,768]{1,0:T(8,128)(2,1)S(1)}, bf16[272,768]{1,0:T(8,128)(2,1)S(1)}, bf16[272,768]{1,0:T(8,128)(2,1)S...) custom-call(bf16[52,768]{1,0:T(8,128)(2,1)S(1)} %get-tuple-element.4, ...), custom_call_target="tpu_custom_call" | custom-call | flops 1155268608 | bytes 9937344 | tf_op jit(solution)/shard_map/forward/pallas_call | solution.py:66
  16.1 0.0 collective-permute-done.refs_1_
  16.2 0.0 collective-permute-done.1.refs_2_
  16.2 0.0 collective-permute-done.2.refs_3_
  16.2 0.0 copy-start.14
  16.2 7.1 %backward.1 = (bf16[56,768]{1,0:T(8,128)(2,1)S(1)}, bf16[208,3072]{1,0:T(8,128)(2,1)S(1)}, f32[208,768]{1,0:T(8,128)S(1)}, bf16[12,272,208]{2,1,0:T(8,128)(2,1)S(1)}, bf16[208,768]{1,0:T(8,128)(2,1)S(1)}) custom-call(bf16[52,768]{1,0:T(8,128)(2,1)S(1)} %get-tuple-element.45.refs_0_, bf16[52,768]{1,0:T(8,128)(2,1)S(1)} %collective-permute-done.refs_1_, ...), custom_call_target="tpu_custom_call" | custom-call | flops 3680501760 | bytes 20416512 | tf_op jit(solution)/shard_map/backward/pallas_call | solution.py:66
  23.3 1.5 %collective-permute-start.8 = (bf16[56,768]{1,0:T(8,128)(2,1)S(1)}, bf16[56,768]{1,0:T(8,128)(2,1)S(1)}, u32[]{:S(2)}, u32[]{:S(2)}) collective-permute-start(bf16[56,768]{1,0:T(8,128)(2,1)S(1)} %get-tuple-element.66.refs_1_), channel_id=1, source_target_pairs={{0,24},{8,16},{16,8},{24,0},{1,25},{9,17},{17,9},{25,1},{2,26},{10... | collective-permute-start | bytes 258056 | tf_op jit(solution)/shard_map/ppermute | solution.py:484
  24.8 1.4 %collective-permute-start.7 = (bf16[56,768]{1,0:T(8,128)(2,1)S(1)}, bf16[56,768]{1,0:T(8,128)(2,1)S(1)}, u32[]{:S(2)}, u32[]{:S(2)}) collective-permute-start(bf16[56,768]{1,0:T(8,128)(2,1)S(1)} %get-tuple-element.66.refs_1_), channel_id=1, source_target_pairs={{0,16},{8,24},{16,0},{24,8},{1,17},{9,25},{17,1},{25,9},{2,18},{10... | collective-permute-start | bytes 258056 | tf_op jit(solution)/shard_map/ppermute | solution.py:484
  26.2 0.6 %collective-permute-start.6 = (bf16[56,768]{1,0:T(8,128)(2,1)S(1)}, bf16[56,768]{1,0:T(8,128)(2,1)S(1)}, u32[]{:S(2)}, u32[]{:S(2)}) collective-permute-start(bf16[56,768]{1,0:T(8,128)(2,1)S(1)} %get-tuple-element.66.refs_1_), channel_id=1, source_target_pairs={{0,8},{8,0},{16,24},{24,16},{1,9},{9,1},{17,25},{25,17},{2,10},{10... | collective-permute-start | bytes 258056 | tf_op jit(solution)/shard_map/ppermute | solution.py:484
  26.8 3.6 %rest.1.refs_5_.pack = bf16[4,104,768]{2,1,0:T(8,128)(2,1)S(1)} custom-call(bf16[208,3072]{1,0:T(8,128)(2,1)S(1)} %get-tuple-element.60.act, f32[208,768]{1,0:T(8,128)S(1)} %get-tuple-element.57.refs_8_.resid, f32[208,768]{1,0:T(8,128)S(1)} %get-tuple-element.61.dres, bf16[12,272,208]{2,1,0:T(8,128)(2,1)S(1)} %get-tuple-element.56.refs_7_.p_bf, ...), custom_call_target="tpu_custom_call" | custom-call | flops 1717567488 | bytes 14911488 | tf_op jit(solution)/shard_map/rest/pallas_call | solution.py:66
  30.5 0.0 collective-permute-done.8.refs_4_
  30.5 0.0 collective-permute-done.7.refs_3_
  30.5 0.2 collective-permute-done.6.refs_2_
  30.7 0.1 combine.1
  30.9 0.1 collective-permute-start.9
  30.9 1.3 %collective-permute-done.9.refs_1_ = f32[56,384]{1,0:T(8,128)S(1)} collective-permute-done((f32[56,384]{1,0:T(8,128)S(1)}, f32[56,384]{1,0:T(8,128)S(1)}, u32[]{:S(2)}, u32[]{:S(2)}) %collective-permute-start.9) | collective-permute-done | bytes 86048 | tf_op jit(solution)/shard_map/ppermute | solution.py:493
  32.2 1.6 %collective-permute-start.12 = (bf16[56,384]{1,0:T(8,128)(2,1)S(1)}, bf16[56,384]{1,0:T(8,128)(2,1)S(1)}, u32[]{:S(2)}, u32[]{:S(2)}) collective-permute-start(bf16[56,384]{1,0:T(8,128)(2,1)S(1)} %add.3.after.refs_0_), channel_id=1, source_target_pairs={{0,2},{1,3},{2,0},{3,1},{4,6},{5,7},{6,4},{7,5},{8,10},{9,11},{10,... | collective-permute-start | bytes 129032 | tf_op jit(solution)/shard_map/ppermute | solution.py:499
  33.9 1.3 %collective-permute-start.10 = (bf16[104,768]{1,0:T(8,128)(2,1)S(1)}, bf16[104,768]{1,0:T(8,128)(2,1)S(1)}, u32[]{:S(2)}, u32[]{:S(2)}) collective-permute-start(bf16[104,768]{1,0:T(8,128)(2,1)S(1)} %get-tuple-element.70), channel_id=1, source_target_pairs={{0,8},{8,0},{16,24},{24,16},{1,9},{9,1},{17,25},{25,17},{2,10},{10... | collective-permute-start | bytes 479240 | tf_op jit(solution)/shard_map/ppermute | solution.py:515
  35.2 0.7 %collective-permute-start.11 = (bf16[104,768]{1,0:T(8,128)(2,1)S(1)}, bf16[104,768]{1,0:T(8,128)(2,1)S(1)}, u32[]{:S(2)}, u32[]{:S(2)}) collective-permute-start(bf16[104,768]{1,0:T(8,128)(2,1)S(1)} %get-tuple-element.71), channel_id=1, source_target_pairs={{0,16},{8,24},{16,0},{24,8},{1,17},{9,25},{17,1},{25,9},{2,18},{10... | collective-permute-start | bytes 479240 | tf_op jit(solution)/shard_map/ppermute | solution.py:515
  35.9 0.4 collective-permute-done.12.refs_1_
  36.3 2.7 %collective-permute-start.14 = (bf16[56,384]{1,0:T(8,128)(2,1)S(1)}, bf16[56,384]{1,0:T(8,128)(2,1)S(1)}, u32[]{:S(2)}, u32[]{:S(2)}) collective-permute-start(bf16[56,384]{1,0:T(8,128)(2,1)S(1)} %add.4.after.refs_0_), channel_id=1, source_target_pairs={{0,4},{1,5},{2,6},{3,7},{4,0},{5,1},{6,2},{7,3},{8,12},{9,13},{10,... | collective-permute-start | bytes 129032 | tf_op jit(solution)/shard_map/ppermute | solution.py:499
  39.0 1.4 %collective-permute-start.13 = (bf16[104,768]{1,0:T(8,128)(2,1)S(1)}, bf16[104,768]{1,0:T(8,128)(2,1)S(1)}, u32[]{:S(2)}, u32[]{:S(2)}) collective-permute-start(bf16[104,768]{1,0:T(8,128)(2,1)S(1)} %pack.3), channel_id=1, source_target_pairs={{0,24},{8,16},{16,8},{24,0},{1,25},{9,17},{17,9},{25,1},{2,26},{10... | collective-permute-start | bytes 479240 | tf_op jit(solution)/shard_map/ppermute | solution.py:515
  40.4 0.9 %collective-permute-done.14.refs_1_ = bf16[56,384]{1,0:T(8,128)(2,1)S(1)} collective-permute-done((bf16[56,384]{1,0:T(8,128)(2,1)S(1)}, bf16[56,384]{1,0:T(8,128)(2,1)S(1)}, u32[]{:S(2)}, u32[]{:S(2)}) %collective-permute-start.14) | collective-permute-done | bytes 43040 | tf_op jit(solution)/shard_map/ppermute | solution.py:499
  41.3 0.1 collective-permute-start.15
  41.4 0.0 collective-permute-done.10.refs_6_.refs_1_
  41.4 0.0 collective-permute-done.11.refs_7_.refs_2_
  41.4 1.2 %collective-permute-done.15.refs_1_ = f32[56,384]{1,0:T(8,128)S(1)} collective-permute-done((f32[56,384]{1,0:T(8,128)S(1)}, f32[56,384]{1,0:T(8,128)S(1)}, u32[]{:S(2)}, u32[]{:S(2)}) %collective-permute-start.15) | collective-permute-done | bytes 86048 | tf_op jit(solution)/shard_map/ppermute | solution.py:502
  42.7 2.1 %final.1 = (f32[8,50]{1,0:T(8,128)}, f32[8,768]{1,0:T(8,128)}, f32[50,1,768]{2,1,0:T(1,128)}, f32[50,768]{1,0:T(8,128)}, f32[50,768]{1,0:T(8,128)}, /*index=5*/bf16[50,768]{1,0:T(8,128)(2,1)}, f32[8,128]{1,0:T(8,128)S(1)}) custom-call(f32[56,384]{1,0:T(8,128)S(1)} %add.5.refs_0_, f32[56,384]{1,0:T(8,128)S(1)} %collective-permute-done.15.refs_1_, ...), custom_call_target="tpu_custom_call" | custom-call | flops 469762048 | bytes 995328 | tf_op jit(solution)/shard_map/final/pallas_call | solution.py:66
  44.8 0.4 collective-permute-done.13.refs_3_
  45.2 0.8 %place.1 = (bf16[3,52,768]{2,1,0:T(8,128)(2,1)}, bf16[3,52,768]{2,1,0:T(8,128)(2,1)}) custom-call(bf16[104,768]{1,0:T(8,128)(2,1)S(1)} %get-tuple-element.69.refs_0_, bf16[104,768]{1,0:T(8,128)(2,1)S(1)} %collective-permute-done.10.refs_6_.refs_1_, bf16[104,768]{1,0:T(8,128)(2,1)S(1)} %collective-permute-done.11.refs_7_.refs_2_, ...), custom_call_target="tpu_custom_call" | custom-call | bytes 643072 | tf_op jit(solution)/shard_map/place/pallas_call | solution.py:66
  (30 shorter events, 0.1 us)
Async XLA Ops:
  0.6 11.5 %copy-start = (bf16[768,2304]{1,0:T(8,128)(2,1)S(1)}, bf16[768,2304]{1,0:T(8,128)(2,1)}, u32[]{:S(2)}) copy-start(bf16[768,2304]{1,0:T(8,128)(2,1)} %w_qkv.1) | copy-start | bytes 10616836
  0.6 11.5 %copy-start.6 = (f32[768]{0:T(1024)S(1)}, f32[768]{0:T(1024)}, u32[]{:S(2)}) copy-start(f32[768]{0:T(1024)} %gain.1) | copy-start | bytes 9220
  0.7 11.5 %copy-start.4 = (f32[50,768]{1,0:T(8,128)S(1)}, f32[50,768]{1,0:T(8,128)}, u32[]{:S(2)}) copy-start(f32[50,768]{1,0:T(8,128)} %refs_4_.3) | copy-start | bytes 460804
  0.7 11.5 %copy-start.1 = (bf16[3072,768]{1,0:T(8,128)(2,1)S(1)}, bf16[3072,768]{1,0:T(8,128)(2,1)}, u32[]{:S(2)}) copy-start(bf16[3072,768]{1,0:T(8,128)(2,1)} %w_down.1) | copy-start | bytes 14155780
  0.7 11.5 %copy-start.7 = (f32[768]{0:T(1024)S(1)}, f32[768]{0:T(1024)}, u32[]{:S(2)}) copy-start(f32[768]{0:T(1024)} %refs_12_.3) | copy-start | bytes 9220
  0.7 11.5 %copy-start.2 = (bf16[768,768]{1,0:T(8,128)(2,1)S(1)}, bf16[768,768]{1,0:T(8,128)(2,1)}, u32[]{:S(2)}) copy-start(bf16[768,768]{1,0:T(8,128)(2,1)} %refs_11_.3) | copy-start | bytes 3538948
  0.7 11.5 %copy-start.13 = (f32[768]{0:T(1024)S(1)}, f32[768]{0:T(1024)}, u32[]{:S(2)}) copy-start(f32[768]{0:T(1024)} %refs_11_.2) | copy-start | bytes 9220
  0.7 11.5 %copy-start.12 = (f32[768]{0:T(1024)S(1)}, f32[768]{0:T(1024)}, u32[]{:S(2)}) copy-start(f32[768]{0:T(1024)} %refs_9_.1) | copy-start | bytes 9220
  0.7 11.5 %copy-start.9 = (f32[2304]{0:T(1024)S(1)}, f32[2304]{0:T(1024)}, u32[]{:S(2)}) copy-start(f32[2304]{0:T(1024)} %refs_8_.1) | copy-start | bytes 27652
  0.7 11.5 %copy-start.11 = (f32[768]{0:T(1024)S(1)}, f32[768]{0:T(1024)}, u32[]{:S(2)}) copy-start(f32[768]{0:T(1024)} %refs_7_.1) | copy-start | bytes 9220
  0.7 11.5 %copy-start.10 = (s32[3,208]{1,0:T(4,128)S(1)}, s32[3,208]{1,0:T(4,128)}, u32[]{:S(2)}) copy-start(s32[3,208]{1,0:T(4,128)} %refs_4_.2) | copy-start | bytes 7492
  2.2 8.0 %collective-permute-start.3 = (bf16[52,768]{1,0:T(8,128)(2,1)S(1)}, bf16[52,768]{1,0:T(8,128)(2,1)S(1)}, u32[]{:S(2)}, u32[]{:S(2)}) collective-permute-start(bf16[52,768]{1,0:T(8,128)(2,1)S(1)} %get-tuple-element.50), channel_id=1, source_target_pairs={{0,24},{8,16},{16,8},{24,0},{1,25},{9,17},{17,9},{25,1},{2,26},{10... | collective-permute-start | bytes 239624 | tf_op jit(solution)/shard_map/ppermute | solution.py:422
  6.1 5.5 %collective-permute-start.4 = (bf16[52,768]{1,0:T(8,128)(2,1)S(1)}, bf16[52,768]{1,0:T(8,128)(2,1)S(1)}, u32[]{:S(2)}, u32[]{:S(2)}) collective-permute-start(bf16[52,768]{1,0:T(8,128)(2,1)S(1)} %get-tuple-element.51), channel_id=1, source_target_pairs={{0,16},{8,24},{16,0},{24,8},{1,17},{9,25},{17,1},{25,9},{2,18},{10... | collective-permute-start | bytes 239624 | tf_op jit(solution)/shard_map/ppermute | solution.py:422
  6.6 5.5 %collective-permute-start.5 = (bf16[52,768]{1,0:T(8,128)(2,1)S(1)}, bf16[52,768]{1,0:T(8,128)(2,1)S(1)}, u32[]{:S(2)}, u32[]{:S(2)}) collective-permute-start(bf16[52,768]{1,0:T(8,128)(2,1)S(1)} %get-tuple-element.52), channel_id=1, source_target_pairs={{0,8},{8,0},{16,24},{24,16},{1,9},{9,1},{17,25},{25,17},{2,10},{10... | collective-permute-start | bytes 239624 | tf_op jit(solution)/shard_map/ppermute | solution.py:422
  6.8 9.4 %collective-permute-start = (bf16[52,768]{1,0:T(8,128)(2,1)S(1)}, bf16[52,768]{1,0:T(8,128)(2,1)S(1)}, u32[]{:S(2)}, u32[]{:S(2)}) collective-permute-start(bf16[52,768]{1,0:T(8,128)(2,1)S(1)} %get-tuple-element.46), channel_id=1, source_target_pairs={{0,24},{8,16},{16,8},{24,0},{1,25},{9,17},{17,9},{25,1},{2,26},{10... | collective-permute-start | bytes 239624 | tf_op jit(solution)/shard_map/ppermute | solution.py:423
  9.6 6.5 %collective-permute-start.1 = (bf16[52,768]{1,0:T(8,128)(2,1)S(1)}, bf16[52,768]{1,0:T(8,128)(2,1)S(1)}, u32[]{:S(2)}, u32[]{:S(2)}) collective-permute-start(bf16[52,768]{1,0:T(8,128)(2,1)S(1)} %get-tuple-element.47), channel_id=1, source_target_pairs={{0,16},{8,24},{16,0},{24,8},{1,17},{9,25},{17,1},{25,9},{2,18},{10... | collective-permute-start | bytes 239624 | tf_op jit(solution)/shard_map/ppermute | solution.py:423
  10.1 6.0 %collective-permute-start.2 = (bf16[52,768]{1,0:T(8,128)(2,1)S(1)}, bf16[52,768]{1,0:T(8,128)(2,1)S(1)}, u32[]{:S(2)}, u32[]{:S(2)}) collective-permute-start(bf16[52,768]{1,0:T(8,128)(2,1)S(1)} %get-tuple-element.48), channel_id=1, source_target_pairs={{0,8},{8,0},{16,24},{24,16},{1,9},{9,1},{17,25},{25,17},{2,10},{10... | collective-permute-start | bytes 239624 | tf_op jit(solution)/shard_map/ppermute | solution.py:423
  12.2 4.0 %copy-start.3 = (bf16[768,3072]{1,0:T(8,128)(2,1)S(1)}, bf16[768,3072]{1,0:T(8,128)(2,1)}, u32[]{:S(2)}) copy-start(bf16[768,3072]{1,0:T(8,128)(2,1)} %refs_13_.3) | copy-start | bytes 14155780
  12.2 4.0 %copy-start.8 = (f32[3072]{0:T(1024)S(1)}, f32[3072]{0:T(1024)}, u32[]{:S(2)}) copy-start(f32[3072]{0:T(1024)} %refs_14_.3) | copy-start | bytes 36868
  16.2 10.6 %copy-start.14 = (f32[768]{0:T(1024)S(1)}, f32[768]{0:T(1024)}, u32[]{:S(2)}) copy-start(f32[768]{0:T(1024)} %b_down.1) | copy-start | bytes 9220
  23.3 7.2 %collective-permute-start.8 = (bf16[56,768]{1,0:T(8,128)(2,1)S(1)}, bf16[56,768]{1,0:T(8,128)(2,1)S(1)}, u32[]{:S(2)}, u32[]{:S(2)}) collective-permute-start(bf16[56,768]{1,0:T(8,128)(2,1)S(1)} %get-tuple-element.66.refs_1_), channel_id=1, source_target_pairs={{0,24},{8,16},{16,8},{24,0},{1,25},{9,17},{17,9},{25,1},{2,26},{10... | collective-permute-start | bytes 258056 | tf_op jit(solution)/shard_map/ppermute | solution.py:484
  24.8 5.7 %collective-permute-start.7 = (bf16[56,768]{1,0:T(8,128)(2,1)S(1)}, bf16[56,768]{1,0:T(8,128)(2,1)S(1)}, u32[]{:S(2)}, u32[]{:S(2)}) collective-permute-start(bf16[56,768]{1,0:T(8,128)(2,1)S(1)} %get-tuple-element.66.refs_1_), channel_id=1, source_target_pairs={{0,16},{8,24},{16,0},{24,8},{1,17},{9,25},{17,1},{25,9},{2,18},{10... | collective-permute-start | bytes 258056 | tf_op jit(solution)/shard_map/ppermute | solution.py:484
  26.2 4.5 %collective-permute-start.6 = (bf16[56,768]{1,0:T(8,128)(2,1)S(1)}, bf16[56,768]{1,0:T(8,128)(2,1)S(1)}, u32[]{:S(2)}, u32[]{:S(2)}) collective-permute-start(bf16[56,768]{1,0:T(8,128)(2,1)S(1)} %get-tuple-element.66.refs_1_), channel_id=1, source_target_pairs={{0,8},{8,0},{16,24},{24,16},{1,9},{9,1},{17,25},{25,17},{2,10},{10... | collective-permute-start | bytes 258056 | tf_op jit(solution)/shard_map/ppermute | solution.py:484
  26.8 3.9 %copy-start.5 = (f32[1,50,768]{2,0,1:T(1,128)S(1)}, f32[1,50,768]{2,0,1:T(1,128)}, u32[]{:S(2)}) copy-start(f32[1,50,768]{2,0,1:T(1,128)} %param.36) | copy-start | bytes 460804
  26.8 15.8 %copy-start.15 = (f32[50,768]{1,0:T(8,128)S(1)}, f32[50,768]{1,0:T(8,128)}, u32[]{:S(2)}) copy-start(f32[50,768]{1,0:T(8,128)} %refs_5_.3) | copy-start | bytes 460804
  26.8 15.8 %copy-start.16 = (f32[768,8]{0,1:T(8,128)S(1)}, f32[768,8]{0,1:T(8,128)}, u32[]{:S(2)}) copy-start(f32[768,8]{0,1:T(8,128)} %param.35) | copy-start | bytes 73732
  30.9 1.3 %collective-permute-start.9 = (f32[56,384]{1,0:T(8,128)S(1)}, f32[56,384]{1,0:T(8,128)S(1)}, u32[]{:S(2)}, u32[]{:S(2)}) collective-permute-start(f32[56,384]{1,0:T(8,128)S(1)} %get-tuple-element.68), channel_id=1, source_target_pairs={{0,1},{1,0},{2,3},{3,2},{4,5},{5,4},{6,7},{7,6},{8,9},{9,8},{10,11... | collective-permute-start | bytes 258056 | tf_op jit(solution)/shard_map/ppermute | solution.py:493
  32.2 4.1 %collective-permute-start.12 = (bf16[56,384]{1,0:T(8,128)(2,1)S(1)}, bf16[56,384]{1,0:T(8,128)(2,1)S(1)}, u32[]{:S(2)}, u32[]{:S(2)}) collective-permute-start(bf16[56,384]{1,0:T(8,128)(2,1)S(1)} %add.3.after.refs_0_), channel_id=1, source_target_pairs={{0,2},{1,3},{2,0},{3,1},{4,6},{5,7},{6,4},{7,5},{8,10},{9,11},{10,... | collective-permute-start | bytes 129032 | tf_op jit(solution)/shard_map/ppermute | solution.py:499
  33.9 7.5 %collective-permute-start.10 = (bf16[104,768]{1,0:T(8,128)(2,1)S(1)}, bf16[104,768]{1,0:T(8,128)(2,1)S(1)}, u32[]{:S(2)}, u32[]{:S(2)}) collective-permute-start(bf16[104,768]{1,0:T(8,128)(2,1)S(1)} %get-tuple-element.70), channel_id=1, source_target_pairs={{0,8},{8,0},{16,24},{24,16},{1,9},{9,1},{17,25},{25,17},{2,10},{10... | collective-permute-start | bytes 479240 | tf_op jit(solution)/shard_map/ppermute | solution.py:515
  35.2 6.2 %collective-permute-start.11 = (bf16[104,768]{1,0:T(8,128)(2,1)S(1)}, bf16[104,768]{1,0:T(8,128)(2,1)S(1)}, u32[]{:S(2)}, u32[]{:S(2)}) collective-permute-start(bf16[104,768]{1,0:T(8,128)(2,1)S(1)} %get-tuple-element.71), channel_id=1, source_target_pairs={{0,16},{8,24},{16,0},{24,8},{1,17},{9,25},{17,1},{25,9},{2,18},{10... | collective-permute-start | bytes 479240 | tf_op jit(solution)/shard_map/ppermute | solution.py:515
  36.3 5.0 %collective-permute-start.14 = (bf16[56,384]{1,0:T(8,128)(2,1)S(1)}, bf16[56,384]{1,0:T(8,128)(2,1)S(1)}, u32[]{:S(2)}, u32[]{:S(2)}) collective-permute-start(bf16[56,384]{1,0:T(8,128)(2,1)S(1)} %add.4.after.refs_0_), channel_id=1, source_target_pairs={{0,4},{1,5},{2,6},{3,7},{4,0},{5,1},{6,2},{7,3},{8,12},{9,13},{10,... | collective-permute-start | bytes 129032 | tf_op jit(solution)/shard_map/ppermute | solution.py:499
  39.0 6.2 %collective-permute-start.13 = (bf16[104,768]{1,0:T(8,128)(2,1)S(1)}, bf16[104,768]{1,0:T(8,128)(2,1)S(1)}, u32[]{:S(2)}, u32[]{:S(2)}) collective-permute-start(bf16[104,768]{1,0:T(8,128)(2,1)S(1)} %pack.3), channel_id=1, source_target_pairs={{0,24},{8,16},{16,8},{24,0},{1,25},{9,17},{17,9},{25,1},{2,26},{10... | collective-permute-start | bytes 479240 | tf_op jit(solution)/shard_map/ppermute | solution.py:515
  41.3 1.3 %collective-permute-start.15 = (f32[56,384]{1,0:T(8,128)S(1)}, f32[56,384]{1,0:T(8,128)S(1)}, u32[]{:S(2)}, u32[]{:S(2)}) collective-permute-start(f32[56,384]{1,0:T(8,128)S(1)} %add.5.refs_0_), channel_id=1, source_target_pairs={{0,1},{1,0},{2,3},{3,2},{4,5},{5,4},{6,7},{7,6},{8,9},{9,8},{10,11... | collective-permute-start | bytes 258056 | tf_op jit(solution)/shard_map/ppermute | solution.py:502

commit v6 on v4

--- a/solution.py
+++ b/solution.py
@@ -165,8 +165,8 @@
         slab = w_down.shape[0] // HEADS
         w_down_t[:, pl.ds(h * slab, slab)] = w_down[pl.ds(h * slab, slab), :].T
     for h in range(HEADS):
-        both = dot_tn(values[:, pl.ds(h // 2 * 2 * head, 2 * head)], p_bf[h])
-        mix_t[pl.ds(h * head, head), :] = both[h % 2 * head :][:head].astype(BF16)
+        part = pl.ds(h * head, head)
+        mix_t[part, :] = dot_tn(values[:, part], p_bf[h]).astype(BF16)
     resid[...] = x[...] + dot_tn(mix_t[...], w_out[...]) + line(b_out)
     hat, _ = normalize(resid[...])
     normed_two[...] = (hat * line(gain_two) + line(shift_two)).astype(BF16)
@@ -210,11 +210,15 @@
     )
     dres[...] = grad_resid
     dmix[...] = dot_nt(dres[...].astype(BF16), w_out[...]).astype(BF16)
-    lane = lax.broadcasted_iota(jnp.int32, (rows, 2 * head), 1) // head
+    lane = lax.broadcasted_iota(jnp.int32, (nkeys, 2 * head), 1) // head
     for h in range(HEADS):
         cols = pl.ds(h // 2 * 2 * head, 2 * head)
-        gp = dmix[:, cols]
-        dprob = dot_nt(values[:, cols], jnp.where(lane == h % 2, gp, jnp.zeros_like(gp)))
+        if h % 2 == 0:
+            vp = values[:, cols]
+            none = jnp.zeros_like(vp)
+            two = jnp.concatenate([jnp.where(lane == side, vp, none) for side in range(2)], 0)
+            dprobs = dot_nt(two, dmix[:, cols])
+        dprob = dprobs[h % 2 * nkeys :][:nkeys]
         prob = p_f[h]
         both = prob * dprob
         inner = jnp.sum(both, axis=0, keepdims=True)
@@ -250,13 +254,12 @@
 
 def rest_kernel(
     seq, act, resid, dres, p_bf, ds_bf, query, dmix, keys, x_bf, w_down, w_qkv, b_down, gain,
-    pack, dqkv, q_t, wide, k_t,
+    pack, dqkv, q_t, wide,
 ):
     rows, width = query.shape
     head = width // HEADS
     chunk = rows // seq
     full = spans(chunk)[0][1]
-    k_t[...] = keys[...].T
     low = lax.broadcasted_iota(jnp.int32, (rows, 2 * head), 1) < head
     for pair in range(HEADS // 2):
         cols = pl.ds(pair * 2 * head, 2 * head)
@@ -268,7 +271,7 @@
             ).astype(BF16)
     for h in range(HEADS):
         part = pl.ds(h * head, head)
-        q_t[part, :] = dot(k_t[part, :], ds_bf[h]).astype(BF16)
+        q_t[part, :] = dot_tn(keys[:, part], ds_bf[h]).astype(BF16)
     dqkv[:, :width] = q_t[...].T
     wide[...] = resid[...] + dot(act[...], w_down[...]) + line(b_down)
     for c in range(seq):
@@ -308,8 +311,8 @@
     combined[...] = tree([part[...].astype(F32) for part in parts])
     combined[:count, :] += error[:, 0, :]
     low, high = combined[:, :half], combined[:, half:]
-    keep[...] = jnp.where(core == 0, low, high)
-    give[...] = jnp.where(core == 0, high, low)
+    keep[...] = jnp.where(core == 0, low, high).astype(keep.dtype)
+    give[...] = jnp.where(core == 0, high, low).astype(give.dtype)
 
 
 def add_kernel(*refs):
@@ -332,7 +335,9 @@
         def _():
             for target, places in ((layer_out, (0, 2 * full)), (input_grad, (full, full + chunk))):
                 for (low, high), at in zip(spans(chunk), places):
-                    target[me ^ k, pl.ds(low, high - low), :] = back[k][pl.ds(at, high - low), :]
+                    target[me ^ k, pl.ds(low, high - low), :] = back[(seq - k) % seq][
+                        pl.ds(at, high - low), :
+                    ]
     half = mine.shape[1]
     count, width = prompts.shape
     rank = start_t.shape[0]
@@ -467,7 +472,6 @@
             pltpu.VMEM((rows, 3 * width), BF16),
             pltpu.VMEM((width, rows), BF16),
             pltpu.VMEM((rows, width), F32),
-            pltpu.VMEM((width, nkeys), BF16),
         ],
         flops=2 * rows * width * (3 * width + ff),
         vmem=8 * MIB,
@@ -478,17 +482,17 @@
     half = width // 2
     combined, keep, give = call(
         combine_kernel,
-        [((pad, width), F32), ((pad, half), F32), ((pad, half), F32)],
+        [((pad, width), F32), ((pad, half), wire), ((pad, half), wire)],
         (error_rows, *parts, chunks),
         in_specs=[VMEM] * (1 + seq) + [ANY],
         name="combine",
     )
     parts = [keep, lax.ppermute(give, "dp", flip(1, dp))]
-    bit = 2
-    first = None
+    if dp > 2:
+        parts += [lax.ppermute(keep, "dp", flip(2, dp)), lax.ppermute(give, "dp", flip(3, dp))]
+    bit = 4
     while bit < dp:
         (mine,) = call(add_kernel, [((pad, half), wire)], parts, name="add")
-        first = mine if first is None else first
         parts = [mine, lax.ppermute(mine, "dp", flip(bit, dp))]
         bit *= 2
     (mine,) = call(add_kernel, [((pad, half), F32)], parts, name="add")
@@ -497,14 +501,12 @@
     packs = call(
         functools.partial(pack_kernel, seq),
         [piece] * seq,
-        (chunks, first),
+        (chunks, keep),
         in_specs=[VMEM, ANY],
-        flops=1 << 32,
         name="pack",
     )
-    back = [packs[0]] + [
-        lax.ppermute(packs[k], "seq", flip(k, seq)) for k in range(1, seq)
-    ]
+    back = [packs[0]] + [lax.ppermute(packs[k], "seq", flip(k, seq)) for k in range(seq - 1, 0, -1)]
+
     rank = start_factor.shape[1]
     layer_out, input_grad, basis_t, right_t, error, new_momentum, new_prompts, prompt_copy = call(
         functools.partial(final_kernel, seq, images, images * dp),

time: 47.1 us -> 46 us (0.977)
  waiting for transfers between devices: 6.34 us -> 4.83 us
    ppermute x1, starting transfers between devices: 0.07 us -> 1.81 us  [body(): parts = [keep, lax.ppermute(give, 'dp', flip(1, dp))]]
    ppermute x2 -> x1, starting transfers between devices: 4.38 us -> 2.69 us  [body(): parts = [mine, lax.ppermute(mine, 'dp', flip(bit, dp))]]
    ppermute x1, waiting for transfers between devices: 1.27 us -> 0.01 us  [body(): parts = [keep, lax.ppermute(give, 'dp', flip(1, dp))]]
    ppermute x2 -> x1, waiting for transfers between devices: 2.65 us -> 2.3 us  [body(): parts = [mine, lax.ppermute(mine, 'dp', flip(bit, dp))]]
    pallas_call x10 -> x9, Pallas kernels: 18.9 us -> 18.8 us  [call(): pl.pallas_call(kernel, out_shape=[held.get(id(spec), jax.ShapeDtypeStruct...]
  transfers between devices with their start and end apart: 16 -> 17, of which waited for: 6 -> 5; matrix products, arithmetic and copies ran while one was open for 0% -> 0% of each run, Pallas kernels for 17% -> 17%
where the time goes in v6:
time: 46 us; the launch traced here: 45.8 us
  starting transfers between devices  21.1 us (46%)
  Pallas kernels  18.8 us (41%)
  waiting for transfers between devices  4.83 us (10%)
  between operations  0.97 us (2%)
    pallas_call x9, Pallas kernels, call(): pl.pallas_call(kernel, out_shape=[held.get(id(spec), jax.ShapeDtypeStruct...  18.8 us
    ppermute x3, starting transfers between devices, body(): lax.ppermute(toks[k], 'seq', flip(k, seq))  4.6 us
    ppermute x3, starting transfers between devices, body(): lax.ppermute(cots[k], 'seq', flip(k, seq))  4.43 us
    ppermute x3, starting transfers between devices, body(): lax.ppermute(packs[k], 'seq', flip(k, seq))  3.55 us
    ppermute x3, starting transfers between devices, body(): lax.ppermute(pgrad, 'seq', flip(k, seq))  3.55 us
    ppermute x1, starting transfers between devices, body(): parts = [mine, lax.ppermute(mine, 'dp', flip(bit, dp))]  2.69 us
    ppermute x1, waiting for transfers between devices, body(): parts = [mine, lax.ppermute(mine, 'dp', flip(bit, dp))]  2.3 us
    ppermute x1, starting transfers between devices, body(): parts = [keep, lax.ppermute(give, 'dp', flip(1, dp))]  1.81 us
  transfers between devices with their start and end apart: 17, of which 5 were waited for; matrix products, arithmetic and copies ran while one was open for 0% of the time, Pallas kernels for 17%

profile of v6, /device:TPU:0, one launch (start us, length us, event | category | flops | bytes accessed | tf_op | source)
XLA Modules:
  0.0 45.8 jit_solution(1686432589932955483)
XLA Ops:
  0.6 0.0 copy-start
  0.7 1.4 %pick.1 = (bf16[52,768]{1,0:T(8,128)(2,1)S(1)}, bf16[52,768]{1,0:T(8,128)(2,1)S(1)}, bf16[52,768]{1,0:T(8,128)(2,1)S(1)}, bf16[52,768]{1,0:T(8,128)(2,1)S(1)}, b...) custom-call(bf16[3,52,768]{2,1,0:T(8,128)(2,1)} %tok.1, ...), custom_call_target="tpu_custom_call" | custom-call | flops 17179869184 | bytes 479232 | tf_op jit(solution)/shard_map/pick/pallas_call | solution.py:66
  2.2 4.0 %collective-permute-start.3 = (bf16[52,768]{1,0:T(8,128)(2,1)S(1)}, bf16[52,768]{1,0:T(8,128)(2,1)S(1)}, u32[]{:S(2)}, u32[]{:S(2)}) collective-permute-start(bf16[52,768]{1,0:T(8,128)(2,1)S(1)} %get-tuple-element.50), channel_id=1, source_target_pairs={{0,24},{8,16},{16,8},{24,0},{1,25},{9,17},{17,9},{25,1},{2,26},{10... | collective-permute-start | bytes 239624 | tf_op jit(solution)/shard_map/ppermute | solution.py:420
  6.1 0.5 %collective-permute-start.4 = (bf16[52,768]{1,0:T(8,128)(2,1)S(1)}, bf16[52,768]{1,0:T(8,128)(2,1)S(1)}, u32[]{:S(2)}, u32[]{:S(2)}) collective-permute-start(bf16[52,768]{1,0:T(8,128)(2,1)S(1)} %get-tuple-element.51), channel_id=1, source_target_pairs={{0,16},{8,24},{16,0},{24,8},{1,17},{9,25},{17,1},{25,9},{2,18},{10... | collective-permute-start | bytes 239624 | tf_op jit(solution)/shard_map/ppermute | solution.py:420
  6.6 0.1 collective-permute-start.5
  6.8 2.8 %collective-permute-start = (bf16[52,768]{1,0:T(8,128)(2,1)S(1)}, bf16[52,768]{1,0:T(8,128)(2,1)S(1)}, u32[]{:S(2)}, u32[]{:S(2)}) collective-permute-start(bf16[52,768]{1,0:T(8,128)(2,1)S(1)} %get-tuple-element.46), channel_id=1, source_target_pairs={{0,24},{8,16},{16,8},{24,0},{1,25},{9,17},{17,9},{25,1},{2,26},{10... | collective-permute-start | bytes 239624 | tf_op jit(solution)/shard_map/ppermute | solution.py:421
  9.6 0.5 %collective-permute-start.1 = (bf16[52,768]{1,0:T(8,128)(2,1)S(1)}, bf16[52,768]{1,0:T(8,128)(2,1)S(1)}, u32[]{:S(2)}, u32[]{:S(2)}) collective-permute-start(bf16[52,768]{1,0:T(8,128)(2,1)S(1)} %get-tuple-element.47), channel_id=1, source_target_pairs={{0,16},{8,24},{16,0},{24,8},{1,17},{9,25},{17,1},{25,9},{2,18},{10... | collective-permute-start | bytes 239624 | tf_op jit(solution)/shard_map/ppermute | solution.py:421
  10.1 0.0 collective-permute-done.3.refs_1_
  10.1 1.1 %collective-permute-start.2 = (bf16[52,768]{1,0:T(8,128)(2,1)S(1)}, bf16[52,768]{1,0:T(8,128)(2,1)S(1)}, u32[]{:S(2)}, u32[]{:S(2)}) collective-permute-start(bf16[52,768]{1,0:T(8,128)(2,1)S(1)} %get-tuple-element.48), channel_id=1, source_target_pairs={{0,8},{8,0},{16,24},{24,16},{1,9},{9,1},{17,25},{25,17},{2,10},{10... | collective-permute-start | bytes 239624 | tf_op jit(solution)/shard_map/ppermute | solution.py:421
  11.2 0.4 collective-permute-done.4.refs_2_
  11.6 0.5 %collective-permute-done.5.refs_3_ = bf16[52,768]{1,0:T(8,128)(2,1)S(1)} collective-permute-done((bf16[52,768]{1,0:T(8,128)(2,1)S(1)}, bf16[52,768]{1,0:T(8,128)(2,1)S(1)}, u32[]{:S(2)}, u32[]{:S(2)}) %collective-permute-start.5) | collective-permute-done | bytes 79904 | tf_op jit(solution)/shard_map/ppermute | solution.py:420
  12.1 0.0 copy-done.7
  12.2 0.0 copy-start.3
  12.2 0.0 copy-start.10
  12.2 3.9 %forward.1 = (bf16[208,768]{1,0:T(8,128)(2,1)S(1)}, bf16[208,768]{1,0:T(8,128)(2,1)S(1)}, bf16[272,768]{1,0:T(8,128)(2,1)S(1)}, bf16[272,768]{1,0:T(8,128)(2,1)S...) custom-call(bf16[52,768]{1,0:T(8,128)(2,1)S(1)} %get-tuple-element.4, ...), custom_call_target="tpu_custom_call" | custom-call | flops 1155268608 | bytes 9937344 | tf_op jit(solution)/shard_map/forward/pallas_call | solution.py:66
  16.1 0.0 collective-permute-done.refs_1_
  16.1 0.0 collective-permute-done.1.refs_2_
  16.1 0.0 collective-permute-done.2.refs_3_
  16.1 0.0 copy-done.3
  16.2 0.0 copy-done.10
  16.2 0.0 copy-start.16
  16.2 7.2 %backward.1 = (bf16[56,768]{1,0:T(8,128)(2,1)S(1)}, bf16[208,3072]{1,0:T(8,128)(2,1)S(1)}, f32[208,768]{1,0:T(8,128)S(1)}, bf16[12,272,208]{2,1,0:T(8,128)(2,1)S(1)}, bf16[208,768]{1,0:T(8,128)(2,1)S(1)}) custom-call(bf16[52,768]{1,0:T(8,128)(2,1)S(1)} %get-tuple-element.45.refs_0_, bf16[52,768]{1,0:T(8,128)(2,1)S(1)} %collective-permute-done.refs_1_, ...), custom_call_target="tpu_custom_call" | custom-call | flops 3680501760 | bytes 20416512 | tf_op jit(solution)/shard_map/backward/pallas_call | solution.py:66
  23.3 1.6 %collective-permute-start.8 = (bf16[56,768]{1,0:T(8,128)(2,1)S(1)}, bf16[56,768]{1,0:T(8,128)(2,1)S(1)}, u32[]{:S(2)}, u32[]{:S(2)}) collective-permute-start(bf16[56,768]{1,0:T(8,128)(2,1)S(1)} %get-tuple-element.66.refs_1_), channel_id=1, source_target_pairs={{0,24},{8,16},{16,8},{24,0},{1,25},{9,17},{17,9},{25,1},{2,26},{10... | collective-permute-start | bytes 258056 | tf_op jit(solution)/shard_map/ppermute | solution.py:481
  24.9 1.4 %collective-permute-start.7 = (bf16[56,768]{1,0:T(8,128)(2,1)S(1)}, bf16[56,768]{1,0:T(8,128)(2,1)S(1)}, u32[]{:S(2)}, u32[]{:S(2)}) collective-permute-start(bf16[56,768]{1,0:T(8,128)(2,1)S(1)} %get-tuple-element.66.refs_1_), channel_id=1, source_target_pairs={{0,16},{8,24},{16,0},{24,8},{1,17},{9,25},{17,1},{25,9},{2,18},{10... | collective-permute-start | bytes 258056 | tf_op jit(solution)/shard_map/ppermute | solution.py:481
  26.3 0.6 %collective-permute-start.6 = (bf16[56,768]{1,0:T(8,128)(2,1)S(1)}, bf16[56,768]{1,0:T(8,128)(2,1)S(1)}, u32[]{:S(2)}, u32[]{:S(2)}) collective-permute-start(bf16[56,768]{1,0:T(8,128)(2,1)S(1)} %get-tuple-element.66.refs_1_), channel_id=1, source_target_pairs={{0,8},{8,0},{16,24},{24,16},{1,9},{9,1},{17,25},{25,17},{2,10},{10... | collective-permute-start | bytes 258056 | tf_op jit(solution)/shard_map/ppermute | solution.py:481
  26.9 3.8 %rest.1.refs_5_.pack = bf16[4,104,768]{2,1,0:T(8,128)(2,1)S(1)} custom-call(bf16[208,3072]{1,0:T(8,128)(2,1)S(1)} %get-tuple-element.60.act, f32[208,768]{1,0:T(8,128)S(1)} %get-tuple-element.57.refs_8_.resid, f32[208,768]{1,0:T(8,128)S(1)} %get-tuple-element.61.dres, bf16[12,272,208]{2,1,0:T(8,128)(2,1)S(1)} %get-tuple-element.56.refs_7_.p_bf, ...), custom_call_target="tpu_custom_call" | custom-call | flops 1717567488 | bytes 14911488 | tf_op jit(solution)/shard_map/rest/pallas_call | solution.py:66
  30.8 0.0 collective-permute-done.8.refs_4_
  30.8 0.0 collective-permute-done.7.refs_3_
  30.8 0.0 collective-permute-done.6.refs_2_
  30.8 0.0 copy-done.6
  30.8 0.1 combine.1
  30.9 0.1 collective-permute-start.14
  31.0 1.8 %collective-permute-start.12 = (bf16[56,384]{1,0:T(8,128)(2,1)S(1)}, bf16[56,384]{1,0:T(8,128)(2,1)S(1)}, u32[]{:S(2)}, u32[]{:S(2)}) collective-permute-start(bf16[56,384]{1,0:T(8,128)(2,1)S(1)} %get-tuple-element.72), channel_id=1, source_target_pairs={{0,1},{1,0},{2,3},{3,2},{4,5},{5,4},{6,7},{7,6},{8,9},{9,8},{10,11... | collective-permute-start | bytes 129032 | tf_op jit(solution)/shard_map/ppermute | solution.py:490
  32.8 0.3 collective-permute-start.13
  33.2 1.6 %collective-permute-start.9 = (bf16[104,768]{1,0:T(8,128)(2,1)S(1)}, bf16[104,768]{1,0:T(8,128)(2,1)S(1)}, u32[]{:S(2)}, u32[]{:S(2)}) collective-permute-start(bf16[104,768]{1,0:T(8,128)(2,1)S(1)} %get-tuple-element.69), channel_id=1, source_target_pairs={{0,24},{8,16},{16,8},{24,0},{1,25},{9,17},{17,9},{25,1},{2,26},{10... | collective-permute-start | bytes 479240 | tf_op jit(solution)/shard_map/ppermute | solution.py:508
  34.7 1.4 %collective-permute-start.10 = (bf16[104,768]{1,0:T(8,128)(2,1)S(1)}, bf16[104,768]{1,0:T(8,128)(2,1)S(1)}, u32[]{:S(2)}, u32[]{:S(2)}) collective-permute-start(bf16[104,768]{1,0:T(8,128)(2,1)S(1)} %get-tuple-element.70), channel_id=1, source_target_pairs={{0,16},{8,24},{16,0},{24,8},{1,17},{9,25},{17,1},{25,9},{2,18},{10... | collective-permute-start | bytes 479240 | tf_op jit(solution)/shard_map/ppermute | solution.py:508
  36.1 0.0 collective-permute-done.14.refs_3_
  36.2 0.6 %collective-permute-start.11 = (bf16[104,768]{1,0:T(8,128)(2,1)S(1)}, bf16[104,768]{1,0:T(8,128)(2,1)S(1)}, u32[]{:S(2)}, u32[]{:S(2)}) collective-permute-start(bf16[104,768]{1,0:T(8,128)(2,1)S(1)} %get-tuple-element.71), channel_id=1, source_target_pairs={{0,8},{8,0},{16,24},{24,16},{1,9},{9,1},{17,25},{25,17},{2,10},{10... | collective-permute-start | bytes 479240 | tf_op jit(solution)/shard_map/ppermute | solution.py:508
  36.7 0.0 collective-permute-done.12.refs_1_
  36.7 0.1 collective-permute-done.13.refs_2_
  36.9 2.7 %collective-permute-start.15 = (bf16[56,384]{1,0:T(8,128)(2,1)S(1)}, bf16[56,384]{1,0:T(8,128)(2,1)S(1)}, u32[]{:S(2)}, u32[]{:S(2)}) collective-permute-start(bf16[56,384]{1,0:T(8,128)(2,1)S(1)} %add.2.refs_0_), channel_id=1, source_target_pairs={{0,4},{1,5},{2,6},{3,7},{4,0},{5,1},{6,2},{7,3},{8,12},{9,13},{10,... | collective-permute-start | bytes 129032 | tf_op jit(solution)/shard_map/ppermute | solution.py:496
  39.5 2.3 %collective-permute-done.15.refs_1_ = bf16[56,384]{1,0:T(8,128)(2,1)S(1)} collective-permute-done((bf16[56,384]{1,0:T(8,128)(2,1)S(1)}, bf16[56,384]{1,0:T(8,128)(2,1)S(1)}, u32[]{:S(2)}, u32[]{:S(2)}) %collective-permute-start.15) | collective-permute-done | bytes 43040 | tf_op jit(solution)/shard_map/ppermute | solution.py:496
  41.9 0.1 collective-permute-start.16
  41.9 0.0 collective-permute-done.9.refs_1_
  41.9 1.5 %collective-permute-done.10.refs_2_ = bf16[104,768]{1,0:T(8,128)(2,1)S(1)} collective-permute-done((bf16[104,768]{1,0:T(8,128)(2,1)S(1)}, bf16[104,768]{1,0:T(8,128)(2,1)S(1)}, u32[]{:S(2)}, u32[]{:S(2)}) %collective-permute-start.10) | collective-permute-done | bytes 159776 | tf_op jit(solution)/shard_map/ppermute | solution.py:508
  43.4 0.0 collective-permute-done.11.refs_3_
  43.4 0.0 collective-permute-done.16.refs_5_
  43.5 2.3 %final.1 = (bf16[3,52,768]{2,1,0:T(8,128)(2,1)}, bf16[3,52,768]{2,1,0:T(8,128)(2,1)}, f32[8,50]{1,0:T(8,128)}, f32[8,768]{1,0:T(8,128)}, f32[50,1,768]{2,1,0:T(1...) custom-call(bf16[104,768]{1,0:T(8,128)(2,1)S(1)} %get-tuple-element.68.refs_0_, ...), custom_call_target="tpu_custom_call" | custom-call | bytes 1314816 | tf_op jit(solution)/shard_map/final/pallas_call | solution.py:66
  (29 shorter events, 0.1 us)
Async XLA Ops:
  0.6 11.5 %copy-start = (bf16[768,2304]{1,0:T(8,128)(2,1)S(1)}, bf16[768,2304]{1,0:T(8,128)(2,1)}, u32[]{:S(2)}) copy-start(bf16[768,2304]{1,0:T(8,128)(2,1)} %w_qkv.1) | copy-start | bytes 10616836
  0.6 11.5 %copy-start.7 = (f32[768]{0:T(1024)S(1)}, f32[768]{0:T(1024)}, u32[]{:S(2)}) copy-start(f32[768]{0:T(1024)} %gain.1) | copy-start | bytes 9220
  0.7 11.5 %copy-start.4 = (f32[50,768]{1,0:T(8,128)S(1)}, f32[50,768]{1,0:T(8,128)}, u32[]{:S(2)}) copy-start(f32[50,768]{1,0:T(8,128)} %refs_8_.3) | copy-start | bytes 460804
  0.7 11.5 %copy-start.1 = (bf16[3072,768]{1,0:T(8,128)(2,1)S(1)}, bf16[3072,768]{1,0:T(8,128)(2,1)}, u32[]{:S(2)}) copy-start(bf16[3072,768]{1,0:T(8,128)(2,1)} %w_down.1) | copy-start | bytes 14155780
  0.7 11.5 %copy-start.9 = (f32[768]{0:T(1024)S(1)}, f32[768]{0:T(1024)}, u32[]{:S(2)}) copy-start(f32[768]{0:T(1024)} %refs_12_.3) | copy-start | bytes 9220
  0.7 11.5 %copy-start.2 = (bf16[768,768]{1,0:T(8,128)(2,1)S(1)}, bf16[768,768]{1,0:T(8,128)(2,1)}, u32[]{:S(2)}) copy-start(bf16[768,768]{1,0:T(8,128)(2,1)} %refs_11_.3) | copy-start | bytes 3538948
  0.7 11.5 %copy-start.15 = (f32[768]{0:T(1024)S(1)}, f32[768]{0:T(1024)}, u32[]{:S(2)}) copy-start(f32[768]{0:T(1024)} %refs_11_.2) | copy-start | bytes 9220
  0.7 11.5 %copy-start.14 = (f32[768]{0:T(1024)S(1)}, f32[768]{0:T(1024)}, u32[]{:S(2)}) copy-start(f32[768]{0:T(1024)} %refs_9_.2) | copy-start | bytes 9220
  0.7 11.5 %copy-start.11 = (f32[2304]{0:T(1024)S(1)}, f32[2304]{0:T(1024)}, u32[]{:S(2)}) copy-start(f32[2304]{0:T(1024)} %refs_8_.2) | copy-start | bytes 27652
  0.7 11.5 %copy-start.13 = (f32[768]{0:T(1024)S(1)}, f32[768]{0:T(1024)}, u32[]{:S(2)}) copy-start(f32[768]{0:T(1024)} %refs_7_.1) | copy-start | bytes 9220
  0.7 11.5 %copy-start.12 = (s32[3,208]{1,0:T(4,128)S(1)}, s32[3,208]{1,0:T(4,128)}, u32[]{:S(2)}) copy-start(s32[3,208]{1,0:T(4,128)} %refs_4_.1) | copy-start | bytes 7492
  2.2 8.0 %collective-permute-start.3 = (bf16[52,768]{1,0:T(8,128)(2,1)S(1)}, bf16[52,768]{1,0:T(8,128)(2,1)S(1)}, u32[]{:S(2)}, u32[]{:S(2)}) collective-permute-start(bf16[52,768]{1,0:T(8,128)(2,1)S(1)} %get-tuple-element.50), channel_id=1, source_target_pairs={{0,24},{8,16},{16,8},{24,0},{1,25},{9,17},{17,9},{25,1},{2,26},{10... | collective-permute-start | bytes 239624 | tf_op jit(solution)/shard_map/ppermute | solution.py:420
  6.1 5.5 %collective-permute-start.4 = (bf16[52,768]{1,0:T(8,128)(2,1)S(1)}, bf16[52,768]{1,0:T(8,128)(2,1)S(1)}, u32[]{:S(2)}, u32[]{:S(2)}) collective-permute-start(bf16[52,768]{1,0:T(8,128)(2,1)S(1)} %get-tuple-element.51), channel_id=1, source_target_pairs={{0,16},{8,24},{16,0},{24,8},{1,17},{9,25},{17,1},{25,9},{2,18},{10... | collective-permute-start | bytes 239624 | tf_op jit(solution)/shard_map/ppermute | solution.py:420
  6.6 5.5 %collective-permute-start.5 = (bf16[52,768]{1,0:T(8,128)(2,1)S(1)}, bf16[52,768]{1,0:T(8,128)(2,1)S(1)}, u32[]{:S(2)}, u32[]{:S(2)}) collective-permute-start(bf16[52,768]{1,0:T(8,128)(2,1)S(1)} %get-tuple-element.52), channel_id=1, source_target_pairs={{0,8},{8,0},{16,24},{24,16},{1,9},{9,1},{17,25},{25,17},{2,10},{10... | collective-permute-start | bytes 239624 | tf_op jit(solution)/shard_map/ppermute | solution.py:420
  6.8 9.3 %collective-permute-start = (bf16[52,768]{1,0:T(8,128)(2,1)S(1)}, bf16[52,768]{1,0:T(8,128)(2,1)S(1)}, u32[]{:S(2)}, u32[]{:S(2)}) collective-permute-start(bf16[52,768]{1,0:T(8,128)(2,1)S(1)} %get-tuple-element.46), channel_id=1, source_target_pairs={{0,24},{8,16},{16,8},{24,0},{1,25},{9,17},{17,9},{25,1},{2,26},{10... | collective-permute-start | bytes 239624 | tf_op jit(solution)/shard_map/ppermute | solution.py:421
  9.6 6.5 %collective-permute-start.1 = (bf16[52,768]{1,0:T(8,128)(2,1)S(1)}, bf16[52,768]{1,0:T(8,128)(2,1)S(1)}, u32[]{:S(2)}, u32[]{:S(2)}) collective-permute-start(bf16[52,768]{1,0:T(8,128)(2,1)S(1)} %get-tuple-element.47), channel_id=1, source_target_pairs={{0,16},{8,24},{16,0},{24,8},{1,17},{9,25},{17,1},{25,9},{2,18},{10... | collective-permute-start | bytes 239624 | tf_op jit(solution)/shard_map/ppermute | solution.py:421
  10.1 6.0 %collective-permute-start.2 = (bf16[52,768]{1,0:T(8,128)(2,1)S(1)}, bf16[52,768]{1,0:T(8,128)(2,1)S(1)}, u32[]{:S(2)}, u32[]{:S(2)}) collective-permute-start(bf16[52,768]{1,0:T(8,128)(2,1)S(1)} %get-tuple-element.48), channel_id=1, source_target_pairs={{0,8},{8,0},{16,24},{24,16},{1,9},{9,1},{17,25},{25,17},{2,10},{10... | collective-permute-start | bytes 239624 | tf_op jit(solution)/shard_map/ppermute | solution.py:421
  12.2 3.9 %copy-start.3 = (bf16[768,3072]{1,0:T(8,128)(2,1)S(1)}, bf16[768,3072]{1,0:T(8,128)(2,1)}, u32[]{:S(2)}) copy-start(bf16[768,3072]{1,0:T(8,128)(2,1)} %refs_13_.3) | copy-start | bytes 14155780
  12.2 3.9 %copy-start.10 = (f32[3072]{0:T(1024)S(1)}, f32[3072]{0:T(1024)}, u32[]{:S(2)}) copy-start(f32[3072]{0:T(1024)} %refs_14_.3) | copy-start | bytes 36868
  16.2 10.7 %copy-start.16 = (f32[768]{0:T(1024)S(1)}, f32[768]{0:T(1024)}, u32[]{:S(2)}) copy-start(f32[768]{0:T(1024)} %b_down.1) | copy-start | bytes 9220
  23.3 7.4 %collective-permute-start.8 = (bf16[56,768]{1,0:T(8,128)(2,1)S(1)}, bf16[56,768]{1,0:T(8,128)(2,1)S(1)}, u32[]{:S(2)}, u32[]{:S(2)}) collective-permute-start(bf16[56,768]{1,0:T(8,128)(2,1)S(1)} %get-tuple-element.66.refs_1_), channel_id=1, source_target_pairs={{0,24},{8,16},{16,8},{24,0},{1,25},{9,17},{17,9},{25,1},{2,26},{10... | collective-permute-start | bytes 258056 | tf_op jit(solution)/shard_map/ppermute | solution.py:481
  24.9 5.9 %collective-permute-start.7 = (bf16[56,768]{1,0:T(8,128)(2,1)S(1)}, bf16[56,768]{1,0:T(8,128)(2,1)S(1)}, u32[]{:S(2)}, u32[]{:S(2)}) collective-permute-start(bf16[56,768]{1,0:T(8,128)(2,1)S(1)} %get-tuple-element.66.refs_1_), channel_id=1, source_target_pairs={{0,16},{8,24},{16,0},{24,8},{1,17},{9,25},{17,1},{25,9},{2,18},{10... | collective-permute-start | bytes 258056 | tf_op jit(solution)/shard_map/ppermute | solution.py:481
  26.3 4.5 %collective-permute-start.6 = (bf16[56,768]{1,0:T(8,128)(2,1)S(1)}, bf16[56,768]{1,0:T(8,128)(2,1)S(1)}, u32[]{:S(2)}, u32[]{:S(2)}) collective-permute-start(bf16[56,768]{1,0:T(8,128)(2,1)S(1)} %get-tuple-element.66.refs_1_), channel_id=1, source_target_pairs={{0,8},{8,0},{16,24},{24,16},{1,9},{9,1},{17,25},{25,17},{2,10},{10... | collective-permute-start | bytes 258056 | tf_op jit(solution)/shard_map/ppermute | solution.py:481
  26.9 3.9 %copy-start.6 = (f32[1,50,768]{2,0,1:T(1,128)S(1)}, f32[1,50,768]{2,0,1:T(1,128)}, u32[]{:S(2)}) copy-start(f32[1,50,768]{2,0,1:T(1,128)} %param.36) | copy-start | bytes 460804
  26.9 16.5 %copy-start.5 = (f32[50,768]{1,0:T(8,128)S(1)}, f32[50,768]{1,0:T(8,128)}, u32[]{:S(2)}) copy-start(f32[50,768]{1,0:T(8,128)} %refs_9_.3) | copy-start | bytes 460804
  26.9 16.6 %copy-start.8 = (f32[768,8]{0,1:T(8,128)S(1)}, f32[768,8]{0,1:T(8,128)}, u32[]{:S(2)}) copy-start(f32[768,8]{0,1:T(8,128)} %param.35) | copy-start | bytes 73732
  30.9 5.2 %collective-permute-start.14 = (bf16[56,384]{1,0:T(8,128)(2,1)S(1)}, bf16[56,384]{1,0:T(8,128)(2,1)S(1)}, u32[]{:S(2)}, u32[]{:S(2)}) collective-permute-start(bf16[56,384]{1,0:T(8,128)(2,1)S(1)} %get-tuple-element.72), channel_id=1, source_target_pairs={{0,3},{1,2},{2,1},{3,0},{4,7},{5,6},{6,5},{7,4},{8,11},{9,10},{10,... | collective-permute-start | bytes 129032 | tf_op jit(solution)/shard_map/ppermute | solution.py:492
  31.0 5.7 %collective-permute-start.12 = (bf16[56,384]{1,0:T(8,128)(2,1)S(1)}, bf16[56,384]{1,0:T(8,128)(2,1)S(1)}, u32[]{:S(2)}, u32[]{:S(2)}) collective-permute-start(bf16[56,384]{1,0:T(8,128)(2,1)S(1)} %get-tuple-element.72), channel_id=1, source_target_pairs={{0,1},{1,0},{2,3},{3,2},{4,5},{5,4},{6,7},{7,6},{8,9},{9,8},{10,11... | collective-permute-start | bytes 129032 | tf_op jit(solution)/shard_map/ppermute | solution.py:490
  32.8 4.0 %collective-permute-start.13 = (bf16[56,384]{1,0:T(8,128)(2,1)S(1)}, bf16[56,384]{1,0:T(8,128)(2,1)S(1)}, u32[]{:S(2)}, u32[]{:S(2)}) collective-permute-start(bf16[56,384]{1,0:T(8,128)(2,1)S(1)} %get-tuple-element.67.after.refs_0_), channel_id=1, source_target_pairs={{0,2},{1,3},{2,0},{3,1},{4,6},{5,7},{6,4},{7,5},{8,10},{9,11},{10,... | collective-permute-start | bytes 129032 | tf_op jit(solution)/shard_map/ppermute | solution.py:492
  33.2 8.8 %collective-permute-start.9 = (bf16[104,768]{1,0:T(8,128)(2,1)S(1)}, bf16[104,768]{1,0:T(8,128)(2,1)S(1)}, u32[]{:S(2)}, u32[]{:S(2)}) collective-permute-start(bf16[104,768]{1,0:T(8,128)(2,1)S(1)} %get-tuple-element.69), channel_id=1, source_target_pairs={{0,24},{8,16},{16,8},{24,0},{1,25},{9,17},{17,9},{25,1},{2,26},{10... | collective-permute-start | bytes 479240 | tf_op jit(solution)/shard_map/ppermute | solution.py:508
  34.7 8.7 %collective-permute-start.10 = (bf16[104,768]{1,0:T(8,128)(2,1)S(1)}, bf16[104,768]{1,0:T(8,128)(2,1)S(1)}, u32[]{:S(2)}, u32[]{:S(2)}) collective-permute-start(bf16[104,768]{1,0:T(8,128)(2,1)S(1)} %get-tuple-element.70), channel_id=1, source_target_pairs={{0,16},{8,24},{16,0},{24,8},{1,17},{9,25},{17,1},{25,9},{2,18},{10... | collective-permute-start | bytes 479240 | tf_op jit(solution)/shard_map/ppermute | solution.py:508
  36.2 7.3 %collective-permute-start.11 = (bf16[104,768]{1,0:T(8,128)(2,1)S(1)}, bf16[104,768]{1,0:T(8,128)(2,1)S(1)}, u32[]{:S(2)}, u32[]{:S(2)}) collective-permute-start(bf16[104,768]{1,0:T(8,128)(2,1)S(1)} %get-tuple-element.71), channel_id=1, source_target_pairs={{0,8},{8,0},{16,24},{24,16},{1,9},{9,1},{17,25},{25,17},{2,10},{10... | collective-permute-start | bytes 479240 | tf_op jit(solution)/shard_map/ppermute | solution.py:508
  36.9 5.0 %collective-permute-start.15 = (bf16[56,384]{1,0:T(8,128)(2,1)S(1)}, bf16[56,384]{1,0:T(8,128)(2,1)S(1)}, u32[]{:S(2)}, u32[]{:S(2)}) collective-permute-start(bf16[56,384]{1,0:T(8,128)(2,1)S(1)} %add.2.refs_0_), channel_id=1, source_target_pairs={{0,4},{1,5},{2,6},{3,7},{4,0},{5,1},{6,2},{7,3},{8,12},{9,13},{10,... | collective-permute-start | bytes 129032 | tf_op jit(solution)/shard_map/ppermute | solution.py:496
  41.9 1.6 %collective-permute-start.16 = (f32[56,384]{1,0:T(8,128)S(1)}, f32[56,384]{1,0:T(8,128)S(1)}, u32[]{:S(2)}, u32[]{:S(2)}) collective-permute-start(f32[56,384]{1,0:T(8,128)S(1)} %add.3.refs_4_), channel_id=1, source_target_pairs={{0,1},{1,0},{2,3},{3,2},{4,5},{5,4},{6,7},{7,6},{8,9},{9,8},{10,11... | collective-permute-start | bytes 258056 | tf_op jit(solution)/shard_map/ppermute | solution.py:499

commit v7 on v6

--- a/solution.py
+++ b/solution.py
@@ -53,6 +53,11 @@
     mean = jnp.mean(inner, axis=-1, keepdims=True)
     along = jnp.mean(inner * hat, axis=-1, keepdims=True)
     return rstd * (inner - mean - hat * along)
+
+
+def bands(rows):
+    band = 16 if rows % 16 == 0 else 8 if rows % 8 == 0 else rows
+    return [pl.ds(low, band) for low in range(0, rows, band)]
 
 
 def call(kernel, outs, ins, scratch=(), in_specs=None, out_specs=None, flops=0, vmem=8 * MIB, name=None):
@@ -135,7 +140,6 @@
     live = jnp.where(me < images, 1.0, 0.0)
     for c in range(seq):
         x[pl.ds(c * chunk, chunk), :] = tbuf[me ^ c].astype(F32) * live
-    x_bf[...] = x[...].astype(BF16)
     mrow = mask[pl.ds(jnp.minimum(me, images - 1), 1), :].astype(F32)
     mcol = dot_tn(
         jnp.broadcast_to(mrow, (8, rows)).astype(BF16), jnp.full((8, rows), 0.125, BF16)
@@ -143,8 +147,10 @@
     rest = lax.broadcasted_iota(jnp.int32, (nkeys - rows, rows), 0)
     bias[:rows, :] = jnp.where(mcol > 0.5, 0.0, -jnp.inf)
     bias[rows:, :] = jnp.where(rest < count, 0.0, -jnp.inf)
-    hat, _ = normalize(x[...])
-    normed[:rows, :] = (hat * gain + shift).astype(BF16)
+    for band in bands(rows):
+        x_bf[band, :] = x[band, :].astype(BF16)
+        hat, _ = normalize(x[band, :])
+        normed[band, :] = (hat * gain + shift).astype(BF16)
     hat, _ = normalize(prompts[...].astype(BF16).astype(F32))
     normed[rows:, :] = jnp.zeros((nkeys - rows, width), BF16)
     normed[rows : rows + count, :] = (hat * gain + shift).astype(BF16)
@@ -168,8 +174,10 @@
         part = pl.ds(h * head, head)
         mix_t[part, :] = dot_tn(values[:, part], p_bf[h]).astype(BF16)
     resid[...] = x[...] + dot_tn(mix_t[...], w_out[...]) + line(b_out)
-    hat, _ = normalize(resid[...])
-    normed_two[...] = (hat * line(gain_two) + line(shift_two)).astype(BF16)
+    scale_two, offset_two = line(gain_two), line(shift_two)
+    for band in bands(rows):
+        hat, _ = normalize(resid[band, :])
+        normed_two[band, :] = (hat * scale_two + offset_two).astype(BF16)
 
 
 def backward_kernel(seq, images, *refs):
@@ -204,11 +212,11 @@
         act[:, cols] = (hidden * cdf).astype(BF16)
         pdf = jnp.exp(-0.5 * hidden * hidden) * (1.0 / math.sqrt(2.0 * math.pi))
         dhid[:, cols] = (grad * (cdf + hidden * pdf)).astype(BF16)
-    hat_two, rstd_two = normalize(resid[...])
-    grad_resid = gbuf[...] + norm_back(
-        hat_two, rstd_two, line(gain_two), dot_nt(dhid[...], w_up[...])
-    )
-    dres[...] = grad_resid
+    dres[...] = dot_nt(dhid[...], w_up[...])
+    scale_two = line(gain_two)
+    for band in bands(rows):
+        hat, rstd = normalize(resid[band, :])
+        dres[band, :] = gbuf[band, :] + norm_back(hat, rstd, scale_two, dres[band, :])
     dmix[...] = dot_nt(dres[...].astype(BF16), w_out[...]).astype(BF16)
     lane = lax.broadcasted_iota(jnp.int32, (nkeys, 2 * head), 1) // head
     for h in range(HEADS):
@@ -279,8 +287,11 @@
             pack[c, pl.ds(at, high - low), :] = wide[pl.ds(c * chunk + low, high - low), :].astype(
                 BF16
             )
-    hat, rstd = normalize(x_bf[...].astype(F32))
-    wide[...] = dres[...] + norm_back(hat, rstd, line(gain), dot_nt(dqkv[...], w_qkv[...]))
+    wide[...] = dot_nt(dqkv[...], w_qkv[...])
+    scale_one = line(gain)
+    for band in bands(rows):
+        hat, rstd = normalize(x_bf[band, :].astype(F32))
+        wide[band, :] = dres[band, :] + norm_back(hat, rstd, scale_one, wide[band, :])
     for c in range(seq):
         for (low, high), at in zip(spans(chunk), (full, full + chunk)):
             pack[c, pl.ds(at, high - low), :] = wide[pl.ds(c * chunk + low, high - low), :].astype(

time: 46 us -> 45.9 us (level)
  transfers between devices with their start and end apart: 17 -> 17, of which waited for: 5 -> 6; matrix products, arithmetic and copies ran while one was open for 0% -> 0% of each run, Pallas kernels for 17% -> 17%
where the time goes in v7:
time: 45.9 us; the launch traced here: 45.7 us
  starting transfers between devices  21.1 us (46%)
  Pallas kernels  18.7 us (41%)
  waiting for transfers between devices  4.84 us (11%)
  between operations  0.97 us (2%)
    pallas_call x9, Pallas kernels, call(): pl.pallas_call(kernel, out_shape=[held.get(id(spec), jax.ShapeDtypeStruct...  18.7 us
    ppermute x3, starting transfers between devices, body(): lax.ppermute(toks[k], 'seq', flip(k, seq))  4.6 us
    ppermute x3, starting transfers between devices, body(): lax.ppermute(cots[k], 'seq', flip(k, seq))  4.43 us
    ppermute x3, starting transfers between devices, body(): lax.ppermute(packs[k], 'seq', flip(k, seq))  3.55 us
    ppermute x3, starting transfers between devices, body(): lax.ppermute(pgrad, 'seq', flip(k, seq))  3.55 us
    ppermute x1, starting transfers between devices, body(): parts = [mine, lax.ppermute(mine, 'dp', flip(bit, dp))]  2.68 us
    ppermute x1, waiting for transfers between devices, body(): parts = [mine, lax.ppermute(mine, 'dp', flip(bit, dp))]  2.3 us
    ppermute x1, starting transfers between devices, body(): parts = [keep, lax.ppermute(give, 'dp', flip(1, dp))]  1.77 us
  transfers between devices with their start and end apart: 17, of which 6 were waited for; matrix products, arithmetic and copies ran while one was open for 0% of the time, Pallas kernels for 17%

profile of v7, /device:TPU:0, one launch (start us, length us, event | category | flops | bytes accessed | tf_op | source)
XLA Modules:
  0.0 45.7 jit_solution(4543594858121306882)
XLA Ops:
  0.6 0.0 copy-start
  0.6 0.0 copy-start.7
  0.7 0.0 copy-start.4
  0.7 1.4 %pick.1 = (bf16[52,768]{1,0:T(8,128)(2,1)S(1)}, bf16[52,768]{1,0:T(8,128)(2,1)S(1)}, bf16[52,768]{1,0:T(8,128)(2,1)S(1)}, bf16[52,768]{1,0:T(8,128)(2,1)S(1)}, b...) custom-call(bf16[3,52,768]{2,1,0:T(8,128)(2,1)} %tok.1, ...), custom_call_target="tpu_custom_call" | custom-call | flops 17179869184 | bytes 479232 | tf_op jit(solution)/shard_map/pick/pallas_call | solution.py:71
  2.2 4.0 %collective-permute-start.3 = (bf16[52,768]{1,0:T(8,128)(2,1)S(1)}, bf16[52,768]{1,0:T(8,128)(2,1)S(1)}, u32[]{:S(2)}, u32[]{:S(2)}) collective-permute-start(bf16[52,768]{1,0:T(8,128)(2,1)S(1)} %get-tuple-element.50), channel_id=1, source_target_pairs={{0,24},{8,16},{16,8},{24,0},{1,25},{9,17},{17,9},{25,1},{2,26},{10... | collective-permute-start | bytes 239624 | tf_op jit(solution)/shard_map/ppermute | solution.py:431
  6.1 0.5 %collective-permute-start.4 = (bf16[52,768]{1,0:T(8,128)(2,1)S(1)}, bf16[52,768]{1,0:T(8,128)(2,1)S(1)}, u32[]{:S(2)}, u32[]{:S(2)}) collective-permute-start(bf16[52,768]{1,0:T(8,128)(2,1)S(1)} %get-tuple-element.51), channel_id=1, source_target_pairs={{0,16},{8,24},{16,0},{24,8},{1,17},{9,25},{17,1},{25,9},{2,18},{10... | collective-permute-start | bytes 239624 | tf_op jit(solution)/shard_map/ppermute | solution.py:431
  6.6 0.1 collective-permute-start.5
  6.8 2.8 %collective-permute-start = (bf16[52,768]{1,0:T(8,128)(2,1)S(1)}, bf16[52,768]{1,0:T(8,128)(2,1)S(1)}, u32[]{:S(2)}, u32[]{:S(2)}) collective-permute-start(bf16[52,768]{1,0:T(8,128)(2,1)S(1)} %get-tuple-element.46), channel_id=1, source_target_pairs={{0,24},{8,16},{16,8},{24,0},{1,25},{9,17},{17,9},{25,1},{2,26},{10... | collective-permute-start | bytes 239624 | tf_op jit(solution)/shard_map/ppermute | solution.py:432
  9.6 0.5 %collective-permute-start.1 = (bf16[52,768]{1,0:T(8,128)(2,1)S(1)}, bf16[52,768]{1,0:T(8,128)(2,1)S(1)}, u32[]{:S(2)}, u32[]{:S(2)}) collective-permute-start(bf16[52,768]{1,0:T(8,128)(2,1)S(1)} %get-tuple-element.47), channel_id=1, source_target_pairs={{0,16},{8,24},{16,0},{24,8},{1,17},{9,25},{17,1},{25,9},{2,18},{10... | collective-permute-start | bytes 239624 | tf_op jit(solution)/shard_map/ppermute | solution.py:432
  10.1 0.0 collective-permute-done.3.refs_1_
  10.1 1.1 %collective-permute-start.2 = (bf16[52,768]{1,0:T(8,128)(2,1)S(1)}, bf16[52,768]{1,0:T(8,128)(2,1)S(1)}, u32[]{:S(2)}, u32[]{:S(2)}) collective-permute-start(bf16[52,768]{1,0:T(8,128)(2,1)S(1)} %get-tuple-element.48), channel_id=1, source_target_pairs={{0,8},{8,0},{16,24},{24,16},{1,9},{9,1},{17,25},{25,17},{2,10},{10... | collective-permute-start | bytes 239624 | tf_op jit(solution)/shard_map/ppermute | solution.py:432
  11.2 0.4 collective-permute-done.4.refs_2_
  11.6 0.5 %collective-permute-done.5.refs_3_ = bf16[52,768]{1,0:T(8,128)(2,1)S(1)} collective-permute-done((bf16[52,768]{1,0:T(8,128)(2,1)S(1)}, bf16[52,768]{1,0:T(8,128)(2,1)S(1)}, u32[]{:S(2)}, u32[]{:S(2)}) %collective-permute-start.5) | collective-permute-done | bytes 79904 | tf_op jit(solution)/shard_map/ppermute | solution.py:431
  12.1 0.0 copy-done
  12.2 0.0 copy-start.3
  12.2 0.0 copy-start.10
  12.2 3.8 %forward.1 = (bf16[208,768]{1,0:T(8,128)(2,1)S(1)}, bf16[208,768]{1,0:T(8,128)(2,1)S(1)}, bf16[272,768]{1,0:T(8,128)(2,1)S(1)}, bf16[272,768]{1,0:T(8,128)(2,1)S...) custom-call(bf16[52,768]{1,0:T(8,128)(2,1)S(1)} %get-tuple-element.4, ...), custom_call_target="tpu_custom_call" | custom-call | flops 1155268608 | bytes 9937344 | tf_op jit(solution)/shard_map/forward/pallas_call | solution.py:71
  16.0 0.0 collective-permute-done.refs_1_
  16.1 0.0 collective-permute-done.1.refs_2_
  16.1 0.0 collective-permute-done.2.refs_3_
  16.1 0.0 copy-start.16
  16.1 7.1 %backward.1 = (bf16[56,768]{1,0:T(8,128)(2,1)S(1)}, bf16[208,3072]{1,0:T(8,128)(2,1)S(1)}, f32[208,768]{1,0:T(8,128)S(1)}, bf16[12,272,208]{2,1,0:T(8,128)(2,1)S(1)}, bf16[208,768]{1,0:T(8,128)(2,1)S(1)}) custom-call(bf16[52,768]{1,0:T(8,128)(2,1)S(1)} %get-tuple-element.45.refs_0_, bf16[52,768]{1,0:T(8,128)(2,1)S(1)} %collective-permute-done.refs_1_, ...), custom_call_target="tpu_custom_call" | custom-call | flops 3680501760 | bytes 20416512 | tf_op jit(solution)/shard_map/backward/pallas_call | solution.py:71
  23.3 1.6 %collective-permute-start.8 = (bf16[56,768]{1,0:T(8,128)(2,1)S(1)}, bf16[56,768]{1,0:T(8,128)(2,1)S(1)}, u32[]{:S(2)}, u32[]{:S(2)}) collective-permute-start(bf16[56,768]{1,0:T(8,128)(2,1)S(1)} %get-tuple-element.66.refs_1_), channel_id=1, source_target_pairs={{0,24},{8,16},{16,8},{24,0},{1,25},{9,17},{17,9},{25,1},{2,26},{10... | collective-permute-start | bytes 258056 | tf_op jit(solution)/shard_map/ppermute | solution.py:492
  24.8 1.4 %collective-permute-start.7 = (bf16[56,768]{1,0:T(8,128)(2,1)S(1)}, bf16[56,768]{1,0:T(8,128)(2,1)S(1)}, u32[]{:S(2)}, u32[]{:S(2)}) collective-permute-start(bf16[56,768]{1,0:T(8,128)(2,1)S(1)} %get-tuple-element.66.refs_1_), channel_id=1, source_target_pairs={{0,16},{8,24},{16,0},{24,8},{1,17},{9,25},{17,1},{25,9},{2,18},{10... | collective-permute-start | bytes 258056 | tf_op jit(solution)/shard_map/ppermute | solution.py:492
  26.2 0.6 %collective-permute-start.6 = (bf16[56,768]{1,0:T(8,128)(2,1)S(1)}, bf16[56,768]{1,0:T(8,128)(2,1)S(1)}, u32[]{:S(2)}, u32[]{:S(2)}) collective-permute-start(bf16[56,768]{1,0:T(8,128)(2,1)S(1)} %get-tuple-element.66.refs_1_), channel_id=1, source_target_pairs={{0,8},{8,0},{16,24},{24,16},{1,9},{9,1},{17,25},{25,17},{2,10},{10... | collective-permute-start | bytes 258056 | tf_op jit(solution)/shard_map/ppermute | solution.py:492
  26.8 3.8 %rest.1.refs_5_.pack = bf16[4,104,768]{2,1,0:T(8,128)(2,1)S(1)} custom-call(bf16[208,3072]{1,0:T(8,128)(2,1)S(1)} %get-tuple-element.60.act, f32[208,768]{1,0:T(8,128)S(1)} %get-tuple-element.57.refs_8_.resid, f32[208,768]{1,0:T(8,128)S(1)} %get-tuple-element.61.dres, bf16[12,272,208]{2,1,0:T(8,128)(2,1)S(1)} %get-tuple-element.56.refs_7_.p_bf, ...), custom_call_target="tpu_custom_call" | custom-call | flops 1717567488 | bytes 14911488 | tf_op jit(solution)/shard_map/rest/pallas_call | solution.py:71
  30.6 0.0 collective-permute-done.8.refs_4_
  30.7 0.0 collective-permute-done.7.refs_3_
  30.7 0.1 collective-permute-done.6.refs_2_
  30.7 0.1 combine.1
  30.8 0.1 collective-permute-start.14
  30.9 1.8 %collective-permute-start.12 = (bf16[56,384]{1,0:T(8,128)(2,1)S(1)}, bf16[56,384]{1,0:T(8,128)(2,1)S(1)}, u32[]{:S(2)}, u32[]{:S(2)}) collective-permute-start(bf16[56,384]{1,0:T(8,128)(2,1)S(1)} %get-tuple-element.72), channel_id=1, source_target_pairs={{0,1},{1,0},{2,3},{3,2},{4,5},{5,4},{6,7},{7,6},{8,9},{9,8},{10,11... | collective-permute-start | bytes 129032 | tf_op jit(solution)/shard_map/ppermute | solution.py:501
  32.7 0.4 collective-permute-start.13
  33.1 1.5 %collective-permute-start.9 = (bf16[104,768]{1,0:T(8,128)(2,1)S(1)}, bf16[104,768]{1,0:T(8,128)(2,1)S(1)}, u32[]{:S(2)}, u32[]{:S(2)}) collective-permute-start(bf16[104,768]{1,0:T(8,128)(2,1)S(1)} %get-tuple-element.69), channel_id=1, source_target_pairs={{0,24},{8,16},{16,8},{24,0},{1,25},{9,17},{17,9},{25,1},{2,26},{10... | collective-permute-start | bytes 479240 | tf_op jit(solution)/shard_map/ppermute | solution.py:519
  34.6 1.4 %collective-permute-start.10 = (bf16[104,768]{1,0:T(8,128)(2,1)S(1)}, bf16[104,768]{1,0:T(8,128)(2,1)S(1)}, u32[]{:S(2)}, u32[]{:S(2)}) collective-permute-start(bf16[104,768]{1,0:T(8,128)(2,1)S(1)} %get-tuple-element.70), channel_id=1, source_target_pairs={{0,16},{8,24},{16,0},{24,8},{1,17},{9,25},{17,1},{25,9},{2,18},{10... | collective-permute-start | bytes 479240 | tf_op jit(solution)/shard_map/ppermute | solution.py:519
  36.0 0.0 collective-permute-done.14.refs_3_
  36.0 0.6 %collective-permute-start.11 = (bf16[104,768]{1,0:T(8,128)(2,1)S(1)}, bf16[104,768]{1,0:T(8,128)(2,1)S(1)}, u32[]{:S(2)}, u32[]{:S(2)}) collective-permute-start(bf16[104,768]{1,0:T(8,128)(2,1)S(1)} %get-tuple-element.71), channel_id=1, source_target_pairs={{0,8},{8,0},{16,24},{24,16},{1,9},{9,1},{17,25},{25,17},{2,10},{10... | collective-permute-start | bytes 479240 | tf_op jit(solution)/shard_map/ppermute | solution.py:519
  36.7 0.0 collective-permute-done.12.refs_1_
  36.7 0.1 collective-permute-done.13.refs_2_
  36.8 2.7 %collective-permute-start.15 = (bf16[56,384]{1,0:T(8,128)(2,1)S(1)}, bf16[56,384]{1,0:T(8,128)(2,1)S(1)}, u32[]{:S(2)}, u32[]{:S(2)}) collective-permute-start(bf16[56,384]{1,0:T(8,128)(2,1)S(1)} %add.2.refs_0_), channel_id=1, source_target_pairs={{0,4},{1,5},{2,6},{3,7},{4,0},{5,1},{6,2},{7,3},{8,12},{9,13},{10,... | collective-permute-start | bytes 129032 | tf_op jit(solution)/shard_map/ppermute | solution.py:507
  39.4 2.3 %collective-permute-done.15.refs_1_ = bf16[56,384]{1,0:T(8,128)(2,1)S(1)} collective-permute-done((bf16[56,384]{1,0:T(8,128)(2,1)S(1)}, bf16[56,384]{1,0:T(8,128)(2,1)S(1)}, u32[]{:S(2)}, u32[]{:S(2)}) %collective-permute-start.15) | collective-permute-done | bytes 43040 | tf_op jit(solution)/shard_map/ppermute | solution.py:507
  41.8 0.1 collective-permute-start.16
  41.8 0.0 collective-permute-done.9.refs_1_
  41.9 1.5 %collective-permute-done.10.refs_2_ = bf16[104,768]{1,0:T(8,128)(2,1)S(1)} collective-permute-done((bf16[104,768]{1,0:T(8,128)(2,1)S(1)}, bf16[104,768]{1,0:T(8,128)(2,1)S(1)}, u32[]{:S(2)}, u32[]{:S(2)}) %collective-permute-start.10) | collective-permute-done | bytes 159776 | tf_op jit(solution)/shard_map/ppermute | solution.py:519
  43.3 0.0 collective-permute-done.11.refs_3_
  43.3 0.0 collective-permute-done.16.refs_5_
  43.4 0.0 copy-done.5
  43.4 2.3 %final.1 = (bf16[3,52,768]{2,1,0:T(8,128)(2,1)}, bf16[3,52,768]{2,1,0:T(8,128)(2,1)}, f32[8,50]{1,0:T(8,128)}, f32[8,768]{1,0:T(8,128)}, f32[50,1,768]{2,1,0:T(1...) custom-call(bf16[104,768]{1,0:T(8,128)(2,1)S(1)} %get-tuple-element.68.refs_0_, ...), custom_call_target="tpu_custom_call" | custom-call | bytes 1314816 | tf_op jit(solution)/shard_map/final/pallas_call | solution.py:71
  (29 shorter events, 0.1 us)
Async XLA Ops:
  0.6 11.5 %copy-start = (bf16[768,2304]{1,0:T(8,128)(2,1)S(1)}, bf16[768,2304]{1,0:T(8,128)(2,1)}, u32[]{:S(2)}) copy-start(bf16[768,2304]{1,0:T(8,128)(2,1)} %w_qkv.1) | copy-start | bytes 10616836
  0.6 11.5 %copy-start.7 = (f32[768]{0:T(1024)S(1)}, f32[768]{0:T(1024)}, u32[]{:S(2)}) copy-start(f32[768]{0:T(1024)} %gain.1) | copy-start | bytes 9220
  0.7 11.5 %copy-start.4 = (f32[50,768]{1,0:T(8,128)S(1)}, f32[50,768]{1,0:T(8,128)}, u32[]{:S(2)}) copy-start(f32[50,768]{1,0:T(8,128)} %refs_8_.3) | copy-start | bytes 460804
  0.7 11.5 %copy-start.1 = (bf16[3072,768]{1,0:T(8,128)(2,1)S(1)}, bf16[3072,768]{1,0:T(8,128)(2,1)}, u32[]{:S(2)}) copy-start(bf16[3072,768]{1,0:T(8,128)(2,1)} %w_down.1) | copy-start | bytes 14155780
  0.7 11.5 %copy-start.9 = (f32[768]{0:T(1024)S(1)}, f32[768]{0:T(1024)}, u32[]{:S(2)}) copy-start(f32[768]{0:T(1024)} %refs_12_.3) | copy-start | bytes 9220
  0.7 11.5 %copy-start.2 = (bf16[768,768]{1,0:T(8,128)(2,1)S(1)}, bf16[768,768]{1,0:T(8,128)(2,1)}, u32[]{:S(2)}) copy-start(bf16[768,768]{1,0:T(8,128)(2,1)} %refs_11_.3) | copy-start | bytes 3538948
  0.7 11.5 %copy-start.15 = (f32[768]{0:T(1024)S(1)}, f32[768]{0:T(1024)}, u32[]{:S(2)}) copy-start(f32[768]{0:T(1024)} %refs_11_.2) | copy-start | bytes 9220
  0.7 11.5 %copy-start.14 = (f32[768]{0:T(1024)S(1)}, f32[768]{0:T(1024)}, u32[]{:S(2)}) copy-start(f32[768]{0:T(1024)} %refs_9_.2) | copy-start | bytes 9220
  0.7 11.5 %copy-start.11 = (f32[2304]{0:T(1024)S(1)}, f32[2304]{0:T(1024)}, u32[]{:S(2)}) copy-start(f32[2304]{0:T(1024)} %refs_8_.2) | copy-start | bytes 27652
  0.7 11.5 %copy-start.13 = (f32[768]{0:T(1024)S(1)}, f32[768]{0:T(1024)}, u32[]{:S(2)}) copy-start(f32[768]{0:T(1024)} %refs_7_.1) | copy-start | bytes 9220
  0.7 11.5 %copy-start.12 = (s32[3,208]{1,0:T(4,128)S(1)}, s32[3,208]{1,0:T(4,128)}, u32[]{:S(2)}) copy-start(s32[3,208]{1,0:T(4,128)} %refs_4_.1) | copy-start | bytes 7492
  2.2 8.0 %collective-permute-start.3 = (bf16[52,768]{1,0:T(8,128)(2,1)S(1)}, bf16[52,768]{1,0:T(8,128)(2,1)S(1)}, u32[]{:S(2)}, u32[]{:S(2)}) collective-permute-start(bf16[52,768]{1,0:T(8,128)(2,1)S(1)} %get-tuple-element.50), channel_id=1, source_target_pairs={{0,24},{8,16},{16,8},{24,0},{1,25},{9,17},{17,9},{25,1},{2,26},{10... | collective-permute-start | bytes 239624 | tf_op jit(solution)/shard_map/ppermute | solution.py:431
  6.1 5.5 %collective-permute-start.4 = (bf16[52,768]{1,0:T(8,128)(2,1)S(1)}, bf16[52,768]{1,0:T(8,128)(2,1)S(1)}, u32[]{:S(2)}, u32[]{:S(2)}) collective-permute-start(bf16[52,768]{1,0:T(8,128)(2,1)S(1)} %get-tuple-element.51), channel_id=1, source_target_pairs={{0,16},{8,24},{16,0},{24,8},{1,17},{9,25},{17,1},{25,9},{2,18},{10... | collective-permute-start | bytes 239624 | tf_op jit(solution)/shard_map/ppermute | solution.py:431
  6.6 5.5 %collective-permute-start.5 = (bf16[52,768]{1,0:T(8,128)(2,1)S(1)}, bf16[52,768]{1,0:T(8,128)(2,1)S(1)}, u32[]{:S(2)}, u32[]{:S(2)}) collective-permute-start(bf16[52,768]{1,0:T(8,128)(2,1)S(1)} %get-tuple-element.52), channel_id=1, source_target_pairs={{0,8},{8,0},{16,24},{24,16},{1,9},{9,1},{17,25},{25,17},{2,10},{10... | collective-permute-start | bytes 239624 | tf_op jit(solution)/shard_map/ppermute | solution.py:431
  6.8 9.3 %collective-permute-start = (bf16[52,768]{1,0:T(8,128)(2,1)S(1)}, bf16[52,768]{1,0:T(8,128)(2,1)S(1)}, u32[]{:S(2)}, u32[]{:S(2)}) collective-permute-start(bf16[52,768]{1,0:T(8,128)(2,1)S(1)} %get-tuple-element.46), channel_id=1, source_target_pairs={{0,24},{8,16},{16,8},{24,0},{1,25},{9,17},{17,9},{25,1},{2,26},{10... | collective-permute-start | bytes 239624 | tf_op jit(solution)/shard_map/ppermute | solution.py:432
  9.6 6.4 %collective-permute-start.1 = (bf16[52,768]{1,0:T(8,128)(2,1)S(1)}, bf16[52,768]{1,0:T(8,128)(2,1)S(1)}, u32[]{:S(2)}, u32[]{:S(2)}) collective-permute-start(bf16[52,768]{1,0:T(8,128)(2,1)S(1)} %get-tuple-element.47), channel_id=1, source_target_pairs={{0,16},{8,24},{16,0},{24,8},{1,17},{9,25},{17,1},{25,9},{2,18},{10... | collective-permute-start | bytes 239624 | tf_op jit(solution)/shard_map/ppermute | solution.py:432
  10.1 5.9 %collective-permute-start.2 = (bf16[52,768]{1,0:T(8,128)(2,1)S(1)}, bf16[52,768]{1,0:T(8,128)(2,1)S(1)}, u32[]{:S(2)}, u32[]{:S(2)}) collective-permute-start(bf16[52,768]{1,0:T(8,128)(2,1)S(1)} %get-tuple-element.48), channel_id=1, source_target_pairs={{0,8},{8,0},{16,24},{24,16},{1,9},{9,1},{17,25},{25,17},{2,10},{10... | collective-permute-start | bytes 239624 | tf_op jit(solution)/shard_map/ppermute | solution.py:432
  12.2 3.9 %copy-start.3 = (bf16[768,3072]{1,0:T(8,128)(2,1)S(1)}, bf16[768,3072]{1,0:T(8,128)(2,1)}, u32[]{:S(2)}) copy-start(bf16[768,3072]{1,0:T(8,128)(2,1)} %refs_13_.3) | copy-start | bytes 14155780
  12.2 3.9 %copy-start.10 = (f32[3072]{0:T(1024)S(1)}, f32[3072]{0:T(1024)}, u32[]{:S(2)}) copy-start(f32[3072]{0:T(1024)} %refs_14_.3) | copy-start | bytes 36868
  16.1 10.7 %copy-start.16 = (f32[768]{0:T(1024)S(1)}, f32[768]{0:T(1024)}, u32[]{:S(2)}) copy-start(f32[768]{0:T(1024)} %b_down.1) | copy-start | bytes 9220
  23.3 7.4 %collective-permute-start.8 = (bf16[56,768]{1,0:T(8,128)(2,1)S(1)}, bf16[56,768]{1,0:T(8,128)(2,1)S(1)}, u32[]{:S(2)}, u32[]{:S(2)}) collective-permute-start(bf16[56,768]{1,0:T(8,128)(2,1)S(1)} %get-tuple-element.66.refs_1_), channel_id=1, source_target_pairs={{0,24},{8,16},{16,8},{24,0},{1,25},{9,17},{17,9},{25,1},{2,26},{10... | collective-permute-start | bytes 258056 | tf_op jit(solution)/shard_map/ppermute | solution.py:492
  24.8 5.8 %collective-permute-start.7 = (bf16[56,768]{1,0:T(8,128)(2,1)S(1)}, bf16[56,768]{1,0:T(8,128)(2,1)S(1)}, u32[]{:S(2)}, u32[]{:S(2)}) collective-permute-start(bf16[56,768]{1,0:T(8,128)(2,1)S(1)} %get-tuple-element.66.refs_1_), channel_id=1, source_target_pairs={{0,16},{8,24},{16,0},{24,8},{1,17},{9,25},{17,1},{25,9},{2,18},{10... | collective-permute-start | bytes 258056 | tf_op jit(solution)/shard_map/ppermute | solution.py:492
  26.2 4.5 %collective-permute-start.6 = (bf16[56,768]{1,0:T(8,128)(2,1)S(1)}, bf16[56,768]{1,0:T(8,128)(2,1)S(1)}, u32[]{:S(2)}, u32[]{:S(2)}) collective-permute-start(bf16[56,768]{1,0:T(8,128)(2,1)S(1)} %get-tuple-element.66.refs_1_), channel_id=1, source_target_pairs={{0,8},{8,0},{16,24},{24,16},{1,9},{9,1},{17,25},{25,17},{2,10},{10... | collective-permute-start | bytes 258056 | tf_op jit(solution)/shard_map/ppermute | solution.py:492
  26.8 3.9 %copy-start.6 = (f32[1,50,768]{2,0,1:T(1,128)S(1)}, f32[1,50,768]{2,0,1:T(1,128)}, u32[]{:S(2)}) copy-start(f32[1,50,768]{2,0,1:T(1,128)} %param.36) | copy-start | bytes 460804
  26.8 16.5 %copy-start.5 = (f32[50,768]{1,0:T(8,128)S(1)}, f32[50,768]{1,0:T(8,128)}, u32[]{:S(2)}) copy-start(f32[50,768]{1,0:T(8,128)} %refs_9_.3) | copy-start | bytes 460804
  26.8 16.5 %copy-start.8 = (f32[768,8]{0,1:T(8,128)S(1)}, f32[768,8]{0,1:T(8,128)}, u32[]{:S(2)}) copy-start(f32[768,8]{0,1:T(8,128)} %param.35) | copy-start | bytes 73732
  30.8 5.2 %collective-permute-start.14 = (bf16[56,384]{1,0:T(8,128)(2,1)S(1)}, bf16[56,384]{1,0:T(8,128)(2,1)S(1)}, u32[]{:S(2)}, u32[]{:S(2)}) collective-permute-start(bf16[56,384]{1,0:T(8,128)(2,1)S(1)} %get-tuple-element.72), channel_id=1, source_target_pairs={{0,3},{1,2},{2,1},{3,0},{4,7},{5,6},{6,5},{7,4},{8,11},{9,10},{10,... | collective-permute-start | bytes 129032 | tf_op jit(solution)/shard_map/ppermute | solution.py:503
  30.9 5.7 %collective-permute-start.12 = (bf16[56,384]{1,0:T(8,128)(2,1)S(1)}, bf16[56,384]{1,0:T(8,128)(2,1)S(1)}, u32[]{:S(2)}, u32[]{:S(2)}) collective-permute-start(bf16[56,384]{1,0:T(8,128)(2,1)S(1)} %get-tuple-element.72), channel_id=1, source_target_pairs={{0,1},{1,0},{2,3},{3,2},{4,5},{5,4},{6,7},{7,6},{8,9},{9,8},{10,11... | collective-permute-start | bytes 129032 | tf_op jit(solution)/shard_map/ppermute | solution.py:501
  32.7 4.0 %collective-permute-start.13 = (bf16[56,384]{1,0:T(8,128)(2,1)S(1)}, bf16[56,384]{1,0:T(8,128)(2,1)S(1)}, u32[]{:S(2)}, u32[]{:S(2)}) collective-permute-start(bf16[56,384]{1,0:T(8,128)(2,1)S(1)} %get-tuple-element.67.after.refs_0_), channel_id=1, source_target_pairs={{0,2},{1,3},{2,0},{3,1},{4,6},{5,7},{6,4},{7,5},{8,10},{9,11},{10,... | collective-permute-start | bytes 129032 | tf_op jit(solution)/shard_map/ppermute | solution.py:503
  33.1 8.7 %collective-permute-start.9 = (bf16[104,768]{1,0:T(8,128)(2,1)S(1)}, bf16[104,768]{1,0:T(8,128)(2,1)S(1)}, u32[]{:S(2)}, u32[]{:S(2)}) collective-permute-start(bf16[104,768]{1,0:T(8,128)(2,1)S(1)} %get-tuple-element.69), channel_id=1, source_target_pairs={{0,24},{8,16},{16,8},{24,0},{1,25},{9,17},{17,9},{25,1},{2,26},{10... | collective-permute-start | bytes 479240 | tf_op jit(solution)/shard_map/ppermute | solution.py:519
  34.6 8.7 %collective-permute-start.10 = (bf16[104,768]{1,0:T(8,128)(2,1)S(1)}, bf16[104,768]{1,0:T(8,128)(2,1)S(1)}, u32[]{:S(2)}, u32[]{:S(2)}) collective-permute-start(bf16[104,768]{1,0:T(8,128)(2,1)S(1)} %get-tuple-element.70), channel_id=1, source_target_pairs={{0,16},{8,24},{16,0},{24,8},{1,17},{9,25},{17,1},{25,9},{2,18},{10... | collective-permute-start | bytes 479240 | tf_op jit(solution)/shard_map/ppermute | solution.py:519
  36.0 7.3 %collective-permute-start.11 = (bf16[104,768]{1,0:T(8,128)(2,1)S(1)}, bf16[104,768]{1,0:T(8,128)(2,1)S(1)}, u32[]{:S(2)}, u32[]{:S(2)}) collective-permute-start(bf16[104,768]{1,0:T(8,128)(2,1)S(1)} %get-tuple-element.71), channel_id=1, source_target_pairs={{0,8},{8,0},{16,24},{24,16},{1,9},{9,1},{17,25},{25,17},{2,10},{10... | collective-permute-start | bytes 479240 | tf_op jit(solution)/shard_map/ppermute | solution.py:519
  36.8 5.0 %collective-permute-start.15 = (bf16[56,384]{1,0:T(8,128)(2,1)S(1)}, bf16[56,384]{1,0:T(8,128)(2,1)S(1)}, u32[]{:S(2)}, u32[]{:S(2)}) collective-permute-start(bf16[56,384]{1,0:T(8,128)(2,1)S(1)} %add.2.refs_0_), channel_id=1, source_target_pairs={{0,4},{1,5},{2,6},{3,7},{4,0},{5,1},{6,2},{7,3},{8,12},{9,13},{10,... | collective-permute-start | bytes 129032 | tf_op jit(solution)/shard_map/ppermute | solution.py:507
  41.8 1.6 %collective-permute-start.16 = (f32[56,384]{1,0:T(8,128)S(1)}, f32[56,384]{1,0:T(8,128)S(1)}, u32[]{:S(2)}, u32[]{:S(2)}) collective-permute-start(f32[56,384]{1,0:T(8,128)S(1)} %add.3.refs_4_), channel_id=1, source_target_pairs={{0,1},{1,0},{2,3},{3,2},{4,5},{5,4},{6,7},{7,6},{8,9},{9,8},{10,11... | collective-permute-start | bytes 258056 | tf_op jit(solution)/shard_map/ppermute | solution.py:510
